TPU v7x, 32 devices: a whole 2x2x4 slice. The times are simulated.
32 devices in a mesh: dp: 8 (over y, x, core), mp: 4 (over z).
Axes of the slice: x: 2, y: 2, z: 4, core: 2. Of those that a mesh axis runs over, the one named last changes fastest.
Arguments:
- tokens: bfloat16 [16384, 1024], P(('dp', 'mp')), may hold values from -6 to 6
- segment_ids: int32 [8, 2048], P('dp'), may hold values from 0 to 5, never falling along the last dimension, each value on 1 to 768 neighbouring positions
- norm1_gain: float32 [1024], replicated, may hold values from 0.5 to 1.5
- norm1_shift: float32 [1024], replicated, may hold values from -3 to 3
- qkv_weight: bfloat16 [1024, 3, 1024], P(None, None, 'mp'), may hold values from -0.1875 to 0.1875
- qv_bias: float32 [2, 1024], P(None, 'mp'), may hold values from -3 to 3
- out_weight: bfloat16 [1024, 1024], P('mp'), may hold values from -0.375 to 0.375
- out_bias: float32 [1024], replicated, may hold values from -3 to 3
- norm2_gain: float32 [1024], replicated, may hold values from 0.5 to 1.5
- norm2_shift: float32 [1024], replicated, may hold values from -3 to 3
- fc1_weight: bfloat16 [1024, 4096], P(None, 'mp'), may hold values from -0.1875 to 0.1875
- fc1_bias: float32 [4096], P('mp'), may hold values from -3 to 3
- fc2_weight: bfloat16 [4096, 1024], P('mp'), may hold values from -0.09375 to 0.09375
- fc2_bias: float32 [1024], replicated, may hold values from -3 to 3
- out_grad: bfloat16 [16384, 1024], P(('dp', 'mp')), may hold values from -6 to 6
Outputs:
- out_tokens: bfloat16 [16384, 1024], P(('dp', 'mp'))
- in_grad: float32 [16384, 1024], P(('dp', 'mp'))
- norm1_gain_grad: float32 [1024], P('mp')
- norm1_shift_grad: float32 [1024], P('mp')
- qkv_weight_grad: float32 [1024, 3, 1024], P(None, None, 'mp')
- qv_bias_grad: float32 [2, 1024], P(None, 'mp')
- out_weight_grad: float32 [1024, 1024], P('mp')
- out_bias_grad: float32 [1024], P('mp')
- norm2_gain_grad: float32 [1024], P('mp')
- norm2_shift_grad: float32 [1024], P('mp')
- fc1_weight_grad: float32 [1024, 4096], P(None, 'mp')
- fc1_bias_grad: float32 [4096], P('mp')
- fc2_weight_grad: float32 [4096, 1024], P('mp')
- fc2_bias_grad: float32 [1024], P('mp')
Inputs may be any that keep to these rules, and one draw needn't show every extreme that they name: `segment_ids`: ids never fall along a sequence; a document has 1 to 768 tokens.
All inputs are finite; a program needn't handle non-finite values.
Results may differ from a plain program's by a relative error of at most 0.015.
Values may be sent and summed in bfloat16 or wider, within the bound.
No kernel may reach another device: no remote copies, remote signals or barrier semaphores. Data moves between devices by JAX's collectives and lax.ppermute only.
A program may use at most 320 MiB of HBM per device.

v0:
```python
import jax
import jax.numpy as jnp
from jax import lax
from jax.sharding import PartitionSpec as P

HEADS = 16
HD = 64
SEQ = 2048


eps = 1e-05


def layer_norm(values_in, gain_vec, shift_vec):
    row_mean = jnp.mean(values_in, axis=-1, keepdims=True)
    centred = values_in - row_mean
    row_var = jnp.mean(centred * centred, axis=-1, keepdims=True)
    return centred * lax.rsqrt(row_var + eps) * gain_vec + shift_vec


def gelu_tanh(values_in):
    return (
        0.5
        * values_in
        * (
            1.0
            + jnp.tanh(
                0.7978845608028654 * (values_in + 0.044715 * values_in * values_in * values_in)
            )
        )
    )


def body(
    tokens,
    segment_ids,
    norm1_gain,
    norm1_shift,
    qkv_weight,
    qv_bias,
    out_weight,
    out_bias,
    norm2_gain,
    norm2_shift,
    fc1_weight,
    fc1_bias,
    fc2_weight,
    fc2_bias,
    out_grad,
):
    shard_rows = tokens.shape[0]
    local_width = qkv_weight.shape[2]
    heads_here = local_width // HD
    seqs_here = segment_ids.shape[0]
    group_rows = seqs_here * SEQ
    block_rows = min(512, SEQ)
    score_scale = HD ** (-0.5)
    first_head = lax.axis_index("mp") * heads_here
    slopes = jnp.exp2(-8.0 * (first_head + jnp.arange(heads_here) + 1).astype(jnp.float32) / HEADS)
    key_at = jnp.arange(SEQ)

    def block_scores(query_block, key_rows, offset, segment):
        query_at = offset + jnp.arange(block_rows)
        raw_scores = (
            jnp.einsum("qhd,khd->hqk", query_block, key_rows, preferred_element_type=jnp.float32)
            * score_scale
        )
        distance = (query_at[:, None] - key_at[None, :]).astype(jnp.float32)
        raw_scores = raw_scores - slopes[:, None, None] * distance[None]
        here_seg = segment[offset : offset + block_rows]
        allowed = (key_at[None, :] <= query_at[:, None]) & (here_seg[:, None] == segment[None, :])
        return jnp.where(allowed[None], raw_scores, -1000000000.0)

    tokens_wide = tokens.astype(jnp.float32)
    norm_first = layer_norm(tokens_wide, norm1_gain, norm1_shift)
    whole_first = lax.all_gather(norm_first.astype(jnp.bfloat16), "mp", axis=0, tiled=True)
    bias_rows = jnp.stack([qv_bias[0], jnp.zeros_like(qv_bias[0]), qv_bias[1]])
    mixed_qkv = (
        jnp.einsum("td,dcf->tcf", whole_first, qkv_weight, preferred_element_type=jnp.float32)
        + bias_rows
    )
    mixed_qkv = mixed_qkv.astype(jnp.bfloat16)
    per_head = mixed_qkv.reshape(seqs_here, SEQ, 3, heads_here, HD)
    queries = per_head[:, :, 0]
    key_all = per_head[:, :, 1]
    value_all = per_head[:, :, 2]

    def attend(member):
        query, key_rows, value_rows, segment = member
        outputs, log_sums = ([], [])
        for offset in range(0, SEQ, block_rows):
            scores = block_scores(query[offset : offset + block_rows], key_rows, offset, segment)
            row_top = jnp.max(scores, axis=-1, keepdims=True)
            exponent = jnp.exp(scores - row_top)
            totals = jnp.sum(exponent, axis=-1, keepdims=True)
            weights = (exponent / totals).astype(jnp.bfloat16)
            outputs.append(
                jnp.einsum("hqk,khd->qhd", weights, value_rows, preferred_element_type=jnp.float32)
            )
            log_sums.append(row_top + jnp.log(totals))
        return (jnp.concatenate(outputs, 0), jnp.concatenate(log_sums, 1))

    context, log_sums = lax.map(attend, (queries, key_all, value_all, segment_ids))
    context = context.reshape(group_rows, local_width).astype(jnp.bfloat16)
    attention = lax.psum_scatter(
        jnp.dot(
            lax.slice_in_dim(context, 0, lax.axis_size("mp") * shard_rows, axis=0),
            out_weight,
            preferred_element_type=jnp.float32,
        ),
        "mp",
        scatter_dimension=0,
        tiled=True,
    )
    resid = attention + out_bias + tokens_wide
    norm_second = layer_norm(resid, norm2_gain, norm2_shift)
    whole_second = lax.all_gather(norm_second.astype(jnp.bfloat16), "mp", axis=0, tiled=True)
    hidden_pre = jnp.dot(whole_second, fc1_weight, preferred_element_type=jnp.float32) + fc1_bias
    hidden = gelu_tanh(hidden_pre).astype(jnp.bfloat16)
    mlp_out = lax.psum_scatter(
        jnp.dot(
            lax.slice_in_dim(hidden, 0, shard_rows * lax.axis_size("mp"), axis=0),
            fc2_weight,
            preferred_element_type=jnp.float32,
        ).astype(jnp.bfloat16),
        "mp",
        scatter_dimension=0,
        tiled=True,
    ).astype(jnp.float32)
    result = (mlp_out + fc2_bias + resid).astype(jnp.bfloat16)
    grad_out_wide = out_grad.astype(jnp.float32)
    grad_rows = lax.all_gather(out_grad, "mp", axis=0, tiled=True)
    grad_fc2 = jnp.einsum("tf,td->fd", hidden, grad_rows, preferred_element_type=jnp.float32)
    grad_act = jnp.einsum("td,fd->tf", grad_rows, fc2_weight, preferred_element_type=jnp.float32)
    unused_value, gelu_pull = jax.vjp(gelu_tanh, hidden_pre)
    grad_pre = gelu_pull(grad_act)[0].astype(jnp.bfloat16)
    grad_fc1_bias = jnp.sum(grad_pre, axis=0, dtype=jnp.float32)
    grad_fc1 = jnp.einsum("td,tf->df", whole_second, grad_pre, preferred_element_type=jnp.float32)
    grad_norm_second = lax.psum_scatter(
        jnp.einsum(
            "tf,df->td",
            lax.slice_in_dim(grad_pre, 0, lax.axis_size("mp") * shard_rows, axis=0),
            fc1_weight,
            preferred_element_type=jnp.float32,
        ),
        "mp",
        scatter_dimension=0,
        tiled=True,
    )
    unused_second, norm_second_pull = jax.vjp(layer_norm, resid, norm2_gain, norm2_shift)
    grad_resid_norm, grad_gain_second, grad_shift_second = norm_second_pull(grad_norm_second)
    grad_resid = grad_out_wide + grad_resid_norm
    grad_attention = grad_resid.astype(jnp.bfloat16)
    grad_attn_rows = lax.all_gather(grad_attention, "mp", axis=0, tiled=True)
    grad_out = jnp.einsum("tf,td->fd", context, grad_attn_rows, preferred_element_type=jnp.float32)
    grad_context = jnp.einsum(
        "td,fd->tf", grad_attn_rows, out_weight, preferred_element_type=jnp.float32
    )
    grad_context = grad_context.astype(jnp.bfloat16).reshape(seqs_here, SEQ, heads_here, HD)

    def attend_back(member):
        query, key_rows, value_rows, segment, sums_here, grad_ctx = member
        grad_query = []
        grad_key = jnp.zeros((SEQ, heads_here, HD), jnp.float32)
        grad_value = jnp.zeros((SEQ, heads_here, HD), jnp.float32)
        for offset in range(0, SEQ, block_rows):
            query_block = query[offset : offset + block_rows]
            scores = block_scores(query_block, key_rows, offset, segment)
            probs = jnp.exp(scores - sums_here[:, offset : offset + block_rows])
            grad_block = grad_ctx[offset : offset + block_rows]
            grad_probs = jnp.einsum(
                "qhd,khd->hqk", grad_block, value_rows, preferred_element_type=jnp.float32
            )
            row_delta = jnp.sum(probs * grad_probs, axis=-1, keepdims=True)
            grad_scores = (probs * (grad_probs - row_delta)).astype(jnp.bfloat16)
            grad_query.append(
                jnp.einsum(
                    "hqk,khd->qhd", grad_scores, key_rows, preferred_element_type=jnp.float32
                )
                * score_scale
            )
            grad_key = (
                grad_key
                + jnp.einsum(
                    "hqk,qhd->khd", grad_scores, query_block, preferred_element_type=jnp.float32
                )
                * score_scale
            )
            grad_value = grad_value + jnp.einsum(
                "hqk,qhd->khd",
                probs.astype(jnp.bfloat16),
                grad_block,
                preferred_element_type=jnp.float32,
            )
        return (jnp.concatenate(grad_query, 0), grad_key, grad_value)

    grad_q, grad_k, grad_v = lax.map(
        attend_back, (queries, key_all, value_all, segment_ids, log_sums, grad_context)
    )
    grad_mixed = (
        jnp.stack([grad_q, grad_k, grad_v], axis=2)
        .astype(jnp.bfloat16)
        .reshape(group_rows, 3, local_width)
    )
    column_sums = jnp.sum(grad_mixed, axis=0, dtype=jnp.float32)
    grad_qv = jnp.stack([column_sums[0], column_sums[2]])
    grad_qkv = jnp.einsum(
        "td,tcf->dcf", whole_first, grad_mixed, preferred_element_type=jnp.float32
    )
    grad_norm_first = lax.psum_scatter(
        jnp.einsum(
            "tcf,dcf->td", grad_mixed, qkv_weight, preferred_element_type=jnp.float32
        ).astype(jnp.bfloat16),
        "mp",
        scatter_dimension=0,
        tiled=True,
    ).astype(jnp.float32)
    unused_first, norm_first_pull = jax.vjp(layer_norm, tokens_wide, norm1_gain, norm1_shift)
    grad_tokens_norm, grad_gain_first, grad_shift_first = norm_first_pull(grad_norm_first)
    grad_tokens = grad_resid + grad_tokens_norm
    small_terms = jnp.stack(
        [
            jnp.sum(grad_resid, axis=0),
            grad_gain_first,
            grad_shift_first,
            grad_gain_second,
            grad_shift_second,
            jnp.sum(grad_out_wide, axis=0),
        ]
    )
    small_shares = lax.psum_scatter(small_terms, "mp", scatter_dimension=1, tiled=True)
    grad_qkv, grad_qv, grad_out, grad_fc1, grad_fc1_bias, grad_fc2, small_shares = lax.psum(
        (grad_qkv, grad_qv, grad_out, grad_fc1, grad_fc1_bias, grad_fc2, small_shares), "dp"
    )
    return (
        result,
        grad_tokens,
        small_shares[1],
        small_shares[2],
        grad_qkv,
        grad_qv,
        grad_out,
        small_shares[0],
        small_shares[3],
        small_shares[4],
        grad_fc1,
        grad_fc1_bias,
        grad_fc2,
        small_shares[5],
    )


def solution(mesh):
    placed = (
        P(("dp", "mp"), None),
        P("dp", None),
        P(),
        P(),
        P(None, None, "mp"),
        P(None, "mp"),
        P("mp", None),
        P(),
        P(),
        P(),
        P(None, "mp"),
        P("mp"),
        P("mp", None),
        P(),
        P(("dp", "mp"), None),
    )
    return jax.shard_map(
        body,
        mesh=mesh,
        in_specs=placed,
        out_specs=(
            P(("dp", "mp"), None),
            P(("dp", "mp"), None),
            P("mp"),
            P("mp"),
            P(None, None, "mp"),
            P(None, "mp"),
            P("mp", None),
            P("mp"),
            P("mp"),
            P("mp"),
            P(None, "mp"),
            P("mp"),
            P("mp", None),
            P("mp"),
        ),
        check_vma=False,
    )
```

profile of v0, /device:TPU:0, one launch (start us, length us, event | category | flops | bytes accessed | tf_op | source)
XLA Modules:
  0.0 1323.9 jit_solution(7468389394136804151)
XLA Ops:
  29.6 68.3 %all-gather.5.cloned.1.call-done = bf16[2048,1024]{1,0:T(8,128)(2,1)} async-done(((bf16[512,1024]{1,0:T(8,128)(2,1)}), bf16[2048,1024]{1,0:T(8,128)(2,1)}) %all-gather.5.cloned.1.call-update) | async-done | bytes 4194320 | tf_op jit(solution)/shard_map/all_gather | solution.py:76
  104.3 8.1 fusion.103
  112.4 8.1 fusion
  129.0 8.3 fusion.102
  145.4 8.6 fusion.75
  154.0 8.1 fusion.101
  170.3 8.8 fusion.76
  179.1 8.1 fusion.100
  209.0 143.2 %reduce-scatter.6.cloned.1.call-done = f32[512,1024]{1,0:T(8,128)} async-done(((f32[2048,1024]{1,0:T(8,128)}), f32[512,1024]{1,0:T(8,128)}) %reduce-scatter.6.cloned.1.call-update) | async-done | bytes 2097168 | tf_op jit(solution)/shard_map/reduce_scatter | solution.py:105
  357.9 80.5 %all-gather.7.cloned.1.call-done = bf16[2048,1024]{1,0:T(8,128)(2,1)} async-done(((bf16[512,1024]{1,0:T(8,128)(2,1)}), bf16[2048,1024]{1,0:T(8,128)(2,1)}) %all-gather.7.cloned.1.call-update) | async-done | bytes 4194320 | tf_op jit(solution)/shard_map/all_gather | solution.py:117
  438.4 10.7 fusion.105
  449.1 70.0 %all-gather.9.cloned.1.call-done = bf16[2048,1024]{1,0:T(8,128)(2,1)} async-done(((bf16[512,1024]{1,0:T(8,128)(2,1)}), bf16[2048,1024]{1,0:T(8,128)(2,1)}) %all-gather.9.cloned.1.call-update) | async-done | bytes 4194320 | tf_op jit(solution)/shard_map/all_gather | solution.py:132
  519.0 15.1 %convert_reduce_fusion = (f32[1024]{0:T(1024)}, bf16[2048,1024]{1,0:T(8,128)(2,1)S(1)}) fusion(f32[2048,1024]{1,0:T(8,128)} %fusion.105, f32[1024]{0:T(1024)S(1)} %copy-done.68, bf16[2048,1024]{1,0:T(8,128)(2,1)} %all-gather.9.cloned.1.call-done, bf16[1024,1024]{1,0:T(8,128)(2,1)S(1)} %copy-done), kind=kOutput, calls=%fused_computation.47 | convolution fusion | flops 4351589376 | bytes 18882560 | tf_op jit(solution)/shard_map/td,fd->tf/dot_general | solution.py:134
  543.4 11.2 convolution_convert_fusion
  554.6 131.8 %reduce-scatter.10.cloned.1.call-done = f32[512,1024]{1,0:T(8,128)} async-done(((f32[2048,1024]{1,0:T(8,128)}), f32[512,1024]{1,0:T(8,128)}) %reduce-scatter.10.cloned.1.call-update) | async-done | bytes 2097168 | tf_op jit(solution)/shard_map/reduce_scatter | solution.py:139
  689.4 77.2 %reduce-scatter.8.cloned.1.call-done = bf16[512,1024]{1,0:T(8,128)(2,1)} async-done(((bf16[2048,1024]{1,0:T(8,128)(2,1)}), bf16[512,1024]{1,0:T(8,128)(2,1)}) %reduce-scatter.8.cloned.1.call-update) | async-done | bytes 1048592 | tf_op jit(solution)/shard_map/reduce_scatter | solution.py:120
  773.3 81.0 %all-gather.11.cloned.1.call-done = bf16[2048,1024]{1,0:T(8,128)(2,1)} async-done(((bf16[512,1024]{1,0:T(8,128)(2,1)}), bf16[2048,1024]{1,0:T(8,128)(2,1)}) %all-gather.11.cloned.1.call-update) | async-done | bytes 4194320 | tf_op jit(solution)/shard_map/all_gather | solution.py:154
  858.7 11.3 multiply_reduce_fusion.3
  870.0 15.8 %multiply_convert_fusion.3 = bf16[4,512,2048]{2,1,0:T(8,128)(2,1)} fusion(f32[4,512,2048]{2,1,0:T(8,128)} %get-tuple-element.132, f32[4,512,2048]{2,1,0:T(8,128)} %get-tuple-element.130, f32[4,512]{1,0:T(4,128)S(1)} %get-tuple-element.131, f32[4,512]{1,0:T(4,128)S(1)} %log_add_fusion.3), kind=kLoop, calls=%fused_computation.9 | loop fusion | flops 16777216 | bytes 41959424 | tf_op jit(solution)/shard_map/while/body/eval_jaxpr/convert_element_type | solution.py:175
  903.3 9.2 multiply_reduce_fusion.2
  912.5 10.1 fusion.16
  922.6 13.2 multiply_reduce_fusion.1
  940.9 9.2 multiply_reduce_fusion
  950.2 8.9 fusion.54
  960.4 11.8 multiply_convert_fusion.2
  979.5 12.4 multiply_convert_fusion.1
  1028.0 10.1 fusion.108
  1038.2 11.6 fusion.91
  1055.4 47.8 %reduce-scatter.12.cloned.1.call-done = bf16[512,1024]{1,0:T(8,128)(2,1)} async-done(((bf16[2048,1024]{1,0:T(8,128)(2,1)}), bf16[512,1024]{1,0:T(8,128)(2,1)}) %reduce-scatter.12.cloned.1.call-update) | async-done | bytes 1048592 | tf_op jit(solution)/shard_map/reduce_scatter | solution.py:210
  1117.9 12.8 reduce-scatter.14.cloned.1.call-done
  1130.7 23.9 %all-reduce = (f32[6,256]{1,0:T(8,128)S(1)}, f32[2,256]{1,0:T(2,128)}, f32[1024]{0:T(1024)}) all-reduce(f32[6,256]{1,0:T(8,128)} %reduce-scatter.14.cloned.1.call-done, f32[2,256]{1,0:T(2,128)S(1)} %pad_maximum_fusion.4, f32[1024]{0:T(1024)S(1)} %copy-done.62), channel_id=1, replica_groups=mesh['dp'=8,'mp'=4] {'dp'}, use_global_device_ids=true, to_apply=%region_31.32 | all-reduce | flops 3072 | bytes 24576 | tf_op jit(solution)/shard_map/psum | solution.py:232
  1155.2 151.0 %all-reduce.4.cloned.1.call-done = (f32[1024,3,256]{2,0,1:T(8,128)}, f32[256,1024]{1,0:T(8,128)}, f32[1024,1024]{1,0:T(8,128)}, f32[1024,1024]{1,0:T(8,128)}) async-done(((f32[1024,3,256]{2,0,1:T(8,128)}, f32[256,1024]{1,0:T(8,128)}, f32[1024,1024]{1,0:T(8,128)}, f32[1024,1024]{1,0:T(8,128)}), (f32[1024,3,256]{2,0,1:T(8,128)}, f32[256,1024]{1,0:T(8,128)}, f32[1024,1024]{1,0:T(8,128)}, ...) | async-done | bytes 12582928 | tf_op jit(solution)/shard_map/psum | solution.py:232
  (263 shorter events, 202.3 us)
Async XLA Ops:
  7.2 511.9 %copy-start = (bf16[1024,1024]{1,0:T(8,128)(2,1)S(1)}, bf16[1024,1024]{1,0:T(8,128)(2,1)}, u32[]{:S(2)}) copy-start(bf16[1024,1024]{1,0:T(8,128)(2,1)} %param.27) | copy-start | bytes 6291460
  7.2 90.7 %all-gather.5.cloned.1.call-start = ((), (), s32[]{:S(2)}) async-start(), calls=%async_computation.5 | async-start | bytes 5242880 | tf_op jit(solution)/shard_map/all_gather | solution.py:76
  14.3 337.9 %reduce-scatter.6.cloned.1.call-start = ((), (), s32[]{:S(2)}) async-start(), calls=%async_computation.6 | async-start | bytes 10485760 | tf_op jit(solution)/shard_map/reduce_scatter | solution.py:105
  208.9 143.3 %copy-start.4 = (bf16[512,1024]{1,0:T(8,128)(2,1)S(1)}, bf16[512,1024]{1,0:T(8,128)(2,1)}, u32[]{:S(2)}) copy-start(bf16[512,1024]{1,0:T(8,128)(2,1)} %param.15) | copy-start | bytes 3145732
  208.9 143.3 %copy-start.63 = (f32[1024]{0:T(1024)S(1)}, f32[1024]{0:T(1024)}, u32[]{:S(2)}) copy-start(f32[1024]{0:T(1024)} %param.22) | copy-start | bytes 12292
  208.9 146.5 %copy-start.46 = (f32[1024]{0:T(1024)S(1)}, f32[1024]{0:T(1024)}, u32[]{:S(2)}) copy-start(f32[1024]{0:T(1024)} %param.23) | copy-start | bytes 12292
  208.9 146.5 %copy-start.60 = (f32[1024]{0:T(1024)S(1)}, f32[1024]{0:T(1024)}, u32[]{:S(2)}) copy-start(f32[1024]{0:T(1024)} %param.24) | copy-start | bytes 12292
  208.9 229.4 %all-gather.7.cloned.1.call-start = ((), (), s32[]{:S(2)}) async-start(), calls=%async_computation.7 | async-start | bytes 5242880 | tf_op jit(solution)/shard_map/all_gather | solution.py:117
  356.8 162.2 %all-gather.9.cloned.1.call-start = ((), (), s32[]{:S(2)}) async-start(), calls=%async_computation.9 | async-start | bytes 5242880 | tf_op jit(solution)/shard_map/all_gather | solution.py:132
  357.4 161.6 %copy-start.68 = (f32[1024]{0:T(1024)S(1)}, f32[1024]{0:T(1024)}, u32[]{:S(2)}) copy-start(f32[1024]{0:T(1024)} %param.26) | copy-start | bytes 12292
  357.4 329.0 %reduce-scatter.10.cloned.1.call-start = ((), (), s32[]{:S(2)}) async-start(), calls=%async_computation.10 | async-start | bytes 10485760 | tf_op jit(solution)/shard_map/reduce_scatter | solution.py:139
  543.2 223.4 %reduce-scatter.8.cloned.1.call-start = ((), (), s32[]{:S(2)}) async-start(), calls=%async_computation.8 | async-start | bytes 5242880 | tf_op jit(solution)/shard_map/reduce_scatter | solution.py:120
  554.5 131.9 %copy-start.3 = (f32[512,1024]{1,0:T(8,128)S(1)}, f32[512,1024]{1,0:T(8,128)}, u32[]{:S(2)}) copy-start(f32[512,1024]{1,0:T(8,128)} %copy-done.2) | copy-start | bytes 6291460
  554.6 212.0 %copy-start.61 = (f32[1024]{0:T(1024)S(1)}, f32[1024]{0:T(1024)}, u32[]{:S(2)}) copy-start(f32[1024]{0:T(1024)} %param.28) | copy-start | bytes 12292
  554.6 299.7 %all-gather.11.cloned.1.call-start = ((), (), s32[]{:S(2)}) async-start(), calls=%async_computation.11 | async-start | bytes 5242880 | tf_op jit(solution)/shard_map/all_gather | solution.py:154
  689.4 82.2 %copy-start.13 = (bf16[512,1024]{1,0:T(8,128)(2,1)S(1)}, bf16[512,1024]{1,0:T(8,128)(2,1)}, u32[]{:S(2)}) copy-start(bf16[512,1024]{1,0:T(8,128)(2,1)} %param.29) | copy-start | bytes 3145732
  770.3 84.0 %copy-start.40 = (bf16[256,1024]{1,0:T(8,128)(2,1)S(1)}, bf16[256,1024]{1,0:T(8,128)(2,1)}, u32[]{:S(2)}) copy-start(bf16[256,1024]{1,0:T(8,128)(2,1)} %param.21) | copy-start | bytes 1572868
  772.9 330.3 %reduce-scatter.12.cloned.1.call-start = ((), (), s32[]{:S(2)}) async-start(), calls=%async_computation.12 | async-start | bytes 5242880 | tf_op jit(solution)/shard_map/reduce_scatter | solution.py:210
  870.0 29.8 %slice-start.8 = ((s8[16777216]{0:T(1024)(128)(4,1)}), s8[4194304]{0:T(1024)(128)(4,1)S(1)}, s32[]{:S(2)}) async-start(s8[16777216]{0:T(1024)(128)(4,1)} %bitcast.155), calls=%async_computation.23 | async-start | bytes 8388608
  870.0 29.8 %slice-start.9 = ((s8[16777216]{0:T(1024)(128)(4,1)}), s8[4194304]{0:T(1024)(128)(4,1)S(1)}, s32[]{:S(2)}) async-start(s8[16777216]{0:T(1024)(128)(4,1)} %bitcast.155), calls=%async_computation.24 | async-start | bytes 8388608
  870.0 29.8 %slice-start.10 = ((s8[16777216]{0:T(1024)(128)(4,1)}), s8[4194304]{0:T(1024)(128)(4,1)S(1)}, s32[]{:S(2)}) async-start(s8[16777216]{0:T(1024)(128)(4,1)} %bitcast.155), calls=%async_computation.25 | async-start | bytes 8388608
  912.5 23.4 %slice-start.1 = ((s8[16777216]{0:T(1024)(128)(4,1)}), s8[4194304]{0:T(1024)(128)(4,1)S(1)}, s32[]{:S(2)}) async-start(s8[16777216]{0:T(1024)(128)(4,1)} %bitcast.151), calls=%async_computation.16 | async-start | bytes 8388608
  1019.2 30.6 %copy-start.27 = (bf16[2048,1,256]{2,0,1:T(8,128)(2,1)}, bf16[2048,1,256]{2,0,1:T(8,128)(2,1)S(1)}, u32[]{:S(2)}) copy-start(bf16[2048,1,256]{2,0,1:T(8,128)(2,1)S(1)} %copy.30) | copy-start | bytes 3145732
  1027.8 102.9 %reduce-scatter.14.cloned.1.call-start = ((), (), s32[]{:S(2)}) async-start(), calls=%async_computation.13 | async-start | bytes 40960 | tf_op jit(solution)/shard_map/reduce_scatter | solution.py:231
  1049.8 53.4 %copy-start.5 = (bf16[512,1024]{1,0:T(8,128)(2,1)S(1)}, bf16[512,1024]{1,0:T(8,128)(2,1)}, u32[]{:S(2)}) copy-start(bf16[512,1024]{1,0:T(8,128)(2,1)} %param.15) | copy-start | bytes 3145732
  1049.8 53.4 %copy-start.44 = (f32[512]{0:T(512)S(1)}, f32[512]{0:T(512)}, u32[]{:S(2)}) copy-start(f32[512]{0:T(512)} %copy-done.43) | copy-start | bytes 6148
  1049.8 53.4 %copy-start.45 = (f32[1024]{0:T(1024)S(1)}, f32[1024]{0:T(1024)}, u32[]{:S(2)}) copy-start(f32[1024]{0:T(1024)} %param.17) | copy-start | bytes 12292
  1049.8 55.4 %copy-start.55 = (f32[512]{0:T(512)S(1)}, f32[512]{0:T(512)}, u32[]{:S(2)}) copy-start(f32[512]{0:T(512)} %copy-done.54) | copy-start | bytes 6148
  1049.8 55.5 %copy-start.53 = (f32[512]{0:T(512)S(1)}, f32[512]{0:T(512)}, u32[]{:S(2)}) copy-start(f32[512]{0:T(512)} %copy-done.52) | copy-start | bytes 6148
  1055.4 52.3 %copy-start.14 = (bf16[512,1024]{1,0:T(8,128)(2,1)S(1)}, bf16[512,1024]{1,0:T(8,128)(2,1)}, u32[]{:S(2)}) copy-start(bf16[512,1024]{1,0:T(8,128)(2,1)} %param.29) | copy-start | bytes 3145732
  1055.4 52.3 %copy-start.57 = (f32[512]{0:T(512)S(1)}, f32[512]{0:T(512)}, u32[]{:S(2)}) copy-start(f32[512]{0:T(512)} %copy-done.56) | copy-start | bytes 6148
  1110.8 195.4 %all-reduce.4.cloned.1.call-start = ((), (), s32[]{:S(2)}) async-start(), calls=%async_computation.14 | async-start | bytes 25165824 | tf_op jit(solution)/shard_map/psum | solution.py:232
  (61 other events, 445.4 us)
Sparse Core Ops, SparseCore 0:
  14.4 83.4 all-gather.4
  209.0 143.0 reduce-scatter.5
  357.0 81.3 all-gather.6
  439.8 79.2 all-gather.8
  543.3 143.0 reduce-scatter.9
  689.1 77.4 reduce-scatter.7
  773.0 81.2 all-gather.10
  1027.9 75.2 reduce-scatter.11
  1110.9 19.7 reduce-scatter.13
  1135.7 170.4 all-reduce.3
where the time goes:
time: 1330 us; the launch traced here: 1320 us
  waiting for transfers between devices  864 us (65%)
  matrix products  272 us (20%)
  other arithmetic  121 us (9%)
  local copies, waits for them, and re-layouts  25.9 us (2%)
  blocking collectives  23.9 us (2%)
  between operations  15.3 us (1%)
    psum x1, waiting for transfers between devices, body(): lax.psum((grad_qkv, grad_qv, grad_out, grad_fc1, grad_fc1_bias, grad_fc2,...  151 us
    reduce_scatter x1, waiting for transfers between devices, body(): lax.psum_scatter(jnp.dot(lax.slice_in_dim(context, 0, lax.axis_size('mp')...  143 us
    reduce_scatter x1, waiting for transfers between devices, body(): lax.psum_scatter(jnp.einsum('tf,df->td', lax.slice_in_dim(grad_pre, 0, la...  132 us
    all_gather x1, waiting for transfers between devices, body(): grad_attn_rows = lax.all_gather(grad_attention, 'mp', axis=0, tiled=True)  81 us
    all_gather x1, waiting for transfers between devices, body(): lax.all_gather(norm_second.astype(jnp.bfloat16), 'mp', axis=0, tiled=True)  80.5 us
    reduce_scatter x1, waiting for transfers between devices, body(): lax.psum_scatter(jnp.dot(lax.slice_in_dim(hidden, 0, shard_rows * lax.axi...  77.2 us
    all_gather x1, waiting for transfers between devices, body(): grad_rows = lax.all_gather(out_grad, 'mp', axis=0, tiled=True)  70 us
    all_gather x1, waiting for transfers between devices, body(): lax.all_gather(norm_first.astype(jnp.bfloat16), 'mp', axis=0, tiled=True)  68.3 us
  transfers between devices with their start and end apart: 10, of which 10 were waited for; matrix products, arithmetic and copies ran while one was open for 6% of the time, Pallas kernels for 0%

commit v1 on v0

v1 whole, which is shorter than its diff:
```python
import functools

import jax
import jax.numpy as jnp
from jax import lax
from jax.experimental import pallas as pl
from jax.experimental.pallas import tpu as pltpu
from jax.sharding import PartitionSpec as P

HEADS = 16
HD = 64
DOC_MOST = 768
QB = 256
MASKED = -1e12
eps = 1e-05
f32 = jnp.float32
bf16 = jnp.bfloat16


def dot(a, b, ca, cb):
    return lax.dot_general(a, b, (((ca,), (cb,)), ((), ())), preferred_element_type=f32)


def fill_mask(segq_ref, segk_ref, mask_ref, window, halo):
    for i in range(mask_ref.shape[0]):
        key_at = lax.broadcasted_iota(jnp.int32, (window, QB), 0) + i * QB
        query_at = lax.broadcasted_iota(jnp.int32, (window, QB), 1) + (i * QB + halo)
        same = segk_ref[i * QB : i * QB + window, :] == segq_ref[:, i * QB : (i + 1) * QB]
        allowed = same & (key_at <= query_at)
        mask_ref[i] = jnp.where(allowed, (key_at - query_at).astype(f32), MASKED)


def halves(rows):
    lane = lax.broadcasted_iota(jnp.int32, (rows, 2 * HD), 1)
    return [lane < HD, lane >= HD]


def attend_kernel(halo, slopes, segq, segk, q_ref, k_ref, v_ref, o_ref, lse_ref, mask_ref):
    window = halo + QB
    pair = pl.program_id(0)

    @pl.when(pair == 0)
    def _():
        fill_mask(segq, segk, mask_ref, window, halo)

    v_t = v_ref[...].T
    pick = halves(QB)
    for i in range(mask_ref.shape[0]):
        rows = slice(i * QB, (i + 1) * QB)
        keys = slice(i * QB, i * QB + window)
        query = q_ref[rows, :] * jnp.asarray(HD**-0.5, bf16)
        key_rows = k_ref[keys, :]
        out = []
        for h in range(2):
            q_h = jnp.where(pick[h], query, jnp.zeros_like(query))
            scores = dot(key_rows, q_h, 1, 1) + slopes[2 * pair + h] * mask_ref[i]
            top = jnp.max(scores, axis=0, keepdims=True)
            expo = jnp.exp(scores - top)
            total = jnp.sum(expo, axis=0, keepdims=True)
            o_t = dot(v_t[:, keys], expo.astype(bf16), 1, 0)
            out.append(o_t[h * HD : (h + 1) * HD, :] * (1.0 / total))
            lse_ref[0, h : h + 1, rows] = top + jnp.log(total)
        o_ref[rows, :] = jnp.concatenate(out, axis=0).T.astype(bf16)


def attend_back_kernel(
    halo, slopes, segq, segk, q_ref, k_ref, v_ref, g_ref, lse_ref, dq_ref, dk_ref, dv_ref,
    mask_ref, dk_acc, dv_acc,
):
    window = halo + QB
    pair = pl.program_id(0)

    @pl.when(pair == 0)
    def _():
        fill_mask(segq, segk, mask_ref, window, halo)

    k_t = k_ref[...].T
    pick = halves(QB)
    dk_acc[...] = jnp.zeros_like(dk_acc)
    dv_acc[...] = jnp.zeros_like(dv_acc)
    for i in range(mask_ref.shape[0]):
        rows = slice(i * QB, (i + 1) * QB)
        keys = slice(i * QB, i * QB + window)
        query = q_ref[rows, :] * jnp.asarray(HD**-0.5, bf16)
        grad = g_ref[rows, :]
        key_rows = k_ref[keys, :]
        value_rows = v_ref[keys, :]
        out = []
        for h in range(2):
            q_h = jnp.where(pick[h], query, jnp.zeros_like(query))
            g_h = jnp.where(pick[h], grad, jnp.zeros_like(grad))
            scores = dot(key_rows, q_h, 1, 1) + slopes[2 * pair + h] * mask_ref[i]
            probs = jnp.exp(scores - lse_ref[0, h : h + 1, rows])
            grad_probs = dot(value_rows, g_h, 1, 1)
            delta = jnp.sum(probs * grad_probs, axis=0, keepdims=True)
            grad_scores = (probs * (grad_probs - delta)).astype(bf16)
            dv_acc[keys, :] += dot(probs.astype(bf16), g_h, 1, 0)
            dk_acc[keys, :] += dot(grad_scores, q_h, 1, 0)
            dq_t = dot(k_t[:, keys], grad_scores, 1, 0)
            out.append(dq_t[h * HD : (h + 1) * HD, :])
        dq_ref[rows, :] = (jnp.concatenate(out, axis=0).T * HD**-0.5).astype(bf16)
    dk_ref[...] = dk_acc[...].astype(bf16)
    dv_ref[...] = dv_acc[...].astype(bf16)


def attend(slopes, segq, segk, q, k, v):
    rows, wide = q.shape
    ext = k.shape[0]
    halo = ext - rows
    pairs = wide // (2 * HD)
    blocks = rows // QB
    col = lambda n: pl.BlockSpec((n, 2 * HD), lambda p: (0, p))
    work = pairs * 2 * blocks * (halo + QB) * QB
    return pl.pallas_call(
        functools.partial(attend_kernel, halo),
        grid=(pairs,),
        in_specs=[
            pl.BlockSpec(memory_space=pltpu.SMEM),
            pl.BlockSpec((1, rows), lambda p: (0, 0)),
            pl.BlockSpec((ext, 1), lambda p: (0, 0)),
            col(rows),
            col(ext),
            col(ext),
        ],
        out_specs=[col(rows), pl.BlockSpec((1, 2, rows), lambda p: (p, 0, 0))],
        out_shape=[
            jax.ShapeDtypeStruct((rows, wide), bf16),
            jax.ShapeDtypeStruct((pairs, 2, rows), f32),
        ],
        scratch_shapes=[pltpu.VMEM((blocks, halo + QB, QB), f32)],
        compiler_params=pltpu.CompilerParams(vmem_limit_bytes=40 << 20),
        cost_estimate=pl.CostEstimate(
            flops=work * 256 * 4, bytes_accessed=2 * wide * (2 * rows + 2 * ext), transcendentals=work
        ),
    )(slopes, segq, segk, q, k, v)


def attend_back(slopes, segq, segk, q, k, v, grad, lse):
    rows, wide = q.shape
    ext = k.shape[0]
    halo = ext - rows
    pairs = wide // (2 * HD)
    blocks = rows // QB
    col = lambda n: pl.BlockSpec((n, 2 * HD), lambda p: (0, p))
    work = pairs * 2 * blocks * (halo + QB) * QB
    return pl.pallas_call(
        functools.partial(attend_back_kernel, halo),
        grid=(pairs,),
        in_specs=[
            pl.BlockSpec(memory_space=pltpu.SMEM),
            pl.BlockSpec((1, rows), lambda p: (0, 0)),
            pl.BlockSpec((ext, 1), lambda p: (0, 0)),
            col(rows),
            col(ext),
            col(ext),
            col(rows),
            pl.BlockSpec((1, 2, rows), lambda p: (p, 0, 0)),
        ],
        out_specs=[col(rows), col(ext), col(ext)],
        out_shape=[
            jax.ShapeDtypeStruct((rows, wide), bf16),
            jax.ShapeDtypeStruct((ext, wide), bf16),
            jax.ShapeDtypeStruct((ext, wide), bf16),
        ],
        scratch_shapes=[
            pltpu.VMEM((blocks, halo + QB, QB), f32),
            pltpu.VMEM((ext, 2 * HD), f32),
            pltpu.VMEM((ext, 2 * HD), f32),
        ],
        compiler_params=pltpu.CompilerParams(vmem_limit_bytes=48 << 20),
        cost_estimate=pl.CostEstimate(
            flops=work * 256 * 10, bytes_accessed=2 * wide * (3 * rows + 4 * ext), transcendentals=work
        ),
    )(slopes, segq, segk, q, k, v, grad, lse)


def swap(value, b):
    n = lax.axis_size("dp")
    return lax.ppermute(value, "dp", [(i, i ^ (1 << b)) for i in range(n)])


def shift(value, s):
    n = lax.axis_size("mp")
    return lax.ppermute(value, "mp", [(i, (i + s) % n) for i in range(n)])


def add(a, b):
    return (a.astype(f32) + b.astype(f32)).astype(bf16)


def spread(a, b):
    x_a, y_b = swap(a, 1), swap(b, 2)
    a2, b2 = jnp.stack([a, x_a], 1), jnp.stack([b, y_b], 1)
    y_a2, x_b2 = swap(a2, 2), swap(b2, 1)
    return jnp.stack([a2, y_a2], 1), jnp.stack([b2, x_b2], 2)


def gather_blocks(a, b):
    n = lax.axis_size("mp")
    both = [shift(jnp.concatenate([a, b], 0), s) for s in range(1, n)]
    cut = a.shape[0]
    return spread(jnp.stack([r[:cut] for r in both]), jnp.stack([r[cut:] for r in both]))


def scatter_blocks(a, b):
    n = lax.axis_size("mp")
    a, b = add(a[:, 0], swap(a[:, 1], 2)), add(b[:, :, 0], swap(b[:, :, 1], 1))
    a, b = add(a[:, 0], swap(a[:, 1], 1)), add(b[:, 0], swap(b[:, 1], 2))
    both = jnp.concatenate([a, b], 1)
    total = both[0].astype(f32)
    for s in range(1, n):
        total = total + shift(both[s], n - s).astype(f32)
    for b_hi in range(3, lax.axis_size("dp").bit_length() - 1):
        total = total + swap(total, b_hi)
    cut = a.shape[1]
    total = total.astype(bf16)
    a4, b4 = spread(total[None, :cut], total[None, cut:])
    return a4[0], b4[0]


def norm_parts(rows):
    mean = jnp.mean(rows, axis=-1, keepdims=True)
    centred = rows - mean
    rstd = lax.rsqrt(jnp.mean(centred * centred, axis=-1, keepdims=True) + eps)
    return centred * rstd, rstd


def norm_back(grad, gain, xhat, rstd):
    scaled = grad * gain
    return rstd * (
        scaled
        - jnp.mean(scaled, axis=-1, keepdims=True)
        - xhat * jnp.mean(scaled * xhat, axis=-1, keepdims=True)
    )


def gelu_both(v):
    c, k = 0.7978845608028654, 0.044715
    t = jnp.tanh(c * (v + k * v * v * v))
    value = 0.5 * v * (1.0 + t)
    slope = 0.5 * (1.0 + t) + 0.5 * v * (1.0 - t * t) * (c * (1.0 + 3.0 * k * v * v))
    return value, slope


def body(
    tokens,
    segment_ids,
    norm1_gain,
    norm1_shift,
    qkv_weight,
    qv_bias,
    out_weight,
    out_bias,
    norm2_gain,
    norm2_shift,
    fc1_weight,
    fc1_bias,
    fc2_weight,
    fc2_bias,
    out_grad,
):
    rows, wide = tokens.shape
    half = wide // 2
    mp = lax.axis_size("mp")
    m = lax.axis_index("mp")
    d = lax.axis_index("dp")
    bits = (d & 1, (d >> 1) & 1, (d >> 2) & 1)
    places = [(ey, ex) for ey in range(2) for ex in range(2)]
    ff_here = fc1_weight.shape[1]
    piece = ff_here // 8
    heads_here = qkv_weight.shape[2] // HD

    def rel(ec, ey, ex):
        return (bits[0] ^ ec), (bits[2] ^ ey) * 2 + (bits[1] ^ ex)

    halo, parts = 0, [tokens]
    t = 1
    while halo < DOC_MOST:
        n = min(rows, DOC_MOST - halo)
        parts.insert(
            0, lax.ppermute(tokens[rows - n :], "mp", [(i, i + t) for i in range(mp - t)])
        )
        halo += n
        t += 1
    halo_parts = [(p.shape[0], i) for p, i in zip(parts[:-1], range(len(parts) - 1, 0, -1))]

    loc = jnp.concatenate(
        [
            jnp.transpose(qkv_weight, (1, 2, 0)),
            out_weight[None],
        ],
        0,
    ).reshape(4, heads_here, HD, wide)
    loc = jnp.stack([loc[0], loc[3], loc[1], loc[2]], 1)

    def loc_half(ec):
        out = []
        for ey, ex in places:
            c_at, head = rel(ec, ey, ex)
            out.append(lax.dynamic_slice(loc, (head, 0, 0, c_at * half), (1, 4, HD, half))[0])
        return jnp.stack(out)

    att_loc = [loc_half(0), loc_half(1)]
    fc1_t = fc1_weight.T

    def loc_rows(weight, ec):
        out = []
        for ey, ex in places:
            c_at, place = rel(ec, ey, ex)
            out.append(lax.dynamic_slice_in_dim(weight, (place * 2 + c_at) * piece, piece, 0))
        return jnp.stack(out)

    fc1_loc = [loc_rows(fc1_t, 0), loc_rows(fc1_t, 1)]
    fc2_loc = [loc_rows(fc2_weight, 0), loc_rows(fc2_weight, 1)]

    bias_own = jnp.concatenate([fc1_bias, qv_bias.reshape(-1)])
    bias_all = jnp.stack([bias_own] + [shift(bias_own, s) for s in range(1, mp)])
    fc1_b = bias_all[:, :ff_here]
    qv_b = bias_all[:, ff_here:].reshape(mp, 2, heads_here, HD)

    def rel_rows(table, ec):
        out = []
        for ey, ex in places:
            c_at, place = rel(ec, ey, ex)
            at = place if ec is None else place * 2 + c_at
            out.append(lax.dynamic_slice_in_dim(table, at, 1, 1))
        return jnp.concatenate(out, 1)

    def rel_heads(table):
        out = []
        for ey, ex in places:
            place = rel(0, ey, ex)[1]
            out.append(lax.dynamic_slice_in_dim(table, place, 1, 1))
        return jnp.concatenate(out, 1)

    q_bias = rel_heads(qv_b[:, 0]).reshape(-1)
    v_bias = rel_heads(qv_b[:, 1]).reshape(-1)
    fc1_bs = [rel_rows(fc1_b.reshape(mp, 8, piece), ec).reshape(-1) for ec in range(2)]

    def gather_att():
        own = att_loc[0][0]
        a4, b4 = gather_blocks(own[:2].reshape(2 * HD, half), own[2:].reshape(2 * HD, half))
        a4 = a4.reshape(mp - 1, 4, 2, HD, half)
        b4 = b4.reshape(mp - 1, 4, 2, HD, half)
        mine = jnp.concatenate(
            [att_loc[0][None], jnp.concatenate([a4, b4], 2)], 0
        )
        mine = jnp.transpose(mine, (2, 0, 1, 3, 4)).reshape(4, HEADS * HD, half)
        return mine, swap(mine, 0)

    def gather_ff(local):
        own = local[0][0]
        a4, b4 = gather_blocks(own[: piece // 2], own[piece // 2 :])
        rest = jnp.stack([a4, b4], 3).reshape(mp - 1, 4, piece, wide)
        mine = jnp.concatenate([local[0][None], rest], 0).reshape(-1, wide)
        return mine, swap(mine, 0)

    w_att = gather_att()
    w_fc1 = gather_ff(fc1_loc)
    w_fc2 = gather_ff(fc2_loc)

    ext = jnp.concatenate(parts, 0).astype(f32)
    xhat_ext, rstd_ext = norm_parts(ext)
    norm1 = (xhat_ext * norm1_gain + norm1_shift).astype(bf16)
    col = [bits[0] * half, (1 - bits[0]) * half]

    def cols(value):
        return [lax.dynamic_slice_in_dim(value, at, half, 1) for at in col]

    def join(own, other):
        first = bits[0] == 0
        return jnp.concatenate([jnp.where(first, own, other), jnp.where(first, other, own)], 1)

    n1 = cols(norm1)

    def project(t, lhs):
        return dot(lhs[0], w_att[0][t], 1, 1) + dot(lhs[1], w_att[1][t], 1, 1)

    q = (project(0, [v[halo:] for v in n1]) + q_bias).astype(bf16)
    k = project(2, n1).astype(bf16)
    v = (project(3, n1) + v_bias).astype(bf16)

    seg_row = jnp.concatenate([jnp.full((1, halo), -1, jnp.int32), segment_ids], 1)
    segk = lax.dynamic_slice_in_dim(seg_row, m * rows, halo + rows, 1)
    segq = segk[:, halo:]
    segk = segk.reshape(halo + rows, 1)
    block = (m + mp - jnp.arange(mp)) % mp
    place = jnp.stack([rel(0, ey, ex)[1] for ey, ex in places])
    head = (block[:, None] * heads_here + place[None]).reshape(-1)
    slopes = jnp.exp2(-8.0 * (head + 1).astype(f32) / HEADS)

    context, lse = attend(slopes, segq, segk, q, k, v)
    attention = join(dot(context, w_att[0][1], 1, 0), dot(context, w_att[1][1], 1, 0))
    tokens_wide = tokens.astype(f32)
    resid = attention + out_bias + tokens_wide
    xhat2, rstd2 = norm_parts(resid)
    norm2 = (xhat2 * norm2_gain + norm2_shift).astype(bf16)
    pre = [dot(norm2, w_fc1[i], 1, 1) + fc1_bs[i] for i in range(2)]
    hidden = [gelu_both(p)[0].astype(bf16) for p in pre]
    mlp = dot(hidden[0], w_fc2[0], 1, 0) + dot(hidden[1], w_fc2[1], 1, 0)
    result = (mlp + fc2_bias + resid).astype(bf16)

    def reduce_ff(lhs, rhs):
        theirs = swap(dot(lhs[1], rhs, 0, 0).astype(bf16), 0)
        mine = (dot(lhs[0], rhs, 0, 0) + theirs.astype(f32)).astype(bf16)
        mine = mine.reshape(mp, 2, 2, 2, piece // 2, wide)
        a4, b4 = scatter_blocks(mine[:, :, :, 0], mine[:, :, :, 1])
        mine = jnp.stack([a4, b4], 2).reshape(4, piece, wide)
        both = jnp.stack([mine, swap(mine, 0)])
        out = []
        for i in range(8):
            at = d ^ i
            at_c, at_p = at & 1, (at >> 1) & 3
            out.append(lax.dynamic_slice(both, (at_c, at_p, 0, 0), (1, 1, piece, wide))[0, 0])
        return jnp.concatenate(out, 0).astype(f32)

    grad_fc2 = reduce_ff(hidden, out_grad)
    grad_pre = [
        (dot(out_grad, w_fc2[i], 1, 1) * gelu_both(pre[i])[1]).astype(bf16) for i in range(2)
    ]
    grad_fc1 = reduce_ff(grad_pre, norm2).T
    grad_norm2 = dot(grad_pre[0], w_fc1[0], 1, 0) + dot(grad_pre[1], w_fc1[1], 1, 0)
    out_grad_wide = out_grad.astype(f32)
    grad_resid = out_grad_wide + norm_back(grad_norm2, norm2_gain, xhat2, rstd2)
    grad_att = cols(grad_resid.astype(bf16))
    grad_context = (
        dot(grad_att[0], w_att[0][1], 1, 1) + dot(grad_att[1], w_att[1][1], 1, 1)
    ).astype(bf16)
    dq, dk, dv = attend_back(slopes, segq, segk, q, k, v, grad_context, lse)

    def back_half(i):
        tail = dot(dk, w_att[i][2], 1, 0) + dot(dv, w_att[i][3], 1, 0)
        return tail[:halo], tail[halo:] + dot(dq, w_att[i][0], 1, 0)

    back = [back_half(0), back_half(1)]
    grad_halo = join(back[0][0], back[1][0]).astype(bf16)
    grad_norm1 = join(back[0][1], back[1][1])

    def weights_half(i):
        return jnp.stack(
            [
                dot(dq, n1[i][halo:], 0, 0).astype(bf16),
                dot(context, grad_att[i], 0, 0).astype(bf16),
                dot(dk, n1[i], 0, 0).astype(bf16),
                dot(dv, n1[i], 0, 0).astype(bf16),
            ]
        )

    theirs = swap(weights_half(1), 0)
    mine = add(weights_half(0), theirs).reshape(4, mp, 2, 2, HD, half)
    mine = jnp.transpose(mine, (1, 2, 3, 0, 4, 5))
    a4, b4 = scatter_blocks(
        mine[:, :, :, :2].reshape(mp, 2, 2, 2 * HD, half),
        mine[:, :, :, 2:].reshape(mp, 2, 2, 2 * HD, half),
    )
    mine = jnp.stack([a4, b4], 2).reshape(4, 4, HD, half)
    both = jnp.stack([mine, swap(mine, 0)])
    out = []
    for p in range(4):
        at_p = ((d >> 1) & 3) ^ p
        pair = lax.dynamic_slice_in_dim(both, at_p, 1, 1)[:, 0]
        first = bits[0] == 0
        out.append(
            jnp.concatenate(
                [jnp.where(first, pair[0], pair[1]), jnp.where(first, pair[1], pair[0])], -1
            )
        )
    grad_att_w = jnp.stack(out, 1).reshape(4, heads_here * HD, wide).astype(f32)
    grad_out = grad_att_w[1]
    grad_qkv = jnp.transpose(
        jnp.stack([grad_att_w[0], grad_att_w[2], grad_att_w[3]]), (2, 0, 1)
    )

    at = 0
    for n, t in halo_parts:
        moved = lax.ppermute(
            grad_halo[at : at + n], "mp", [(i, i - t) for i in range(t, mp)]
        ).astype(f32)
        grad_norm1 = grad_norm1 + jnp.pad(moved, ((rows - n, 0), (0, 0)))
        at += n
    xhat1, rstd1 = xhat_ext[halo:], rstd_ext[halo:]
    in_grad = grad_resid + norm_back(grad_norm1, norm1_gain, xhat1, rstd1)

    def in_order(pieces, n):
        table = jnp.stack(
            [lax.dynamic_index_in_dim(pieces, (m + mp - j) % mp, 0, False) for j in range(mp)]
        )
        table = jnp.where(bits[2] == 0, table, table[:, ::-1])
        table = jnp.where(bits[1] == 0, table, table[:, :, ::-1])
        if table.shape[3] == 2:
            table = jnp.where(bits[0] == 0, table, table[:, :, :, ::-1])
        return table.reshape(mp, -1)

    ff_sums = jnp.stack(
        [jnp.sum(g.astype(f32), axis=0).reshape(mp, 2, 2, piece) for g in grad_pre], 3
    )
    q_sums = jnp.sum(dq.astype(f32), axis=0).reshape(mp, 2, 2, 1, HD)
    v_sums = jnp.sum(dv.astype(f32), axis=0).reshape(mp, 2, 2, 1, HD)
    small = jnp.stack(
        [
            jnp.sum(grad_resid, axis=0),
            jnp.sum(grad_norm1 * xhat1, axis=0),
            jnp.sum(grad_norm1, axis=0),
            jnp.sum(grad_norm2 * xhat2, axis=0),
            jnp.sum(grad_norm2, axis=0),
            jnp.sum(out_grad_wide, axis=0),
        ]
    )
    n_small = wide // mp
    vectors = jnp.concatenate(
        [
            jnp.transpose(small.reshape(6, mp, n_small), (1, 0, 2)).reshape(mp, -1),
            in_order(q_sums, HD),
            in_order(v_sums, HD),
            in_order(ff_sums, piece),
        ],
        1,
    )
    for b in range(lax.axis_size("dp").bit_length() - 1):
        vectors = vectors + swap(vectors, b)
    mine = lax.dynamic_index_in_dim(vectors, m, 0, False)
    for s in range(1, mp):
        sent = lax.dynamic_index_in_dim(vectors, (m + mp - s) % mp, 0, False)
        mine = mine + shift(sent, mp - s)
    six = mine[: 6 * n_small].reshape(6, n_small)
    rest = mine[6 * n_small :]
    n_qv = heads_here * HD
    grad_qv = rest[: 2 * n_qv].reshape(2, n_qv)
    grad_fc1_bias = rest[2 * n_qv :]
    return (
        result,
        in_grad,
        six[1],
        six[2],
        grad_qkv,
        grad_qv,
        grad_out,
        six[0],
        six[3],
        six[4],
        grad_fc1,
        grad_fc1_bias,
        grad_fc2,
        six[5],
    )


def solution(mesh):
    placed = (
        P(("dp", "mp"), None),
        P("dp", None),
        P(),
        P(),
        P(None, None, "mp"),
        P(None, "mp"),
        P("mp", None),
        P(),
        P(),
        P(),
        P(None, "mp"),
        P("mp"),
        P("mp", None),
        P(),
        P(("dp", "mp"), None),
    )
    return jax.shard_map(
        body,
        mesh=mesh,
        in_specs=placed,
        out_specs=(
            P(("dp", "mp"), None),
            P(("dp", "mp"), None),
            P("mp"),
            P("mp"),
            P(None, None, "mp"),
            P(None, "mp"),
            P("mp", None),
            P("mp"),
            P("mp"),
            P("mp"),
            P(None, "mp"),
            P("mp"),
            P("mp", None),
            P("mp"),
        ),
        check_vma=False,
    )
```

time: 1330 us -> 613 us (0.46)
  waiting for transfers between devices: 864 us -> 202 us
  matrix products: 272 us -> 108 us
  starting transfers between devices: 1.41 us -> 105 us
  Pallas kernels: 0 us -> 58.8 us
  other arithmetic: 121 us -> 70.3 us
  local copies, waits for them, and re-layouts: 25.9 us -> 56 us
  blocking collectives: 23.9 us -> 0 us
    reduce_scatter x5 -> x0, waiting for transfers between devices: 413 us -> none  [the longest x1 143 us: body(): lax.psum_scatter(jnp.dot(lax.slice_in_dim(context, 0, lax.axis_size('mp')...]
    all_gather x4 -> x0, waiting for transfers between devices: 300 us -> none  [the longest x1 81 us: body(): grad_attn_rows = lax.all_gather(grad_attention, 'mp', axis=0, tiled=True)]
    ppermute x0 -> x76, waiting for transfers between devices: none -> 202 us  [the longest x48 121 us: swap(): return lax.ppermute(value, 'dp', [(i, i ^ 1 << b) for i in range(n)])]
    dot_general x36, matrix products: 272 us -> 108 us  [dot(): lax.dot_general(a, b, (((ca,), (cb,)), ((), ())), preferred_element_type=...]
    psum x1 -> x0, waiting for transfers between devices: 151 us -> none  [body(): lax.psum((grad_qkv, grad_qv, grad_out, grad_fc1, grad_fc1_bias, grad_fc2,...]
    ppermute x0 -> x76, starting transfers between devices: none -> 105 us  [the longest x24 52.2 us: shift(): return lax.ppermute(value, 'mp', [(i, (i + s) % n) for i in range(n)])]
    pallas_call x0 -> x2, Pallas kernels: none -> 58.8 us  [the longest x1 32.7 us: attend_back(): pl.pallas_call(functools.partial(attend_back_kernel, halo), grid=(pairs,)...]
    convert_element_type x11 -> x20, other arithmetic: 62.7 us -> 10.6 us  [the longest x13 6.83 us: add(): return (a.astype(f32) + b.astype(f32)).astype(bf16)]
  transfers between devices with their start and end apart: 10 -> 76, of which waited for: 10 -> 24; matrix products, arithmetic and copies ran while one was open for 6% -> 28% of each run, Pallas kernels for 0% -> 4%
where the time goes in v1:
time: 613 us; the launch traced here: 604 us
  waiting for transfers between devices  202 us (33%)
  matrix products  108 us (18%)
  starting transfers between devices  105 us (17%)
  other arithmetic  70.3 us (11%)
  Pallas kernels  58.8 us (10%)
  local copies, waits for them, and re-layouts  56 us (9%)
    ppermute x48, waiting for transfers between devices, swap(): return lax.ppermute(value, 'dp', [(i, i ^ 1 << b) for i in range(n)])  121 us
    dot_general x36, matrix products, dot(): lax.dot_general(a, b, (((ca,), (cb,)), ((), ())), preferred_element_type=...  108 us
    ppermute x24, waiting for transfers between devices, shift(): return lax.ppermute(value, 'mp', [(i, (i + s) % n) for i in range(n)])  52.8 us
    ppermute x24, starting transfers between devices, shift(): return lax.ppermute(value, 'mp', [(i, (i + s) % n) for i in range(n)])  52.2 us
    ppermute x48, starting transfers between devices, swap(): return lax.ppermute(value, 'dp', [(i, i ^ 1 << b) for i in range(n)])  47.1 us
    pallas_call x1, Pallas kernels, attend_back(): pl.pallas_call(functools.partial(attend_back_kernel, halo), grid=(pairs,)...  32.7 us
    unnamed x162, local copies, waits for them, and re-layouts  29.4 us
    ppermute x2, waiting for transfers between devices, body(): lax.ppermute(grad_halo[at:at + n], 'mp', [(i, i - t) for i in range(t, mp)])  27.4 us
  transfers between devices with their start and end apart: 76, of which 24 were waited for; matrix products, arithmetic and copies ran while one was open for 28% of the time, Pallas kernels for 4%

profile of v1, /device:TPU:0, one launch (start us, length us, event | category | flops | bytes accessed | tf_op | source)
XLA Modules:
  0.0 603.7 jit_solution(6741597116934225999)
XLA Ops:
  5.9 5.1 collective-permute-start.4
  43.0 5.1 collective-permute-start.14
  50.3 13.2 %collective-permute-done.21 = bf16[128,1024]{1,0:T(8,128)(2,1)} collective-permute-done((bf16[128,1024]{1,0:T(8,128)(2,1)S(1)}, bf16[128,1024]{1,0:T(8,128)(2,1)}, u32[]{:S(2)}, u32[]{:S(2)}) %collective-permute-start.21) | collective-permute-done | bytes 262176 | tf_op jit(solution)/shard_map/ppermute | solution.py:184
  70.8 11.9 %collective-permute-done.14 = bf16[128,1024]{1,0:T(8,128)(2,1)S(1)} collective-permute-done((bf16[128,1024]{1,0:T(8,128)(2,1)S(1)}, bf16[128,1024]{1,0:T(8,128)(2,1)S(1)}, u32[]{:S(2)}, u32[]{:S(2)}) %collective-permute-start.14) | collective-permute-done | bytes 262176 | tf_op jit(solution)/shard_map/ppermute | solution.py:184
  100.4 14.8 %collective-permute-done.18 = bf16[3,64,1024]{2,1,0:T(8,128)(2,1)} collective-permute-done((bf16[3,64,1024]{2,1,0:T(8,128)(2,1)}, bf16[3,64,1024]{2,1,0:T(8,128)(2,1)}, u32[]{:S(2)}, u32[]{:S(2)}) %collective-permute-start.18) | collective-permute-done | bytes 393248 | tf_op jit(solution)/shard_map/ppermute | solution.py:179
  136.3 21.6 %collective-permute-done.19 = bf16[3,2,64,1024]{3,2,0,1:T(8,128)(2,1)S(1)} collective-permute-done((bf16[3,2,64,1024]{3,2,0,1:T(8,128)(2,1)S(1)}, bf16[3,2,64,1024]{3,2,0,1:T(8,128)(2,1)S(1)}, u32[]{:S(2)}, u32[]{:S(2)}) %collective-permute-start.19) | collective-permute-done | bytes 786464 | tf_op jit(solution)/shard_map/ppermute | solution.py:179
  174.2 26.1 %shard_map.254 = (bf16[512,1024]{1,0:T(8,128)(2,1)S(1)}, f32[8,2,512]{2,1,0:T(2,128)S(1)}) custom-call(f32[16]{0:T(128)S(1)} %reshape.362.slopes, s32[1,512]{1,0:T(1,128)S(1)} %constant_dynamic-slice_fusion.6.segq, s32[1280,1]{1,0:T(8,128)S(1)} %copy.117.segk, bf16[512,1024]{1,0:T(8,128)(2,1)S(1)} %add_convert_fusion.9.q_ref, ...), custom_call_target="tpu_custom_call" | custom-call | flops 8589934592 | bytes 7340032 | tf_op jit(solution)/shard_map/pallas_call | solution.py:114
  207.8 8.1 %fusion.180 = f32[512,2048]{1,0:T(8,128)} fusion(bf16[512,1024]{0,1:T(8,128)(2,1)S(1)} %add_convert_fusion.8, bf16[2048,1024]{1,0:T(8,128)(2,1)} %collective-permute-done.27), kind=kOutput, calls=%fused_computation.545 | convolution fusion | flops 2147483648 | bytes 9437184 | tf_op jit(solution)/shard_map/dot_general | solution.py:21
  215.9 5.2 convert_reduce_fusion.3
  228.8 8.1 %convert_reduce_fusion.2 = (f32[2048]{0:T(1024)S(1)}, bf16[512,2048]{1,0:T(8,128)(2,1)S(1)}) fusion(f32[512,2048]{1,0:T(8,128)} %fusion.180, f32[2048]{0:T(1024)S(1)} %bitcast.666, bf16[2048,1024]{1,0:T(8,128)(2,1)} %collective-permute-done.28, bf16[512,1024]{1,0:T(8,128)(2,1)S(1)} %copy-done.29), kind=kOutput, calls=%fused_computation.38 | convolution fusion | flops 2170550272 | bytes 11550720 | tf_op jit(solution)/shard_map/dot_general | solution.py:21
  236.8 6.0 multiply_reduce_fusion
  247.6 32.7 %shard_map.255 = (bf16[512,1024]{1,0:T(8,128)(2,1)S(1)}, bf16[1280,1024]{1,0:T(8,128)(2,1)}, bf16[1280,1024]{1,0:T(8,128)(2,1)}) custom-call(f32[16]{0:T(128)S(1)} %reshape.362.slopes, s32[1,512]{1,0:T(1,128)S(1)} %constant_dynamic-slice_fusion.6.segq, s32[1280,1]{1,0:T(8,128)S(1)} %copy.117.segk, bf16[512,1024]{1,0:T(8,128)(2,1)S(1)} %add_convert_fusion.9.q_ref, ...), custom_call_target="tpu_custom_call" | custom-call | flops 21474836480 | bytes 13631488 | tf_op jit(solution)/shard_map/pallas_call | solution.py:146
  303.4 4.4 convolution_convert_fusion.1
  307.8 5.3 convolution_convert_fusion
  321.1 6.4 %add_convert_fusion.7 = bf16[512,1024]{0,1:T(8,128)(2,1)} fusion(f32[512,1024]{0,1:T(8,128)S(1)} %copy-done.3, f32[512,1024]{0,1:T(8,128)} %fusion.165, bf16[2048,1024]{1,0:T(8,128)(2,1)} %collective-permute-done.28, f32[1024]{0:T(1024)S(1)} %copy-done.58, f32[512,2048]{1,0:T(8,128)S(1)} %copy-done.63, f32[2048]{0:T(1024)S(1)} %bitcast.668), kind=kOutput, calls=%fused_computation.121 | convolution fusion | flops 2160066560 | bytes 13643776 | tf_op jit(solution)/shard_map/dot_general | solution.py:21
  330.0 4.7 fusion.27
  334.7 27.4 %collective-permute-done.29 = bf16[256,1024]{0,1:T(8,128)(2,1)} collective-permute-done((bf16[256,1024]{0,1:T(8,128)(2,1)}, bf16[256,1024]{0,1:T(8,128)(2,1)}, u32[]{:S(2)}, u32[]{:S(2)}) %collective-permute-start.29) | collective-permute-done | bytes 524320 | tf_op jit(solution)/shard_map/ppermute | solution.py:476
  366.2 4.7 fusion.28
  381.4 5.4 collective-permute-done.36
  403.6 4.6 add_convert_fusion.1
  412.4 5.7 add_convert_fusion
  420.9 5.3 collective-permute-done.38
  429.7 19.0 %collective-permute-done.51 = bf16[4,2,64,1024]{3,2,0,1:T(8,128)(2,1)S(1)} collective-permute-done((bf16[4,2,64,1024]{3,2,0,1:T(8,128)(2,1)S(1)}, bf16[4,2,64,1024]{3,2,0,1:T(8,128)(2,1)S(1)}, u32[]{:S(2)}, u32[]{:S(2)}) %collective-permute-start.51) | collective-permute-done | bytes 1048608 | tf_op jit(solution)/shard_map/ppermute | solution.py:179
  452.6 18.6 %collective-permute-done.64 = bf16[4,2,64,1024]{3,2,0,1:T(8,128)(2,1)S(1)} collective-permute-done((bf16[4,2,64,1024]{3,2,0,1:T(8,128)(2,1)S(1)}, bf16[4,2,64,1024]{3,2,0,1:T(8,128)(2,1)S(1)}, u32[]{:S(2)}, u32[]{:S(2)}) %collective-permute-start.64) | collective-permute-done | bytes 1048608 | tf_op jit(solution)/shard_map/ppermute | solution.py:179
  475.0 9.2 %collective-permute-done.39 = bf16[4,128,512]{2,1,0:T(8,128)(2,1)S(1)} collective-permute-done((bf16[4,128,512]{2,1,0:T(8,128)(2,1)S(1)}, bf16[4,128,512]{2,1,0:T(8,128)(2,1)S(1)}, u32[]{:S(2)}, u32[]{:S(2)}) %collective-permute-start.39) | collective-permute-done | bytes 524320 | tf_op jit(solution)/shard_map/ppermute | solution.py:179
  487.3 8.1 %collective-permute-done.52 = bf16[4,64,1024]{2,1,0:T(8,128)(2,1)S(1)} collective-permute-done((bf16[4,64,1024]{2,1,0:T(8,128)(2,1)S(1)}, bf16[4,64,1024]{2,1,0:T(8,128)(2,1)S(1)}, u32[]{:S(2)}, u32[]{:S(2)}) %collective-permute-start.52) | collective-permute-done | bytes 524320 | tf_op jit(solution)/shard_map/ppermute | solution.py:179
  508.0 10.3 %collective-permute-done.43 = bf16[256,512]{1,0:T(8,128)(2,1)S(1)} collective-permute-done((bf16[256,512]{1,0:T(8,128)(2,1)S(1)}, bf16[256,512]{1,0:T(8,128)(2,1)S(1)}, u32[]{:S(2)}, u32[]{:S(2)}) %collective-permute-start.43) | collective-permute-done | bytes 262176 | tf_op jit(solution)/shard_map/ppermute | solution.py:184
  518.3 14.9 %collective-permute-start.69 = (bf16[128,1024]{1,0:T(8,128)(2,1)S(1)}, bf16[128,1024]{1,0:T(8,128)(2,1)S(1)}, u32[]{:S(2)}, u32[]{:S(2)}) collective-permute-start(bf16[128,1024]{1,0:T(8,128)(2,1)S(1)} %get-tuple-element.124), channel_id=1, source_target_pairs={{0,2},{1,3},{2,0},{3,1},{4,6},{5,7},{6,4},{7,5},{8,10},{9,11},{10,... | collective-permute-start | bytes 786440 | tf_op jit(solution)/shard_map/ppermute | solution.py:184
  536.8 5.3 collective-permute-done.56
  545.7 6.8 %collective-permute-done.69 = bf16[128,1024]{1,0:T(8,128)(2,1)S(1)} collective-permute-done((bf16[128,1024]{1,0:T(8,128)(2,1)S(1)}, bf16[128,1024]{1,0:T(8,128)(2,1)S(1)}, u32[]{:S(2)}, u32[]{:S(2)}) %collective-permute-start.69) | collective-permute-done | bytes 262176 | tf_op jit(solution)/shard_map/ppermute | solution.py:184
  568.6 4.7 collective-permute-done.59
  594.4 5.3 copy.154
  (537 shorter events, 266.6 us)
Async XLA Ops:
  5.9 31.2 %collective-permute-start.4 = (bf16[256,512]{1,0:T(8,128)(2,1)}, bf16[256,512]{1,0:T(8,128)(2,1)}, u32[]{:S(2)}, u32[]{:S(2)}) collective-permute-start(bf16[256,512]{1,0:T(8,128)(2,1)} %pad_maximum_fusion.29), channel_id=1, source_target_pairs={{0,3},{1,0},{2,1},{3,2},{4,7},{5,4},{6,5},{7,6},{8,11},{9,8},{10,9... | collective-permute-start | bytes 786440 | tf_op jit(solution)/shard_map/ppermute | solution.py:184
  37.1 28.9 %collective-permute-start.20 = (bf16[128,1024]{1,0:T(8,128)(2,1)S(1)}, bf16[128,1024]{1,0:T(8,128)(2,1)S(1)}, u32[]{:S(2)}, u32[]{:S(2)}) collective-permute-start(bf16[128,1024]{1,0:T(8,128)(2,1)S(1)} %get-tuple-element.108), channel_id=1, source_target_pairs={{0,1},{1,2},{2,3},{3,0},{4,5},{5,6},{6,7},{7,4},{8,9},{9,10},{10,1... | collective-permute-start | bytes 786440 | tf_op jit(solution)/shard_map/ppermute | solution.py:184
  38.7 29.9 %collective-permute-start.15 = (bf16[128,1024]{1,0:T(8,128)(2,1)S(1)}, bf16[128,1024]{1,0:T(8,128)(2,1)S(1)}, u32[]{:S(2)}, u32[]{:S(2)}) collective-permute-start(bf16[128,1024]{1,0:T(8,128)(2,1)S(1)} %bitcast.622), channel_id=1, source_target_pairs={{0,3},{1,0},{2,1},{3,2},{4,7},{5,4},{6,5},{7,6},{8,11},{9,8},{10,9... | collective-permute-start | bytes 786440 | tf_op jit(solution)/shard_map/ppermute | solution.py:184
  43.0 39.6 %collective-permute-start.14 = (bf16[128,1024]{1,0:T(8,128)(2,1)S(1)}, bf16[128,1024]{1,0:T(8,128)(2,1)S(1)}, u32[]{:S(2)}, u32[]{:S(2)}) collective-permute-start(bf16[128,1024]{1,0:T(8,128)(2,1)S(1)} %bitcast.623), channel_id=1, source_target_pairs={{0,2},{1,3},{2,0},{3,1},{4,6},{5,7},{6,4},{7,5},{8,10},{9,11},{10,... | collective-permute-start | bytes 786440 | tf_op jit(solution)/shard_map/ppermute | solution.py:184
  49.2 35.7 %collective-permute-start.13 = (bf16[128,1024]{1,0:T(8,128)(2,1)S(1)}, bf16[128,1024]{1,0:T(8,128)(2,1)S(1)}, u32[]{:S(2)}, u32[]{:S(2)}) collective-permute-start(bf16[128,1024]{1,0:T(8,128)(2,1)S(1)} %bitcast.624), channel_id=1, source_target_pairs={{0,1},{1,2},{2,3},{3,0},{4,5},{5,6},{6,7},{7,4},{8,9},{9,10},{10,1... | collective-permute-start | bytes 786440 | tf_op jit(solution)/shard_map/ppermute | solution.py:184
  86.5 31.4 %collective-permute-start.8 = (bf16[3,2,128,512]{3,2,1,0:T(8,128)(2,1)}, bf16[3,2,128,512]{3,2,1,0:T(8,128)(2,1)}, u32[]{:S(2)}, u32[]{:S(2)}) collective-permute-start(bf16[3,2,128,512]{3,2,1,0:T(8,128)(2,1)} %get-tuple-element.143), channel_id=1, source_target_pairs={{0,8},{4,12},{8,0},{12,4},{16,24},{20,28},{24,16},{28,20},{1,9},{5... | collective-permute-start | bytes 2359304 | tf_op jit(solution)/shard_map/ppermute | solution.py:179
  88.3 31.5 %collective-permute-start.6 = (bf16[3,2,128,512]{3,2,0,1:T(8,128)(2,1)}, bf16[3,2,128,512]{3,2,0,1:T(8,128)(2,1)}, u32[]{:S(2)}, u32[]{:S(2)}) collective-permute-start(bf16[3,2,128,512]{3,2,0,1:T(8,128)(2,1)} %get-tuple-element.141), channel_id=1, source_target_pairs={{0,16},{4,20},{8,24},{12,28},{16,0},{20,4},{24,8},{28,12},{1,17},{... | collective-permute-start | bytes 2359304 | tf_op jit(solution)/shard_map/ppermute | solution.py:179
  94.5 35.3 %collective-permute-start.1 = (bf16[512,1024]{0,1:T(8,128)(2,1)S(1)}, bf16[512,1024]{0,1:T(8,128)(2,1)S(1)}, u32[]{:S(2)}, u32[]{:S(2)}) collective-permute-start(bf16[512,1024]{0,1:T(8,128)(2,1)S(1)} %copy.108), channel_id=1, source_target_pairs={{0,1},{1,2},{2,3},{4,5},{5,6},{6,7},{8,9},{9,10},{10,11},{12,13},{... | collective-permute-start | bytes 3145736 | tf_op jit(solution)/shard_map/ppermute | solution.py:281
  97.3 31.0 %collective-permute-start = (bf16[256,1024]{0,1:T(8,128)(2,1)S(1)}, bf16[256,1024]{0,1:T(8,128)(2,1)S(1)}, u32[]{:S(2)}, u32[]{:S(2)}) collective-permute-start(bf16[256,1024]{0,1:T(8,128)(2,1)S(1)} %copy-done.43), channel_id=1, source_target_pairs={{0,2},{1,3},{4,6},{5,7},{8,10},{9,11},{12,14},{13,15},{16,18},{17,... | collective-permute-start | bytes 1572872 | tf_op jit(solution)/shard_map/ppermute | solution.py:281
  117.9 41.0 %collective-permute-start.26 = (bf16[3,2,64,1024]{3,2,1,0:T(8,128)(2,1)S(1)}, bf16[3,2,64,1024]{3,2,1,0:T(8,128)(2,1)S(1)}, u32[]{:S(2)}, u32[]{:S(2)}) collective-permute-start(bf16[3,2,64,1024]{3,2,1,0:T(8,128)(2,1)S(1)} %get-tuple-element.139), channel_id=1, source_target_pairs={{0,8},{4,12},{8,0},{12,4},{16,24},{20,28},{24,16},{28,20},{1,9},{5... | collective-permute-start | bytes 2359304 | tf_op jit(solution)/shard_map/ppermute | solution.py:179
  119.8 39.2 %collective-permute-start.24 = (bf16[3,2,64,1024]{3,2,0,1:T(8,128)(2,1)S(1)}, bf16[3,2,64,1024]{3,2,0,1:T(8,128)(2,1)S(1)}, u32[]{:S(2)}, u32[]{:S(2)}) collective-permute-start(bf16[3,2,64,1024]{3,2,0,1:T(8,128)(2,1)S(1)} %get-tuple-element.137), channel_id=1, source_target_pairs={{0,16},{4,20},{8,24},{12,28},{16,0},{20,4},{24,8},{28,12},{1,17},{... | collective-permute-start | bytes 2359304 | tf_op jit(solution)/shard_map/ppermute | solution.py:179
  127.2 41.9 %collective-permute-start.9 = (bf16[4,1024,512]{2,1,0:T(8,128)(2,1)S(1)}, bf16[4,1024,512]{2,1,0:T(8,128)(2,1)S(1)}, u32[]{:S(2)}, u32[]{:S(2)}) collective-permute-start(bf16[4,1024,512]{2,1,0:T(8,128)(2,1)S(1)} %bitcast.598), channel_id=1, source_target_pairs={{0,4},{4,0},{8,12},{12,8},{16,20},{20,16},{24,28},{28,24},{1,5},{5... | collective-permute-start | bytes 12582920 | tf_op jit(solution)/shard_map/ppermute | solution.py:179
  128.3 29.6 %collective-permute-start.19 = (bf16[3,2,64,1024]{3,2,0,1:T(8,128)(2,1)S(1)}, bf16[3,2,64,1024]{3,2,0,1:T(8,128)(2,1)S(1)}, u32[]{:S(2)}, u32[]{:S(2)}) collective-permute-start(bf16[3,2,64,1024]{3,2,0,1:T(8,128)(2,1)S(1)} %get-tuple-element.135), channel_id=1, source_target_pairs={{0,8},{4,12},{8,0},{12,4},{16,24},{20,28},{24,16},{28,20},{1,9},{5... | collective-permute-start | bytes 2359304 | tf_op jit(solution)/shard_map/ppermute | solution.py:179
  162.7 66.1 %collective-permute-start.28 = (bf16[2048,1024]{1,0:T(8,128)(2,1)}, bf16[2048,1024]{1,0:T(8,128)(2,1)}, u32[]{:S(2)}, u32[]{:S(2)}) collective-permute-start(bf16[2048,1024]{1,0:T(8,128)(2,1)} %bitcast.599), channel_id=1, source_target_pairs={{0,4},{4,0},{8,12},{12,8},{16,20},{20,16},{24,28},{28,24},{1,5},{5... | collective-permute-start | bytes 12582920 | tf_op jit(solution)/shard_map/ppermute | solution.py:179
  165.0 42.7 %collective-permute-start.27 = (bf16[2048,1024]{1,0:T(8,128)(2,1)}, bf16[2048,1024]{1,0:T(8,128)(2,1)}, u32[]{:S(2)}, u32[]{:S(2)}) collective-permute-start(bf16[2048,1024]{1,0:T(8,128)(2,1)} %bitcast.602), channel_id=1, source_target_pairs={{0,4},{4,0},{8,12},{12,8},{16,20},{20,16},{24,28},{28,24},{1,5},{5... | collective-permute-start | bytes 12582920 | tf_op jit(solution)/shard_map/ppermute | solution.py:179
  313.0 49.1 %collective-permute-start.30 = (bf16[512,1024]{0,1:T(8,128)(2,1)}, bf16[512,1024]{0,1:T(8,128)(2,1)}, u32[]{:S(2)}, u32[]{:S(2)}) collective-permute-start(bf16[512,1024]{0,1:T(8,128)(2,1)} %pad_maximum_fusion.9), channel_id=1, source_target_pairs={{1,0},{2,1},{3,2},{5,4},{6,5},{7,6},{9,8},{10,9},{11,10},{13,12},{... | collective-permute-start | bytes 3145736 | tf_op jit(solution)/shard_map/ppermute | solution.py:476
  314.3 47.8 %collective-permute-start.29 = (bf16[256,1024]{0,1:T(8,128)(2,1)}, bf16[256,1024]{0,1:T(8,128)(2,1)}, u32[]{:S(2)}, u32[]{:S(2)}) collective-permute-start(bf16[256,1024]{0,1:T(8,128)(2,1)} %pad_maximum_fusion.19), channel_id=1, source_target_pairs={{2,0},{3,1},{6,4},{7,5},{10,8},{11,9},{14,12},{15,13},{18,16},{19,... | collective-permute-start | bytes 1572872 | tf_op jit(solution)/shard_map/ppermute | solution.py:476
  319.9 75.8 %collective-permute-start.37 = (bf16[4,1024,512]{2,1,0:T(8,128)(2,1)}, bf16[4,1024,512]{2,1,0:T(8,128)(2,1)}, u32[]{:S(2)}, u32[]{:S(2)}) collective-permute-start(bf16[4,1024,512]{2,1,0:T(8,128)(2,1)} %pad_maximum_fusion.2), channel_id=1, source_target_pairs={{0,4},{4,0},{8,12},{12,8},{16,20},{20,16},{24,28},{28,24},{1,5},{5... | collective-permute-start | bytes 12582920 | tf_op jit(solution)/shard_map/ppermute | solution.py:179
  319.9 83.5 %collective-permute-start.50 = (bf16[2048,1024]{1,0:T(8,128)(2,1)}, bf16[2048,1024]{1,0:T(8,128)(2,1)}, u32[]{:S(2)}, u32[]{:S(2)}) collective-permute-start(bf16[2048,1024]{1,0:T(8,128)(2,1)} %convolution_convert_fusion.1), channel_id=1, source_target_pairs={{0,4},{4,0},{8,12},{12,8},{16,20},{20,16},{24,28},{28,24},{1,5},{5... | collective-permute-start | bytes 12582920 | tf_op jit(solution)/shard_map/ppermute | solution.py:179
  376.6 34.9 %collective-permute-start.63 = (bf16[2048,1024]{1,0:T(8,128)(2,1)}, bf16[2048,1024]{1,0:T(8,128)(2,1)}, u32[]{:S(2)}, u32[]{:S(2)}) collective-permute-start(bf16[2048,1024]{1,0:T(8,128)(2,1)} %convolution_convert_fusion), channel_id=1, source_target_pairs={{0,4},{4,0},{8,12},{12,8},{16,20},{20,16},{24,28},{28,24},{1,5},{5... | collective-permute-start | bytes 12582920 | tf_op jit(solution)/shard_map/ppermute | solution.py:179
  409.3 39.4 %collective-permute-start.51 = (bf16[4,2,64,1024]{3,2,0,1:T(8,128)(2,1)S(1)}, bf16[4,2,64,1024]{3,2,0,1:T(8,128)(2,1)S(1)}, u32[]{:S(2)}, u32[]{:S(2)}) collective-permute-start(bf16[4,2,64,1024]{3,2,0,1:T(8,128)(2,1)S(1)} %slice_bitcast_fusion.6), channel_id=1, source_target_pairs={{0,16},{4,20},{8,24},{12,28},{16,0},{20,4},{24,8},{28,12},{1,17},{... | collective-permute-start | bytes 3145736 | tf_op jit(solution)/shard_map/ppermute | solution.py:179
  410.1 40.6 %collective-permute-start.53 = (bf16[4,2,64,1024]{3,2,0,1:T(8,128)(2,1)S(1)}, bf16[4,2,64,1024]{3,2,0,1:T(8,128)(2,1)S(1)}, u32[]{:S(2)}, u32[]{:S(2)}) collective-permute-start(bf16[4,2,64,1024]{3,2,0,1:T(8,128)(2,1)S(1)} %slice_bitcast_fusion.4), channel_id=1, source_target_pairs={{0,8},{4,12},{8,0},{12,4},{16,24},{20,28},{24,16},{28,20},{1,9},{5... | collective-permute-start | bytes 3145736 | tf_op jit(solution)/shard_map/ppermute | solution.py:179
  419.0 52.1 %collective-permute-start.64 = (bf16[4,2,64,1024]{3,2,0,1:T(8,128)(2,1)S(1)}, bf16[4,2,64,1024]{3,2,0,1:T(8,128)(2,1)S(1)}, u32[]{:S(2)}, u32[]{:S(2)}) collective-permute-start(bf16[4,2,64,1024]{3,2,0,1:T(8,128)(2,1)S(1)} %slice_bitcast_fusion.2), channel_id=1, source_target_pairs={{0,16},{4,20},{8,24},{12,28},{16,0},{20,4},{24,8},{28,12},{1,17},{... | collective-permute-start | bytes 3145736 | tf_op jit(solution)/shard_map/ppermute | solution.py:179
  426.2 46.9 %collective-permute-start.66 = (bf16[4,2,64,1024]{3,2,0,1:T(8,128)(2,1)S(1)}, bf16[4,2,64,1024]{3,2,0,1:T(8,128)(2,1)S(1)}, u32[]{:S(2)}, u32[]{:S(2)}) collective-permute-start(bf16[4,2,64,1024]{3,2,0,1:T(8,128)(2,1)S(1)} %slice_bitcast_fusion), channel_id=1, source_target_pairs={{0,8},{4,12},{8,0},{12,4},{16,24},{20,28},{24,16},{28,20},{1,9},{5... | collective-permute-start | bytes 3145736 | tf_op jit(solution)/shard_map/ppermute | solution.py:179
  428.0 56.2 %collective-permute-start.39 = (bf16[4,128,512]{2,1,0:T(8,128)(2,1)S(1)}, bf16[4,128,512]{2,1,0:T(8,128)(2,1)S(1)}, u32[]{:S(2)}, u32[]{:S(2)}) collective-permute-start(bf16[4,128,512]{2,1,0:T(8,128)(2,1)S(1)} %slice_bitcast_fusion.34), channel_id=1, source_target_pairs={{0,8},{4,12},{8,0},{12,4},{16,24},{20,28},{24,16},{28,20},{1,9},{5... | collective-permute-start | bytes 1572872 | tf_op jit(solution)/shard_map/ppermute | solution.py:179
  448.7 36.2 %collective-permute-start.41 = (bf16[4,128,512]{2,1,0:T(8,128)(2,1)S(1)}, bf16[4,128,512]{2,1,0:T(8,128)(2,1)S(1)}, u32[]{:S(2)}, u32[]{:S(2)}) collective-permute-start(bf16[4,128,512]{2,1,0:T(8,128)(2,1)S(1)} %slice_bitcast_fusion.32), channel_id=1, source_target_pairs={{0,16},{4,20},{8,24},{12,28},{16,0},{20,4},{24,8},{28,12},{1,17},{... | collective-permute-start | bytes 1572872 | tf_op jit(solution)/shard_map/ppermute | solution.py:179
  450.7 44.7 %collective-permute-start.52 = (bf16[4,64,1024]{2,1,0:T(8,128)(2,1)S(1)}, bf16[4,64,1024]{2,1,0:T(8,128)(2,1)S(1)}, u32[]{:S(2)}, u32[]{:S(2)}) collective-permute-start(bf16[4,64,1024]{2,1,0:T(8,128)(2,1)S(1)} %slice_bitcast_fusion.30), channel_id=1, source_target_pairs={{0,8},{4,12},{8,0},{12,4},{16,24},{20,28},{24,16},{28,20},{1,9},{5... | collective-permute-start | bytes 1572872 | tf_op jit(solution)/shard_map/ppermute | solution.py:179
  473.2 30.1 %collective-permute-start.65 = (bf16[4,64,1024]{2,1,0:T(8,128)(2,1)S(1)}, bf16[4,64,1024]{2,1,0:T(8,128)(2,1)S(1)}, u32[]{:S(2)}, u32[]{:S(2)}) collective-permute-start(bf16[4,64,1024]{2,1,0:T(8,128)(2,1)S(1)} %slice_bitcast_fusion.26), channel_id=1, source_target_pairs={{0,8},{4,12},{8,0},{12,4},{16,24},{20,28},{24,16},{28,20},{1,9},{5... | collective-permute-start | bytes 1572872 | tf_op jit(solution)/shard_map/ppermute | solution.py:179
  503.3 30.0 %collective-permute-start.57 = (bf16[128,1024]{1,0:T(8,128)(2,1)S(1)}, bf16[128,1024]{1,0:T(8,128)(2,1)S(1)}, u32[]{:S(2)}, u32[]{:S(2)}) collective-permute-start(bf16[128,1024]{1,0:T(8,128)(2,1)S(1)} %get-tuple-element.126), channel_id=1, source_target_pairs={{0,1},{1,2},{2,3},{3,0},{4,5},{5,6},{6,7},{7,4},{8,9},{9,10},{10,1... | collective-permute-start | bytes 786440 | tf_op jit(solution)/shard_map/ppermute | solution.py:184
  505.2 36.8 %collective-permute-start.56 = (bf16[128,1024]{1,0:T(8,128)(2,1)S(1)}, bf16[128,1024]{1,0:T(8,128)(2,1)S(1)}, u32[]{:S(2)}, u32[]{:S(2)}) collective-permute-start(bf16[128,1024]{1,0:T(8,128)(2,1)S(1)} %get-tuple-element.127), channel_id=1, source_target_pairs={{0,2},{1,3},{2,0},{3,1},{4,6},{5,7},{6,4},{7,5},{8,10},{9,11},{10,... | collective-permute-start | bytes 786440 | tf_op jit(solution)/shard_map/ppermute | solution.py:184
  505.6 37.0 %collective-permute-start.55 = (bf16[128,1024]{1,0:T(8,128)(2,1)S(1)}, bf16[128,1024]{1,0:T(8,128)(2,1)S(1)}, u32[]{:S(2)}, u32[]{:S(2)}) collective-permute-start(bf16[128,1024]{1,0:T(8,128)(2,1)S(1)} %get-tuple-element.125), channel_id=1, source_target_pairs={{0,3},{1,0},{2,1},{3,2},{4,7},{5,4},{6,5},{7,6},{8,11},{9,8},{10,9... | collective-permute-start | bytes 786440 | tf_op jit(solution)/shard_map/ppermute | solution.py:184
  518.3 34.2 %collective-permute-start.69 = (bf16[128,1024]{1,0:T(8,128)(2,1)S(1)}, bf16[128,1024]{1,0:T(8,128)(2,1)S(1)}, u32[]{:S(2)}, u32[]{:S(2)}) collective-permute-start(bf16[128,1024]{1,0:T(8,128)(2,1)S(1)} %get-tuple-element.124), channel_id=1, source_target_pairs={{0,2},{1,3},{2,0},{3,1},{4,6},{5,7},{6,4},{7,5},{8,10},{9,11},{10,... | collective-permute-start | bytes 786440 | tf_op jit(solution)/shard_map/ppermute | solution.py:184
  (113 other events, 1354.3 us)

commit v2 on v1

v2 whole, which is shorter than its diff:
```python
import functools

import jax
import jax.numpy as jnp
from jax import lax
from jax.experimental import pallas as pl
from jax.experimental.pallas import tpu as pltpu
from jax.sharding import PartitionSpec as P

HEADS = 16
HD = 64
DOC_MOST = 768
QB = 256
MASKED = -1e12
eps = 1e-05
f32 = jnp.float32
bf16 = jnp.bfloat16


def dot(a, b, ca, cb):
    return lax.dot_general(a, b, (((ca,), (cb,)), ((), ())), preferred_element_type=f32)


def fill_mask(segq_ref, segk_ref, mask_ref, window, halo):
    for i in range(mask_ref.shape[0]):
        key_at = lax.broadcasted_iota(jnp.int32, (window, QB), 0) + i * QB
        query_at = lax.broadcasted_iota(jnp.int32, (window, QB), 1) + (i * QB + halo)
        same = segk_ref[i * QB : i * QB + window, :] == segq_ref[:, i * QB : (i + 1) * QB]
        allowed = same & (key_at <= query_at)
        mask_ref[i] = jnp.where(allowed, (key_at - query_at).astype(f32), MASKED)


def halves(rows):
    lane = lax.broadcasted_iota(jnp.int32, (rows, 2 * HD), 1)
    return [lane < HD, lane >= HD]


def attend_kernel(halo, slopes, segq, segk, q_ref, k_ref, v_ref, o_ref, lse_ref, mask_ref):
    window = halo + QB
    pair = pl.program_id(0)

    @pl.when(pair == 0)
    def _():
        fill_mask(segq, segk, mask_ref, window, halo)

    v_t = v_ref[...].T
    pick = halves(QB)
    for i in range(mask_ref.shape[0]):
        rows = slice(i * QB, (i + 1) * QB)
        keys = slice(i * QB, i * QB + window)
        query = q_ref[rows, :] * jnp.asarray(HD**-0.5, bf16)
        key_rows = k_ref[keys, :]
        out = []
        for h in range(2):
            q_h = jnp.where(pick[h], query, jnp.zeros_like(query))
            scores = dot(key_rows, q_h, 1, 1) + slopes[2 * pair + h] * mask_ref[i]
            top = jnp.max(scores, axis=0, keepdims=True)
            expo = jnp.exp(scores - top)
            total = jnp.sum(expo, axis=0, keepdims=True)
            o_t = dot(v_t[:, keys], expo.astype(bf16), 1, 0)
            out.append(o_t[h * HD : (h + 1) * HD, :] * (1.0 / total))
            lse_ref[0, h : h + 1, rows] = top + jnp.log(total)
        o_ref[rows, :] = jnp.concatenate(out, axis=0).T.astype(bf16)


def attend_back_kernel(
    halo, slopes, segq, segk, q_ref, k_ref, v_ref, g_ref, lse_ref, dq_ref, dk_ref, dv_ref,
    mask_ref, dk_acc, dv_acc,
):
    window = halo + QB
    pair = pl.program_id(0)

    @pl.when(pair == 0)
    def _():
        fill_mask(segq, segk, mask_ref, window, halo)

    k_t = k_ref[...].T
    pick = halves(QB)
    dk_acc[...] = jnp.zeros_like(dk_acc)
    dv_acc[...] = jnp.zeros_like(dv_acc)
    for i in range(mask_ref.shape[0]):
        rows = slice(i * QB, (i + 1) * QB)
        keys = slice(i * QB, i * QB + window)
        query = q_ref[rows, :] * jnp.asarray(HD**-0.5, bf16)
        grad = g_ref[rows, :]
        key_rows = k_ref[keys, :]
        value_rows = v_ref[keys, :]
        out = []
        for h in range(2):
            q_h = jnp.where(pick[h], query, jnp.zeros_like(query))
            g_h = jnp.where(pick[h], grad, jnp.zeros_like(grad))
            scores = dot(key_rows, q_h, 1, 1) + slopes[2 * pair + h] * mask_ref[i]
            probs = jnp.exp(scores - lse_ref[0, h : h + 1, rows])
            grad_probs = dot(value_rows, g_h, 1, 1)
            delta = jnp.sum(probs * grad_probs, axis=0, keepdims=True)
            grad_scores = (probs * (grad_probs - delta)).astype(bf16)
            dv_acc[keys, :] += dot(probs.astype(bf16), g_h, 1, 0)
            dk_acc[keys, :] += dot(grad_scores, q_h, 1, 0)
            dq_t = dot(k_t[:, keys], grad_scores, 1, 0)
            out.append(dq_t[h * HD : (h + 1) * HD, :])
        dq_ref[rows, :] = (jnp.concatenate(out, axis=0).T * HD**-0.5).astype(bf16)
    dk_ref[...] = dk_acc[...].astype(bf16)
    dv_ref[...] = dv_acc[...].astype(bf16)


def attend(slopes, segq, segk, q, k, v):
    rows, wide = q.shape
    ext = k.shape[0]
    halo = ext - rows
    pairs = wide // (2 * HD)
    blocks = rows // QB
    col = lambda n: pl.BlockSpec((n, 2 * HD), lambda p: (0, p))
    work = pairs * 2 * blocks * (halo + QB) * QB
    return pl.pallas_call(
        functools.partial(attend_kernel, halo),
        grid=(pairs,),
        in_specs=[
            pl.BlockSpec(memory_space=pltpu.SMEM),
            pl.BlockSpec((1, rows), lambda p: (0, 0)),
            pl.BlockSpec((ext, 1), lambda p: (0, 0)),
            col(rows),
            col(ext),
            col(ext),
        ],
        out_specs=[col(rows), pl.BlockSpec((1, 2, rows), lambda p: (p, 0, 0))],
        out_shape=[
            jax.ShapeDtypeStruct((rows, wide), bf16),
            jax.ShapeDtypeStruct((pairs, 2, rows), f32),
        ],
        scratch_shapes=[pltpu.VMEM((blocks, halo + QB, QB), f32)],
        compiler_params=pltpu.CompilerParams(vmem_limit_bytes=40 << 20),
        cost_estimate=pl.CostEstimate(
            flops=work * 256 * 4, bytes_accessed=2 * wide * (2 * rows + 2 * ext), transcendentals=work
        ),
    )(slopes, segq, segk, q, k, v)


def attend_back(slopes, segq, segk, q, k, v, grad, lse):
    rows, wide = q.shape
    ext = k.shape[0]
    halo = ext - rows
    pairs = wide // (2 * HD)
    blocks = rows // QB
    col = lambda n: pl.BlockSpec((n, 2 * HD), lambda p: (0, p))
    work = pairs * 2 * blocks * (halo + QB) * QB
    return pl.pallas_call(
        functools.partial(attend_back_kernel, halo),
        grid=(pairs,),
        in_specs=[
            pl.BlockSpec(memory_space=pltpu.SMEM),
            pl.BlockSpec((1, rows), lambda p: (0, 0)),
            pl.BlockSpec((ext, 1), lambda p: (0, 0)),
            col(rows),
            col(ext),
            col(ext),
            col(rows),
            pl.BlockSpec((1, 2, rows), lambda p: (p, 0, 0)),
        ],
        out_specs=[col(rows), col(ext), col(ext)],
        out_shape=[
            jax.ShapeDtypeStruct((rows, wide), bf16),
            jax.ShapeDtypeStruct((ext, wide), bf16),
            jax.ShapeDtypeStruct((ext, wide), bf16),
        ],
        scratch_shapes=[
            pltpu.VMEM((blocks, halo + QB, QB), f32),
            pltpu.VMEM((ext, 2 * HD), f32),
            pltpu.VMEM((ext, 2 * HD), f32),
        ],
        compiler_params=pltpu.CompilerParams(vmem_limit_bytes=48 << 20),
        cost_estimate=pl.CostEstimate(
            flops=work * 256 * 10, bytes_accessed=2 * wide * (3 * rows + 4 * ext), transcendentals=work
        ),
    )(slopes, segq, segk, q, k, v, grad, lse)


def own_att_kernel(at, qkv_ref, out_ref, own_ref):
    for t, rows in enumerate((qkv_ref[0], out_ref[...], qkv_ref[1], qkv_ref[2])):
        half = rows.shape[1] // 2
        left, right = rows[:, :half], rows[:, half:]
        own_ref[0, t, 0] = jnp.where(at[0] == 0, left, right)
        own_ref[1, t, 0] = jnp.where(at[0] == 0, right, left)


def own_att(at, qkv_t, out_weight):
    wide = out_weight.shape[1]
    return pl.pallas_call(
        own_att_kernel,
        grid_spec=pltpu.PrefetchScalarGridSpec(
            num_scalar_prefetch=1,
            grid=(4,),
            in_specs=[
                pl.BlockSpec((3, HD, wide), lambda p, at: (0, at[1 + p], 0)),
                pl.BlockSpec((HD, wide), lambda p, at: (at[1 + p], 0)),
            ],
            out_specs=pl.BlockSpec((2, 4, 1, HD, wide // 2), lambda p, at: (0, 0, p, 0, 0)),
        ),
        out_shape=jax.ShapeDtypeStruct((2, 4, 4, HD, wide // 2), bf16),
    )(at, qkv_t, out_weight)


def own_ff_kernel(at, fc1_ref, fc2_ref, o1_ref, o2_ref):
    o1_ref[...] = fc1_ref[...].T
    o2_ref[...] = fc2_ref[...]


def own_ff(at, fc1_weight, fc2_weight):
    hidden, wide = fc2_weight.shape
    piece = hidden // 8
    return pl.pallas_call(
        own_ff_kernel,
        grid_spec=pltpu.PrefetchScalarGridSpec(
            num_scalar_prefetch=1,
            grid=(8,),
            in_specs=[
                pl.BlockSpec((wide, piece), lambda i, at: (0, at[i])),
                pl.BlockSpec((piece, wide), lambda i, at: (at[i], 0)),
            ],
            out_specs=[pl.BlockSpec((piece, wide), lambda i, at: (i, 0))] * 2,
        ),
        out_shape=[jax.ShapeDtypeStruct((hidden, wide), bf16)] * 2,
    )(at, fc1_weight, fc2_weight)


def join_att_kernel(core, own_ref, x0_ref, x1_ref, y_ref, out_ref):
    p1, p2 = x1_ref[:, 0], y_ref[0, :, 0]
    first = core[0] == 0
    out_ref[0, :, 0] = own_ref[0]
    out_ref[0, 0, 1:] = x0_ref[:, 0]
    out_ref[0, 1, 1:] = jnp.where(first, p1, p2)
    out_ref[0, 2, 1:] = jnp.where(first, p2, p1)
    out_ref[0, 3, 1:] = y_ref[1, :, 0]


def join_att(core, own, x0, x1, y):
    rest, _, hd, half = x0.shape
    one = pl.BlockSpec((rest, 1, hd, half), lambda t: (0, t, 0, 0))
    return pl.pallas_call(
        join_att_kernel,
        grid=(4,),
        in_specs=[
            pl.BlockSpec(memory_space=pltpu.SMEM),
            pl.BlockSpec((1, 4, hd, half), lambda t: (t, 0, 0, 0)),
            one,
            one,
            pl.BlockSpec((2, rest, 1, hd, half), lambda t: (0, 0, t, 0, 0)),
        ],
        out_specs=pl.BlockSpec((1, 4, rest + 1, hd, half), lambda t: (t, 0, 0, 0, 0)),
        out_shape=jax.ShapeDtypeStruct((4, 4, rest + 1, hd, half), bf16),
    )(core, own, x0, x1, y)


def add_att_kernel(at, *refs):
    mine, theirs, (hi_ref, lo_ref) = refs[:4], refs[4:8], refs[8:]
    i = pl.program_id(0)
    for t in range(4):
        total = (mine[t][...].astype(f32) + theirs[t][...].astype(f32)).astype(bf16)

        @pl.when(i < 2)
        def _():
            hi_ref[0, t] = total

        @pl.when(i >= 2)
        def _():
            lo_ref[0, t] = total


def add_att(at, mine, theirs):
    rows, half = mine[0].shape
    block = pl.BlockSpec((rows // 4, half), lambda i, at: (at[i], 0))
    shape = jax.ShapeDtypeStruct((2, 4, rows // 4, half), bf16)
    return pl.pallas_call(
        add_att_kernel,
        grid_spec=pltpu.PrefetchScalarGridSpec(
            num_scalar_prefetch=1,
            grid=(4,),
            in_specs=[block] * 8,
            out_specs=[
                pl.BlockSpec((1, 4, rows // 4, half), lambda i, at: (jnp.minimum(i, 1), 0, 0, 0)),
                pl.BlockSpec((1, 4, rows // 4, half), lambda i, at: (jnp.maximum(i - 2, 0), 0, 0, 0)),
            ],
        ),
        out_shape=[shape, shape],
    )(at, *mine, *theirs)


def swap(value, b):
    n = lax.axis_size("dp")
    return lax.ppermute(value, "dp", [(i, i ^ (1 << b)) for i in range(n)])


def hop(value, stage):
    n = lax.axis_size("dp")
    return lax.ppermute(
        value, "dp", [(i, i ^ (2 if (i & 1) == stage - 1 else 4)) for i in range(n)]
    )


def move(value, pairs):
    return lax.ppermute(value, "mp", pairs)


def shift(value, s):
    n = lax.axis_size("mp")
    return move(value, [(i, (i + s) % n) for i in range(n)])


def all_eight(value):
    n = lax.axis_size("dp")
    groups = None if n == 8 else [list(range(g, g + 8)) for g in range(0, n, 8)]
    return lax.all_gather(value, "dp", axis=0, axis_index_groups=groups)


def beyond(value):
    for b in range(3, lax.axis_size("dp").bit_length() - 1):
        value = value + swap(value, b)
    return value


def add(a, b):
    return (a.astype(f32) + b.astype(f32)).astype(bf16)


tie = lax.optimization_barrier
NEAR = [(0, 1), (1, 0), (2, 3), (3, 2)]
MIDDLE = [(1, 2), (2, 1)]
OUTWARD = [(1, 0), (2, 3)]
INWARD = [(0, 1), (3, 2)]


def norm_parts(rows):
    mean = jnp.mean(rows, axis=-1, keepdims=True)
    centred = rows - mean
    rstd = lax.rsqrt(jnp.mean(centred * centred, axis=-1, keepdims=True) + eps)
    return centred * rstd, rstd


def norm_back(grad, gain, xhat, rstd):
    scaled = grad * gain
    return rstd * (
        scaled
        - jnp.mean(scaled, axis=-1, keepdims=True)
        - xhat * jnp.mean(scaled * xhat, axis=-1, keepdims=True)
    )


def gelu_both(v):
    c, k = 0.7978845608028654, 0.044715
    t = jnp.tanh(c * (v + k * v * v * v))
    value = 0.5 * v * (1.0 + t)
    slope = 0.5 * (1.0 + t) + 0.5 * v * (1.0 - t * t) * (c * (1.0 + 3.0 * k * v * v))
    return value, slope


def body(
    tokens,
    segment_ids,
    norm1_gain,
    norm1_shift,
    qkv_weight,
    qv_bias,
    out_weight,
    out_bias,
    norm2_gain,
    norm2_shift,
    fc1_weight,
    fc1_bias,
    fc2_weight,
    fc2_bias,
    out_grad,
):
    rows, wide = tokens.shape
    half = wide // 2
    mp = lax.axis_size("mp")
    m = lax.axis_index("mp")
    d = lax.axis_index("dp") & 7
    core = d & 1
    ff_here = fc1_weight.shape[1]
    piece = ff_here // 8
    heads_here = qkv_weight.shape[2] // HD
    rest = mp - 1

    b1 = jnp.where(core == 0, 2, 4)
    b2 = 6 - b1
    zero = jnp.zeros_like(b1)
    mine_masks = jnp.stack([zero, b1, b2, zero + 6])
    their_masks = jnp.stack([zero + 1, 1 + b2, 1 + b1, zero + 7])
    slices = d ^ jnp.concatenate([mine_masks, their_masks])
    place = (d >> 1) ^ jnp.arange(4)
    far = jnp.where(m < 2, 2, 1)
    ff_blocks = jnp.stack([m ^ 1, far, far ^ 1])
    ff_rows = jnp.concatenate(
        [m * 8 + slices]
        + [(ff_blocks[None, :] * 8 + slices[i : i + 2, None]).reshape(-1) for i in range(0, 8, 2)]
    )
    att_blocks = (m + mp - jnp.arange(mp)) % mp
    heads = (att_blocks[None, :] * heads_here + place[:, None]).reshape(-1)
    slopes = jnp.exp2(-8.0 * (heads + 1).astype(f32) / HEADS)

    qkv_t = jnp.transpose(qkv_weight, (1, 2, 0))
    own = own_att(jnp.concatenate([core[None], place]), qkv_t, out_weight)
    att_me = own[0, :, 0]
    att_z = [shift(att_me, s) for s in range(1, mp)]

    near_rows = DOC_MOST - rows
    tokens_late, _ = tie((tokens, att_me))
    halo1 = move(tokens_late, [(i, i + 1) for i in range(mp - 1)])
    halo2 = move(halo1[rows - near_rows :], [(i, i + 1) for i in range(mp - 1)])
    halo = DOC_MOST

    own1, own2 = own_ff(slices, fc1_weight, fc2_weight)
    ff_me = jnp.concatenate([own1[:piece], own2[:piece]])
    ff_near = move(ff_me, NEAR)
    ff_mid = move(jnp.concatenate([ff_me, ff_near]), MIDDLE)
    ff_out = move(ff_mid, OUTWARD)
    ff_far = jnp.where((m == 1) | (m == 2), ff_mid, ff_out)
    ff_x0 = jnp.concatenate(
        [
            ff_near[:piece],
            ff_far[:piece],
            ff_far[2 * piece : 3 * piece],
            ff_near[piece:],
            ff_far[piece : 2 * piece],
            ff_far[3 * piece :],
        ]
    )

    bias_all = lax.all_gather(jnp.concatenate([fc1_bias, qv_bias.reshape(-1)]), "mp", axis=0)
    fc1_b = bias_all[:, :ff_here].reshape(mp * 8, piece)[ff_rows].reshape(-1)
    qv_b = bias_all[:, ff_here:].reshape(mp, 2, heads_here, HD)
    qv_b = jnp.transpose(qv_b, (0, 2, 1, 3)).reshape(mp * heads_here, 2 * HD)[heads]
    q_bias, v_bias = qv_b[:, :HD].reshape(-1), qv_b[:, HD:].reshape(-1)

    att_x0 = jnp.stack(att_z)
    att_x1 = hop(att_x0, 1)
    att_y = hop(jnp.stack([att_x0, att_x1]), 2)
    att_mine = join_att(core[None], own[0], att_x0, att_x1, att_y)
    att_mine = att_mine.reshape(4, HEADS * HD, half)
    w_att = [att_mine, swap(att_mine, 0)]

    ext = jnp.concatenate([halo2, halo1, tokens], 0).astype(f32)
    xhat_ext, rstd_ext = norm_parts(ext)
    norm1 = (xhat_ext * norm1_gain + norm1_shift).astype(bf16)
    col = [core * half, (1 - core) * half]

    def cols(value):
        return [lax.dynamic_slice_in_dim(value, at, half, 1) for at in col]

    def join(own, other):
        first = core == 0
        return jnp.concatenate([jnp.where(first, own, other), jnp.where(first, other, own)], 1)

    n1 = cols(norm1)

    def project(t, lhs):
        return dot(lhs[0], w_att[0][t], 1, 1) + dot(lhs[1], w_att[1][t], 1, 1)

    q = (project(0, [v[halo:] for v in n1]) + q_bias).astype(bf16)
    k = project(2, n1).astype(bf16)
    v = (project(3, n1) + v_bias).astype(bf16)

    seg_row = jnp.concatenate([jnp.full((1, halo), -1, jnp.int32), segment_ids], 1)
    segk = lax.dynamic_slice_in_dim(seg_row, m * rows, halo + rows, 1)
    segq = segk[:, halo:]
    segk = segk.reshape(halo + rows, 1)

    q, ff_x0 = tie((q, ff_x0))
    ff_x1 = hop(ff_x0, 1)
    cut = rest * piece
    z1 = jnp.concatenate([ff_x0[:cut], ff_x1[:cut]])
    z2 = jnp.concatenate([ff_x0[cut:], ff_x1[cut:]])
    y1, y2 = hop(z1, 2), hop(z2, 2)
    w1 = [own1, z1, y1, swap(z1, 0), swap(y1, 0)]
    w2 = [own2, z2, y2, swap(z2, 0), swap(y2, 0)]

    context, lse = attend(slopes, segq, segk, q, k, v)
    attention = join(dot(context, w_att[0][1], 1, 0), dot(context, w_att[1][1], 1, 0))
    tokens_wide = tokens.astype(f32)
    resid = attention + out_bias + tokens_wide
    xhat2, rstd2 = norm_parts(resid)
    norm2 = (xhat2 * norm2_gain + norm2_shift).astype(bf16)

    pre, at = [], 0
    for w in w1:
        pre.append(dot(norm2, w, 1, 1) + fc1_b[at : at + w.shape[0]])
        at += w.shape[0]
    hidden = [gelu_both(p)[0].astype(bf16) for p in pre]

    def partials(lhs, rhs):
        send = [lhs[3], lhs[4], lhs[0][:, 4 * piece :]]
        return [dot(v, rhs, 0, 0).astype(bf16) for v in send]

    def after_core(lhs, rhs, got):
        hi = jnp.concatenate(
            [
                (dot(lhs[2], rhs, 0, 0) + got[1].astype(f32)).astype(bf16),
                (dot(lhs[0][:, 2 * piece : 4 * piece], rhs, 0, 0) + got[2][2 * piece :].astype(f32)).astype(bf16),
            ]
        )
        lo = [
            (dot(lhs[1], rhs, 0, 0) + got[0].astype(f32)).astype(bf16),
            (dot(lhs[0][:, : 2 * piece], rhs, 0, 0) + got[2][: 2 * piece].astype(f32)).astype(bf16),
        ]
        return hi, lo

    def after_hop2(lo, got):
        send = jnp.concatenate([add(lo[0][cut:], got[cut : 2 * cut]), add(lo[1][piece:], got[2 * cut + piece :])])
        keep = [add(lo[0][:cut], got[:cut]), add(lo[1][:piece], got[2 * cut : 2 * cut + piece])]
        return send, keep

    def along_mp(keep, got):
        near = add(keep[0][:piece], got[:piece])
        far = add(keep[0][piece:], got[piece:cut])
        mine = keep[1].astype(f32) + got[cut:].astype(f32)
        far = add(far, move(far, INWARD))
        back = move(far, MIDDLE)
        mine = mine + back[:piece].astype(f32)
        near = add(near, back[piece:])
        return beyond(mine + move(near, NEAR).astype(f32)).astype(bf16)

    send2 = partials(hidden, out_grad)
    got2 = [swap(v, 0) for v in send2]
    mlp = sum(dot(h, w, 1, 0) for h, w in zip(hidden, w2))
    result = (mlp + fc2_bias + resid).astype(bf16)
    grad_pre = [
        (dot(out_grad, w, 1, 1) * gelu_both(p)[1]).astype(bf16) for w, p in zip(w2, pre)
    ]
    send1 = partials(grad_pre, norm2)
    got1 = [swap(v, 0) for v in send1]
    hi2, lo2 = after_core(hidden, out_grad, got2)
    hop2_2 = hop(hi2, 2)

    grad_norm2 = sum(dot(g, w, 1, 0) for g, w in zip(grad_pre, w1))
    out_grad_wide = out_grad.astype(f32)
    grad_resid = out_grad_wide + norm_back(grad_norm2, norm2_gain, xhat2, rstd2)
    hi1, lo1 = after_core(grad_pre, norm2, got1)
    grad_att = cols(grad_resid.astype(bf16))
    grad_context = (
        dot(grad_att[0], w_att[0][1], 1, 1) + dot(grad_att[1], w_att[1][1], 1, 1)
    ).astype(bf16)

    grad_context, hi1, hop2_2 = tie((grad_context, hi1, hop2_2))
    hop2_1 = hop(hi1, 2)
    send2, keep2 = after_hop2(lo2, hop2_2)
    hop1_2 = hop(send2, 1)
    dq, dk, dv = attend_back(slopes, segq, segk, q, k, v, grad_context, lse)
    dq, hop2_1, hop1_2 = tie((dq, hop2_1, hop1_2))
    send1, keep1 = after_hop2(lo1, hop2_1)
    hop1_1 = hop(send1, 1)
    sum2 = along_mp(keep2, hop1_2)

    def weights_half(i):
        return [
            dot(dq, n1[i][halo:], 0, 0).astype(bf16),
            dot(context, grad_att[i], 0, 0).astype(bf16),
            dot(dk, n1[i], 0, 0).astype(bf16),
            dot(dv, n1[i], 0, 0).astype(bf16),
        ]

    theirs = [swap(v, 0) for v in weights_half(1)]
    mine = weights_half(0)
    slots = jnp.where(core == 0, jnp.asarray([2, 3, 0, 1]), jnp.asarray([1, 3, 0, 2]))
    att_hi, att_lo = add_att(slots, mine, theirs)
    att_got = hop(att_hi, 2)
    sum1 = along_mp(keep1, hop1_1)
    ff_sums = all_eight(jnp.stack([sum1, sum2]))
    att_keep = add(att_lo[0], att_got[0]), add(att_lo[1], att_got[1])
    att_keep = add(att_keep[0], hop(att_keep[1], 1)).reshape(4, mp, HD, half)
    att_sum = att_keep[:, 0].astype(f32)
    for s in range(1, mp):
        att_sum = att_sum + shift(att_keep[:, s], mp - s).astype(f32)
    att_sum = all_eight(beyond(att_sum).astype(bf16))
    att_sum = att_sum.reshape(4, 2, 4, HD, half)
    grad_out = jnp.transpose(att_sum[:, :, 1], (0, 2, 1, 3)).reshape(4 * HD, wide).astype(f32)
    grad_qkv = jnp.transpose(
        jnp.stack([att_sum[:, :, 0], att_sum[:, :, 2], att_sum[:, :, 3]]), (2, 4, 0, 1, 3)
    ).reshape(wide, 3, 4 * HD).astype(f32)
    grad_fc1 = ff_sums[:, 0].reshape(ff_here, wide).T.astype(f32)
    grad_fc2 = ff_sums[:, 1].reshape(ff_here, wide).astype(f32)

    def back_half(i):
        tail = dot(dk, w_att[i][2], 1, 0) + dot(dv, w_att[i][3], 1, 0)
        return tail[:halo], tail[halo:] + dot(dq, w_att[i][0], 1, 0)

    back = [back_half(0), back_half(1)]
    grad_halo = join(back[0][0], back[1][0])
    grad_norm1 = join(back[0][1], back[1][1])
    down = [(i, i - 1) for i in range(1, mp)]
    passed = move(grad_halo[:near_rows].astype(bf16), down).astype(f32)
    near = grad_halo[near_rows:]
    near = jnp.concatenate([near[: rows - near_rows], near[rows - near_rows :] + passed])
    grad_norm1 = grad_norm1 + move(near.astype(bf16), down).astype(f32)
    xhat1, rstd1 = xhat_ext[halo:], rstd_ext[halo:]
    in_grad = grad_resid + norm_back(grad_norm1, norm1_gain, xhat1, rstd1)

    ff_bias = jnp.concatenate([jnp.sum(g.astype(f32), axis=0) for g in grad_pre])
    ff_bias = ff_bias.reshape(mp * 8, piece)
    qv_sums = jnp.concatenate(
        [jnp.sum(g.astype(f32), axis=0).reshape(mp * heads_here, HD) for g in (dq, dv[:, :])], 1
    )

    def in_order(table, at):
        n = table.shape[0]
        pick = (at[None, :] == jnp.arange(n)[:, None]).astype(f32)
        return lax.dot(pick, table, precision=lax.Precision.HIGHEST)

    small = jnp.stack(
        [
            jnp.sum(grad_resid, axis=0),
            jnp.sum(grad_norm1 * xhat1, axis=0),
            jnp.sum(grad_norm1, axis=0),
            jnp.sum(grad_norm2 * xhat2, axis=0),
            jnp.sum(grad_norm2, axis=0),
            jnp.sum(out_grad_wide, axis=0),
        ]
    )
    n_small = wide // mp
    vectors = jnp.concatenate(
        [
            jnp.transpose(small.reshape(6, mp, n_small), (1, 0, 2)).reshape(mp, -1),
            in_order(qv_sums, heads).reshape(mp, -1),
            in_order(ff_bias, ff_rows).reshape(mp, -1),
        ],
        1,
    )
    vectors = lax.psum(vectors, ("dp", "mp"))
    total = lax.dynamic_index_in_dim(vectors, m, 0, False)
    six = total[: 6 * n_small].reshape(6, n_small)
    n_qv = heads_here * HD
    grad_qv = total[6 * n_small : 6 * n_small + 2 * n_qv].reshape(heads_here, 2, HD)
    grad_qv = jnp.transpose(grad_qv, (1, 0, 2)).reshape(2, n_qv)
    grad_fc1_bias = total[6 * n_small + 2 * n_qv :]
    return (
        result,
        in_grad,
        six[1],
        six[2],
        grad_qkv,
        grad_qv,
        grad_out,
        six[0],
        six[3],
        six[4],
        grad_fc1,
        grad_fc1_bias,
        grad_fc2,
        six[5],
    )


def solution(mesh):
    placed = (
        P(("dp", "mp"), None),
        P("dp", None),
        P(),
        P(),
        P(None, None, "mp"),
        P(None, "mp"),
        P("mp", None),
        P(),
        P(),
        P(),
        P(None, "mp"),
        P("mp"),
        P("mp", None),
        P(),
        P(("dp", "mp"), None),
    )
    return jax.shard_map(
        body,
        mesh=mesh,
        in_specs=placed,
        out_specs=(
            P(("dp", "mp"), None),
            P(("dp", "mp"), None),
            P("mp"),
            P("mp"),
            P(None, None, "mp"),
            P(None, "mp"),
            P("mp", None),
            P("mp"),
            P("mp"),
            P("mp"),
            P(None, "mp"),
            P("mp"),
            P("mp", None),
            P("mp"),
        ),
        check_vma=False,
    )
```

time: 613 us -> 635 us (1.036)
  blocking collectives: 0 us -> 72.3 us
  waiting for transfers between devices: 202 us -> 157 us
  starting transfers between devices: 105 us -> 76.9 us
  Pallas kernels: 58.8 us -> 82.4 us
  other arithmetic: 70.3 us -> 49.5 us
  between operations: 3.13 us -> 16.1 us
  local copies, waits for them, and re-layouts: 56 us -> 64 us
    ppermute x48 -> x15, waiting for transfers between devices: 121 us -> 0.04 us  [swap(): return lax.ppermute(value, 'dp', [(i, i ^ 1 << b) for i in range(n)])]
    ppermute x28 -> x30, waiting for transfers between devices: 81.2 us -> 157 us  [the longest x11 78.7 us: hop(): lax.ppermute(value, 'dp', [(i, i ^ (2 if i & 1 == stage - 1 else 4)) for...]
    ppermute x48 -> x15, starting transfers between devices: 47.1 us -> 2.68 us  [swap(): return lax.ppermute(value, 'dp', [(i, i ^ 1 << b) for i in range(n)])]
    psum x0 -> x1, blocking collectives: none -> 39.4 us  [body(): vectors = lax.psum(vectors, ('dp', 'mp'))]
    all_gather x0 -> x1, blocking collectives: none -> 32.9 us  [body(): lax.all_gather(jnp.concatenate([fc1_bias, qv_bias.reshape(-1)]), 'mp', ax...]
    pallas_call x0 -> x4, Pallas kernels: none -> 24 us  [the longest x1 7.38 us: add_att(): pl.pallas_call(add_att_kernel, grid_spec=pltpu.PrefetchScalarGridSpec(num...]
    ppermute x28 -> x30, starting transfers between devices: 58.3 us -> 74.1 us  [the longest x19 60.1 us: move(): return lax.ppermute(value, 'mp', pairs)]
    another operation x21 -> x0, local copies, waits for them, and re-layouts: 13.1 us -> none  [the longest x9 6.94 us: gather_blocks(): jnp.stack([r[:cut] for r in both])]
  transfers between devices with their start and end apart: 76 -> 47, of which waited for: 24 -> 16; matrix products, arithmetic and copies ran while one was open for 28% -> 30% of each run, Pallas kernels for 4% -> 11%
where the time goes in v2:
time: 635 us; the launch traced here: 629 us
  waiting for transfers between devices  157 us (25%)
  matrix products  110 us (17%)
  Pallas kernels  82.4 us (13%)
  starting transfers between devices  76.9 us (12%)
  blocking collectives  72.3 us (11%)
  local copies, waits for them, and re-layouts  64 us (10%)
  other arithmetic  49.5 us (8%)
  between operations  16.1 us (3%)
    dot_general x58, matrix products, dot(): lax.dot_general(a, b, (((ca,), (cb,)), ((), ())), preferred_element_type=...  110 us
    ppermute x11, waiting for transfers between devices, hop(): lax.ppermute(value, 'dp', [(i, i ^ (2 if i & 1 == stage - 1 else 4)) for...  78.7 us
    ppermute x19, waiting for transfers between devices, move(): return lax.ppermute(value, 'mp', pairs)  78.5 us
    ppermute x19, starting transfers between devices, move(): return lax.ppermute(value, 'mp', pairs)  60.1 us
    unnamed x225, local copies, waits for them, and re-layouts  39.4 us
    psum x1, blocking collectives, body(): vectors = lax.psum(vectors, ('dp', 'mp'))  39.4 us
    all_gather x1, blocking collectives, body(): lax.all_gather(jnp.concatenate([fc1_bias, qv_bias.reshape(-1)]), 'mp', ax...  32.9 us
    pallas_call x1, Pallas kernels, attend_back(): pl.pallas_call(functools.partial(attend_back_kernel, halo), grid=(pairs,)...  32.3 us
  transfers between devices with their start and end apart: 47, of which 16 were waited for; matrix products, arithmetic and copies ran while one was open for 30% of the time, Pallas kernels for 11%

profile of v2, /device:TPU:0, one launch (start us, length us, event | category | flops | bytes accessed | tf_op | source)
XLA Modules:
  0.0 628.8 jit_solution(14043842708111008815)
XLA Ops:
  10.4 4.6 shard_map.272
  16.0 5.1 collective-permute-start.4
  28.5 7.3 %shard_map.274 = (bf16[1024,1024]{1,0:T(8,128)(2,1)}, bf16[1024,1024]{1,0:T(8,128)(2,1)}) custom-call(s32[8]{0:T(128)} %get-tuple-element.131.at, bf16[1024,1024]{1,0:T(8,128)(2,1)} %fc1_ref.1, bf16[1024,1024]{1,0:T(8,128)(2,1)} %fc2_ref.1), custom_call_target="tpu_custom_call" | custom-call | tf_op jit(solution)/shard_map/pallas_call | solution.py:210
  38.9 4.6 collective-permute-done.3
  46.3 32.9 %all-gather.3 = f32[4,1,1536]{2,1,0:T(1,128)S(1)} all-gather(f32[1,1,1536]{2,1,0:T(1,128)S(1)} %reshape.757), channel_id=2, replica_groups=mesh['dp'=8,'mp'=4] {'mp'}, dimensions={0}, use_global_device_ids=true | all-gather | bytes 30720 | tf_op jit(solution)/shard_map/all_gather | solution.py:428
  91.1 12.8 %collective-permute-done.6.y_ref = bf16[2,3,4,64,512]{4,3,2,1,0:T(8,128)(2,1)} collective-permute-done((bf16[2,3,4,64,512]{4,3,2,1,0:T(8,128)(2,1)}, bf16[2,3,4,64,512]{4,3,2,1,0:T(8,128)(2,1)}, u32[]{:S(2)}, u32[]{:S(2)}) %collective-permute-start.6) | collective-permute-done | bytes 1572896 | tf_op jit(solution)/shard_map/ppermute | solution.py:294
  103.9 4.7 shard_map.273
  120.3 8.6 %collective-permute-done.1 = bf16[256,1024]{0,1:T(8,128)(2,1)S(1)} collective-permute-done((bf16[256,1024]{0,1:T(8,128)(2,1)S(1)}, bf16[256,1024]{0,1:T(8,128)(2,1)S(1)}, u32[]{:S(2)}, u32[]{:S(2)}) %collective-permute-start.1) | collective-permute-done | bytes 524320 | tf_op jit(solution)/shard_map/ppermute | solution.py:300
  133.6 12.7 %collective-permute-done.10 = bf16[512,1024]{1,0:T(8,128)(2,1)S(1)} collective-permute-done((bf16[512,1024]{1,0:T(8,128)(2,1)}, bf16[512,1024]{1,0:T(8,128)(2,1)S(1)}, u32[]{:S(2)}, u32[]{:S(2)}) %collective-permute-start.10) | collective-permute-done | bytes 1048608 | tf_op jit(solution)/shard_map/ppermute | solution.py:300
  166.3 26.1 %shard_map.275 = (bf16[512,1024]{1,0:T(8,128)(2,1)S(1)}, f32[8,2,512]{2,1,0:T(2,128)S(1)}) custom-call(f32[16]{0:T(128)S(1)} %multiply_exponential_fusion.slopes, s32[1,512]{1,0:T(1,128)S(1)} %pad_dynamic-slice_fusion.segq, s32[1280,1]{1,0:T(8,128)S(1)} %copy.151.segk, bf16[512,1024]{1,0:T(8,128)(2,1)S(1)} %add_convert_fusion.12.q_ref, ...), custom_call_target="tpu_custom_call" | custom-call | flops 8589934592 | bytes 7340032 | tf_op jit(solution)/shard_map/pallas_call | solution.py:114
  221.6 11.4 %collective-permute-done.13 = bf16[768,1024]{1,0:T(8,128)(2,1)S(1)} collective-permute-done((bf16[768,1024]{1,0:T(8,128)(2,1)S(1)}, bf16[768,1024]{1,0:T(8,128)(2,1)S(1)}, u32[]{:S(2)}, u32[]{:S(2)}) %collective-permute-start.13) | collective-permute-done | bytes 1572896 | tf_op jit(solution)/shard_map/ppermute | solution.py:294
  233.0 16.8 %collective-permute-done.12 = bf16[768,1024]{1,0:T(8,128)(2,1)S(1)} collective-permute-done((bf16[768,1024]{1,0:T(8,128)(2,1)S(1)}, bf16[768,1024]{1,0:T(8,128)(2,1)S(1)}, u32[]{:S(2)}, u32[]{:S(2)}) %collective-permute-start.12) | collective-permute-done | bytes 1572896 | tf_op jit(solution)/shard_map/ppermute | solution.py:294
  284.3 13.7 %collective-permute-done.22 = bf16[1024,1024]{1,0:T(8,128)(2,1)S(1)} collective-permute-done((bf16[1024,1024]{1,0:T(8,128)(2,1)S(1)}, bf16[1024,1024]{1,0:T(8,128)(2,1)S(1)}, u32[]{:S(2)}, u32[]{:S(2)}) %collective-permute-start.22) | collective-permute-done | bytes 2097184 | tf_op jit(solution)/shard_map/ppermute | solution.py:294
  301.0 32.3 %shard_map.276 = (bf16[512,1024]{1,0:T(8,128)(2,1)S(1)}, bf16[1280,1024]{1,0:T(8,128)(2,1)}, bf16[1280,1024]{1,0:T(8,128)(2,1)}) custom-call(f32[16]{0:T(128)S(1)} %multiply_exponential_fusion.slopes, s32[1,512]{1,0:T(1,128)S(1)} %pad_dynamic-slice_fusion.segq, s32[1280,1]{1,0:T(8,128)S(1)} %copy.151.segk, bf16[512,1024]{1,0:T(8,128)(2,1)S(1)} %add_convert_fusion.12.q_ref, ...), custom_call_target="tpu_custom_call" | custom-call | flops 21474836480 | bytes 13631488 | tf_op jit(solution)/shard_map/pallas_call | solution.py:146
  349.8 7.4 %shard_map.277 = (bf16[2,4,256,512]{3,2,1,0:T(8,128)(2,1)}, bf16[2,4,256,512]{3,2,1,0:T(8,128)(2,1)}) custom-call(s32[4]{0:T(128)} %broadcast_select_fusion.5.at, bf16[1024,512]{1,0:T(8,128)(2,1)} %convolution_convert_fusion.11.refs_0_, bf16[1024,512]{1,0:T(8,128)(2,1)} %convolution_convert_fusion.10.refs_1_, ...), custom_call_target="tpu_custom_call" | custom-call | tf_op jit(solution)/shard_map/pallas_call | solution.py:272
  363.4 4.7 fusion.142
  368.1 15.6 %collective-permute-done.32 = bf16[2,4,256,512]{3,2,1,0:T(8,128)(2,1)} collective-permute-done((bf16[2,4,256,512]{3,2,1,0:T(8,128)(2,1)}, bf16[2,4,256,512]{3,2,1,0:T(8,128)(2,1)}, u32[]{:S(2)}, u32[]{:S(2)}) %collective-permute-start.32) | collective-permute-done | bytes 2097184 | tf_op jit(solution)/shard_map/ppermute | solution.py:294
  391.7 8.4 %collective-permute-done.33 = bf16[4,256,512]{2,1,0:T(8,128)(2,1)S(1)} collective-permute-done((bf16[4,256,512]{2,1,0:T(8,128)(2,1)S(1)}, bf16[4,256,512]{2,1,0:T(8,128)(2,1)S(1)}, u32[]{:S(2)}, u32[]{:S(2)}) %collective-permute-start.33) | collective-permute-done | bytes 1048608 | tf_op jit(solution)/shard_map/ppermute | solution.py:294
  402.9 8.9 %collective-permute-start.35 = (bf16[4,64,512]{2,1,0:T(8,128)(2,1)S(1)}, bf16[4,64,512]{2,1,0:T(8,128)(2,1)S(1)}, u32[]{:S(2)}, u32[]{:S(2)}) collective-permute-start(bf16[4,64,512]{2,1,0:T(8,128)(2,1)S(1)} %get-tuple-element.163), channel_id=1, source_target_pairs={{0,2},{1,3},{2,0},{3,1},{4,6},{5,7},{6,4},{7,5},{8,10},{9,11},{10,... | collective-permute-start | bytes 786440 | tf_op jit(solution)/shard_map/ppermute | solution.py:300
  418.4 8.9 %collective-permute-done.35 = bf16[4,64,512]{2,1,0:T(8,128)(2,1)S(1)} collective-permute-done((bf16[4,64,512]{2,1,0:T(8,128)(2,1)S(1)}, bf16[4,64,512]{2,1,0:T(8,128)(2,1)S(1)}, u32[]{:S(2)}, u32[]{:S(2)}) %collective-permute-start.35) | collective-permute-done | bytes 262176 | tf_op jit(solution)/shard_map/ppermute | solution.py:300
  428.3 4.4 fusion.124
  433.0 8.0 %collective-permute-start.42 = (bf16[256,1024]{1,0:T(8,128)(2,1)S(1)}, bf16[256,1024]{1,0:T(8,128)(2,1)S(1)}, u32[]{:S(2)}, u32[]{:S(2)}) collective-permute-start(bf16[256,1024]{1,0:T(8,128)(2,1)S(1)} %add_convert_fusion.18), channel_id=1, source_target_pairs={{0,1},{3,2},{4,5},{7,6},{8,9},{11,10},{12,13},{15,14},{16,17},{19,... | collective-permute-start | bytes 1572872 | tf_op jit(solution)/shard_map/ppermute | solution.py:300
  446.2 7.1 %collective-permute-done.42 = bf16[256,1024]{1,0:T(8,128)(2,1)S(1)} collective-permute-done((bf16[256,1024]{1,0:T(8,128)(2,1)S(1)}, bf16[256,1024]{1,0:T(8,128)(2,1)S(1)}, u32[]{:S(2)}, u32[]{:S(2)}) %collective-permute-start.42) | collective-permute-done | bytes 524320 | tf_op jit(solution)/shard_map/ppermute | solution.py:300
  456.7 6.8 %collective-permute-done.39 = bf16[256,1024]{1,0:T(8,128)(2,1)S(1)} collective-permute-done((bf16[256,1024]{1,0:T(8,128)(2,1)S(1)}, bf16[256,1024]{1,0:T(8,128)(2,1)S(1)}, u32[]{:S(2)}, u32[]{:S(2)}) %collective-permute-start.39) | collective-permute-done | bytes 524320 | tf_op jit(solution)/shard_map/ppermute | solution.py:300
  465.3 4.8 collective-permute-start.44
  471.2 11.2 %collective-permute-start.41 = (bf16[128,1024]{1,0:T(8,128)(2,1)S(1)}, bf16[128,1024]{1,0:T(8,128)(2,1)S(1)}, u32[]{:S(2)}, u32[]{:S(2)}) collective-permute-start(bf16[128,1024]{1,0:T(8,128)(2,1)S(1)} %add_convert_fusion.30), channel_id=1, source_target_pairs={{0,1},{1,0},{2,3},{3,2},{4,5},{5,4},{6,7},{7,6},{8,9},{9,8},{10,11... | collective-permute-start | bytes 786440 | tf_op jit(solution)/shard_map/ppermute | solution.py:300
  508.4 8.5 %collective-permute-done.26 = bf16[256,1024]{0,1:T(8,128)(2,1)S(1)} collective-permute-done((bf16[256,1024]{0,1:T(8,128)(2,1)S(1)}, bf16[256,1024]{0,1:T(8,128)(2,1)S(1)}, u32[]{:S(2)}, u32[]{:S(2)}) %collective-permute-start.26) | collective-permute-done | bytes 524320 | tf_op jit(solution)/shard_map/ppermute | solution.py:300
  526.9 15.4 %collective-permute-done.27 = bf16[512,1024]{0,1:T(8,128)(2,1)S(1)} collective-permute-done((bf16[512,1024]{0,1:T(8,128)(2,1)}, bf16[512,1024]{0,1:T(8,128)(2,1)S(1)}, u32[]{:S(2)}, u32[]{:S(2)}) %collective-permute-start.27) | collective-permute-done | bytes 1048608 | tf_op jit(solution)/shard_map/ppermute | solution.py:300
  550.4 39.4 %psum.7 = f32[4,3072]{1,0:T(4,128)S(1)} all-reduce(f32[4,3072]{1,0:T(4,128)S(1)} %pad_maximum_fusion.14), channel_id=1, replica_groups=mesh['dp'=8,'mp'=4] {'dp','mp'}, use_global_device_ids=true, to_apply=%region_21.22 | all-reduce | flops 12288 | bytes 98304 | tf_op jit(solution)/shard_map/psum | solution.py:626
  594.9 4.5 copy.188
  599.4 7.0 %reshape.760 = f32[1024,3,256]{2,0,1:T(8,128)} reshape(f32[2,512,3,4,64]{4,3,1,0,2:T(4,128)} %copy.188) | data formatting | bytes 6291456
  613.8 5.3 copy.189
  (484 shorter events, 242.5 us)
Async XLA Ops:
  7.2 584.8 %all-gather.7.cloned.1.call-start = ((), (), s32[]{:S(2)}) async-start(), calls=%async_computation | async-start | bytes 2359296 | tf_op jit(solution)/shard_map/all_gather | solution.py:311
  16.0 22.9 %collective-permute-start.4 = (bf16[4,64,512]{2,1,0:T(8,128)(2,1)S(1)}, bf16[4,64,512]{2,1,0:T(8,128)(2,1)S(1)}, u32[]{:S(2)}, u32[]{:S(2)}) collective-permute-start(bf16[4,64,512]{2,1,0:T(8,128)(2,1)S(1)} %slice_bitcast_fusion.23), channel_id=1, source_target_pairs={{0,3},{1,0},{2,1},{3,2},{4,7},{5,4},{6,5},{7,6},{8,11},{9,8},{10,9... | collective-permute-start | bytes 786440 | tf_op jit(solution)/shard_map/ppermute | solution.py:300
  21.1 22.4 %collective-permute-start.3 = (bf16[4,64,512]{2,1,0:T(8,128)(2,1)S(1)}, bf16[4,64,512]{2,1,0:T(8,128)(2,1)S(1)}, u32[]{:S(2)}, u32[]{:S(2)}) collective-permute-start(bf16[4,64,512]{2,1,0:T(8,128)(2,1)S(1)} %slice_bitcast_fusion.23), channel_id=1, source_target_pairs={{0,2},{1,3},{2,0},{3,1},{4,6},{5,7},{6,4},{7,5},{8,10},{9,11},{10,... | collective-permute-start | bytes 786440 | tf_op jit(solution)/shard_map/ppermute | solution.py:300
  21.1 22.4 %collective-permute-start.2 = (bf16[4,64,512]{2,1,0:T(8,128)(2,1)S(1)}, bf16[4,64,512]{2,1,0:T(8,128)(2,1)S(1)}, u32[]{:S(2)}, u32[]{:S(2)}) collective-permute-start(bf16[4,64,512]{2,1,0:T(8,128)(2,1)S(1)} %slice_bitcast_fusion.23), channel_id=1, source_target_pairs={{0,1},{1,2},{2,3},{3,0},{4,5},{5,6},{6,7},{7,4},{8,9},{9,10},{10,1... | collective-permute-start | bytes 786440 | tf_op jit(solution)/shard_map/ppermute | solution.py:300
  23.4 89.4 %collective-permute-start = (bf16[512,1024]{0,1:T(8,128)(2,1)}, bf16[512,1024]{0,1:T(8,128)(2,1)S(1)}, u32[]{:S(2)}, u32[]{:S(2)}) collective-permute-start(bf16[512,1024]{0,1:T(8,128)(2,1)} %copy.148), channel_id=1, source_target_pairs={{0,1},{1,2},{2,3},{4,5},{5,6},{6,7},{8,9},{9,10},{10,11},{12,13},{... | collective-permute-start | bytes 3145736 | tf_op jit(solution)/shard_map/ppermute | solution.py:300
  38.7 47.8 %collective-permute-start.8 = (bf16[256,1024]{1,0:T(8,128)(2,1)}, bf16[256,1024]{1,0:T(8,128)(2,1)}, u32[]{:S(2)}, u32[]{:S(2)}) collective-permute-start(bf16[256,1024]{1,0:T(8,128)(2,1)} %pad_maximum_fusion.12), channel_id=1, source_target_pairs={{0,1},{1,0},{2,3},{3,2},{4,5},{5,4},{6,7},{7,6},{8,9},{9,8},{10,11... | collective-permute-start | bytes 1572872 | tf_op jit(solution)/shard_map/ppermute | solution.py:300
  44.8 35.7 %collective-permute-start.5 = (bf16[3,4,64,512]{3,2,1,0:T(8,128)(2,1)}, bf16[3,4,64,512]{3,2,1,0:T(8,128)(2,1)}, u32[]{:S(2)}, u32[]{:S(2)}) collective-permute-start(bf16[3,4,64,512]{3,2,1,0:T(8,128)(2,1)} %get-tuple-element.167.x0_ref), channel_id=1, source_target_pairs={{0,8},{4,20},{8,0},{12,28},{16,24},{20,4},{24,16},{28,12},{1,9},{5... | collective-permute-start | bytes 2359304 | tf_op jit(solution)/shard_map/ppermute | solution.py:294
  83.1 20.7 %collective-permute-start.6 = (bf16[2,3,4,64,512]{4,3,2,1,0:T(8,128)(2,1)}, bf16[2,3,4,64,512]{4,3,2,1,0:T(8,128)(2,1)}, u32[]{:S(2)}, u32[]{:S(2)}) collective-permute-start(bf16[2,3,4,64,512]{4,3,2,1,0:T(8,128)(2,1)} %pad_maximum_fusion.4), channel_id=1, source_target_pairs={{0,16},{4,12},{8,24},{12,4},{16,0},{20,28},{24,8},{28,20},{1,17},{... | collective-permute-start | bytes 4718600 | tf_op jit(solution)/shard_map/ppermute | solution.py:294
  88.6 30.3 %collective-permute-start.9 = (bf16[512,1024]{1,0:T(8,128)(2,1)}, bf16[512,1024]{1,0:T(8,128)(2,1)}, u32[]{:S(2)}, u32[]{:S(2)}) collective-permute-start(bf16[512,1024]{1,0:T(8,128)(2,1)} %pad_maximum_fusion.7), channel_id=1, source_target_pairs={{1,2},{2,1},{5,6},{6,5},{9,10},{10,9},{13,14},{14,13},{17,18},{18,... | collective-permute-start | bytes 3145736 | tf_op jit(solution)/shard_map/ppermute | solution.py:300
  108.6 42.8 %collective-permute-start.7 = (bf16[4,1024,512]{2,1,0:T(8,128)(2,1)}, bf16[4,1024,512]{2,1,0:T(8,128)(2,1)}, u32[]{:S(2)}, u32[]{:S(2)}) collective-permute-start(bf16[4,1024,512]{2,1,0:T(8,128)(2,1)} %bitcast.237), channel_id=1, source_target_pairs={{0,4},{4,0},{8,12},{12,8},{16,20},{20,16},{24,28},{28,24},{1,5},{5... | collective-permute-start | bytes 12582920 | tf_op jit(solution)/shard_map/ppermute | solution.py:289
  112.9 16.0 %collective-permute-start.1 = (bf16[256,1024]{0,1:T(8,128)(2,1)S(1)}, bf16[256,1024]{0,1:T(8,128)(2,1)S(1)}, u32[]{:S(2)}, u32[]{:S(2)}) collective-permute-start(bf16[256,1024]{0,1:T(8,128)(2,1)S(1)} %slice.489), channel_id=1, source_target_pairs={{0,1},{1,2},{2,3},{4,5},{5,6},{6,7},{8,9},{9,10},{10,11},{12,13},{... | collective-permute-start | bytes 1572872 | tf_op jit(solution)/shard_map/ppermute | solution.py:300
  118.8 27.5 %collective-permute-start.10 = (bf16[512,1024]{1,0:T(8,128)(2,1)}, bf16[512,1024]{1,0:T(8,128)(2,1)S(1)}, u32[]{:S(2)}, u32[]{:S(2)}) collective-permute-start(bf16[512,1024]{1,0:T(8,128)(2,1)} %collective-permute-done.9), channel_id=1, source_target_pairs={{1,0},{2,3},{5,4},{6,7},{9,8},{10,11},{13,12},{14,15},{17,16},{18,... | collective-permute-start | bytes 3145736 | tf_op jit(solution)/shard_map/ppermute | solution.py:300
  155.0 53.8 %collective-permute-start.11 = (bf16[768,1024]{1,0:T(8,128)(2,1)}, bf16[768,1024]{1,0:T(8,128)(2,1)}, u32[]{:S(2)}, u32[]{:S(2)}) collective-permute-start(bf16[768,1024]{1,0:T(8,128)(2,1)} %slice_dynamic-update-slice_fusion), channel_id=1, source_target_pairs={{0,8},{4,20},{8,0},{12,28},{16,24},{20,4},{24,16},{28,12},{1,9},{5... | collective-permute-start | bytes 4718600 | tf_op jit(solution)/shard_map/ppermute | solution.py:294
  212.6 37.3 %collective-permute-start.15 = (bf16[768,1024]{1,0:T(8,128)(2,1)S(1)}, bf16[768,1024]{1,0:T(8,128)(2,1)S(1)}, u32[]{:S(2)}, u32[]{:S(2)}) collective-permute-start(bf16[768,1024]{1,0:T(8,128)(2,1)S(1)} %pad_maximum_fusion.6), channel_id=1, source_target_pairs={{0,4},{4,0},{8,12},{12,8},{16,20},{20,16},{24,28},{28,24},{1,5},{5... | collective-permute-start | bytes 4718600 | tf_op jit(solution)/shard_map/ppermute | solution.py:289
  212.6 20.4 %collective-permute-start.13 = (bf16[768,1024]{1,0:T(8,128)(2,1)S(1)}, bf16[768,1024]{1,0:T(8,128)(2,1)S(1)}, u32[]{:S(2)}, u32[]{:S(2)}) collective-permute-start(bf16[768,1024]{1,0:T(8,128)(2,1)S(1)} %pad_maximum_fusion.6), channel_id=1, source_target_pairs={{0,16},{4,12},{8,24},{12,4},{16,0},{20,28},{24,8},{28,20},{1,17},{... | collective-permute-start | bytes 4718600 | tf_op jit(solution)/shard_map/ppermute | solution.py:294
  214.1 35.7 %collective-permute-start.12 = (bf16[768,1024]{1,0:T(8,128)(2,1)S(1)}, bf16[768,1024]{1,0:T(8,128)(2,1)S(1)}, u32[]{:S(2)}, u32[]{:S(2)}) collective-permute-start(bf16[768,1024]{1,0:T(8,128)(2,1)S(1)} %pad_maximum_fusion.5), channel_id=1, source_target_pairs={{0,16},{4,12},{8,24},{12,4},{16,0},{20,28},{24,8},{28,20},{1,17},{... | collective-permute-start | bytes 4718600 | tf_op jit(solution)/shard_map/ppermute | solution.py:294
  221.6 58.2 %collective-permute-start.24 = (bf16[768,1024]{1,0:T(8,128)(2,1)S(1)}, bf16[768,1024]{1,0:T(8,128)(2,1)S(1)}, u32[]{:S(2)}, u32[]{:S(2)}) collective-permute-start(bf16[768,1024]{1,0:T(8,128)(2,1)S(1)} %convolution_convert_fusion.1), channel_id=1, source_target_pairs={{0,4},{4,0},{8,12},{12,8},{16,20},{20,16},{24,28},{28,24},{1,5},{5... | collective-permute-start | bytes 4718600 | tf_op jit(solution)/shard_map/ppermute | solution.py:289
  233.0 29.0 %collective-permute-start.17 = (bf16[768,1024]{1,0:T(8,128)(2,1)S(1)}, bf16[768,1024]{1,0:T(8,128)(2,1)S(1)}, u32[]{:S(2)}, u32[]{:S(2)}) collective-permute-start(bf16[768,1024]{1,0:T(8,128)(2,1)S(1)} %collective-permute-done.13), channel_id=1, source_target_pairs={{0,4},{4,0},{8,12},{12,8},{16,20},{20,16},{24,28},{28,24},{1,5},{5... | collective-permute-start | bytes 4718600 | tf_op jit(solution)/shard_map/ppermute | solution.py:289
  271.9 26.1 %collective-permute-start.22 = (bf16[1024,1024]{1,0:T(8,128)(2,1)S(1)}, bf16[1024,1024]{1,0:T(8,128)(2,1)S(1)}, u32[]{:S(2)}, u32[]{:S(2)}) collective-permute-start(bf16[1024,1024]{1,0:T(8,128)(2,1)S(1)} %pad_maximum_fusion.3), channel_id=1, source_target_pairs={{0,16},{4,12},{8,24},{12,4},{16,0},{20,28},{24,8},{28,20},{1,17},{... | collective-permute-start | bytes 6291464 | tf_op jit(solution)/shard_map/ppermute | solution.py:294
  275.2 73.6 %collective-permute-start.29 = (bf16[1024,512]{1,0:T(8,128)(2,1)}, bf16[1024,512]{1,0:T(8,128)(2,1)S(1)}, u32[]{:S(2)}, u32[]{:S(2)}) collective-permute-start(bf16[1024,512]{1,0:T(8,128)(2,1)} %convolution_convert_fusion.8), channel_id=1, source_target_pairs={{0,4},{4,0},{8,12},{12,8},{16,20},{20,16},{24,28},{28,24},{1,5},{5... | collective-permute-start | bytes 3145736 | tf_op jit(solution)/shard_map/ppermute | solution.py:289
  298.0 41.1 %collective-permute-start.23 = (bf16[1024,1024]{1,0:T(8,128)(2,1)}, bf16[1024,1024]{1,0:T(8,128)(2,1)S(1)}, u32[]{:S(2)}, u32[]{:S(2)}) collective-permute-start(bf16[1024,1024]{1,0:T(8,128)(2,1)} %pad_maximum_fusion.2), channel_id=1, source_target_pairs={{0,16},{4,12},{8,24},{12,4},{16,0},{20,28},{24,8},{28,20},{1,17},{... | collective-permute-start | bytes 6291464 | tf_op jit(solution)/shard_map/ppermute | solution.py:294
  300.4 38.6 %collective-permute-start.25 = (bf16[512,1024]{1,0:T(8,128)(2,1)S(1)}, bf16[512,1024]{1,0:T(8,128)(2,1)S(1)}, u32[]{:S(2)}, u32[]{:S(2)}) collective-permute-start(bf16[512,1024]{1,0:T(8,128)(2,1)S(1)} %pad_maximum_fusion.8), channel_id=1, source_target_pairs={{0,8},{4,20},{8,0},{12,28},{16,24},{20,4},{24,16},{28,12},{1,9},{5... | collective-permute-start | bytes 3145736 | tf_op jit(solution)/shard_map/ppermute | solution.py:294
  357.2 26.4 %collective-permute-start.32 = (bf16[2,4,256,512]{3,2,1,0:T(8,128)(2,1)}, bf16[2,4,256,512]{3,2,1,0:T(8,128)(2,1)}, u32[]{:S(2)}, u32[]{:S(2)}) collective-permute-start(bf16[2,4,256,512]{3,2,1,0:T(8,128)(2,1)} %get-tuple-element.47), channel_id=1, source_target_pairs={{0,16},{4,12},{8,24},{12,4},{16,0},{20,28},{24,8},{28,20},{1,17},{... | collective-permute-start | bytes 6291464 | tf_op jit(solution)/shard_map/ppermute | solution.py:294
  361.5 26.7 %collective-permute-start.37 = (bf16[768,1024]{1,0:T(8,128)(2,1)}, bf16[768,1024]{1,0:T(8,128)(2,1)}, u32[]{:S(2)}, u32[]{:S(2)}) collective-permute-start(bf16[768,1024]{1,0:T(8,128)(2,1)} %convolution_convert_fusion), channel_id=1, source_target_pairs={{0,4},{4,0},{8,12},{12,8},{16,20},{20,16},{24,28},{28,24},{1,5},{5... | collective-permute-start | bytes 4718600 | tf_op jit(solution)/shard_map/ppermute | solution.py:289
  401.8 16.6 %collective-permute-start.36 = (bf16[4,64,512]{2,1,0:T(8,128)(2,1)S(1)}, bf16[4,64,512]{2,1,0:T(8,128)(2,1)S(1)}, u32[]{:S(2)}, u32[]{:S(2)}) collective-permute-start(bf16[4,64,512]{2,1,0:T(8,128)(2,1)S(1)} %get-tuple-element.164), channel_id=1, source_target_pairs={{0,1},{1,2},{2,3},{3,0},{4,5},{5,6},{6,7},{7,4},{8,9},{9,10},{10,1... | collective-permute-start | bytes 786440 | tf_op jit(solution)/shard_map/ppermute | solution.py:300
  402.9 24.5 %collective-permute-start.35 = (bf16[4,64,512]{2,1,0:T(8,128)(2,1)S(1)}, bf16[4,64,512]{2,1,0:T(8,128)(2,1)S(1)}, u32[]{:S(2)}, u32[]{:S(2)}) collective-permute-start(bf16[4,64,512]{2,1,0:T(8,128)(2,1)S(1)} %get-tuple-element.163), channel_id=1, source_target_pairs={{0,2},{1,3},{2,0},{3,1},{4,6},{5,7},{6,4},{7,5},{8,10},{9,11},{10,... | collective-permute-start | bytes 786440 | tf_op jit(solution)/shard_map/ppermute | solution.py:300
  414.8 28.7 %collective-permute-start.38 = (bf16[512,1024]{1,0:T(8,128)(2,1)}, bf16[512,1024]{1,0:T(8,128)(2,1)}, u32[]{:S(2)}, u32[]{:S(2)}) collective-permute-start(bf16[512,1024]{1,0:T(8,128)(2,1)} %pad_maximum_fusion.10), channel_id=1, source_target_pairs={{0,8},{4,20},{8,0},{12,28},{16,24},{20,4},{24,16},{28,12},{1,9},{5... | collective-permute-start | bytes 3145736 | tf_op jit(solution)/shard_map/ppermute | solution.py:294
  428.2 180.1 %all-gather.9.cloned.1.call-start = ((), (), s32[]{:S(2)}) async-start(), calls=%async_computation.1 | async-start | bytes 4718592 | tf_op jit(solution)/shard_map/all_gather | solution.py:311
  433.0 20.3 %collective-permute-start.42 = (bf16[256,1024]{1,0:T(8,128)(2,1)S(1)}, bf16[256,1024]{1,0:T(8,128)(2,1)S(1)}, u32[]{:S(2)}, u32[]{:S(2)}) collective-permute-start(bf16[256,1024]{1,0:T(8,128)(2,1)S(1)} %add_convert_fusion.18), channel_id=1, source_target_pairs={{0,1},{3,2},{4,5},{7,6},{8,9},{11,10},{12,13},{15,14},{16,17},{19,... | collective-permute-start | bytes 1572872 | tf_op jit(solution)/shard_map/ppermute | solution.py:300
  444.9 18.7 %collective-permute-start.39 = (bf16[256,1024]{1,0:T(8,128)(2,1)S(1)}, bf16[256,1024]{1,0:T(8,128)(2,1)S(1)}, u32[]{:S(2)}, u32[]{:S(2)}) collective-permute-start(bf16[256,1024]{1,0:T(8,128)(2,1)S(1)} %add_convert_fusion.20), channel_id=1, source_target_pairs={{0,1},{3,2},{4,5},{7,6},{8,9},{11,10},{12,13},{15,14},{16,17},{19,... | collective-permute-start | bytes 1572872 | tf_op jit(solution)/shard_map/ppermute | solution.py:300
  465.3 17.2 %collective-permute-start.44 = (bf16[128,1024]{1,0:T(8,128)(2,1)S(1)}, bf16[128,1024]{1,0:T(8,128)(2,1)S(1)}, u32[]{:S(2)}, u32[]{:S(2)}) collective-permute-start(bf16[128,1024]{1,0:T(8,128)(2,1)S(1)} %add_convert_fusion.26), channel_id=1, source_target_pairs={{0,1},{1,0},{2,3},{3,2},{4,5},{5,4},{6,7},{7,6},{8,9},{9,8},{10,11... | collective-permute-start | bytes 786440 | tf_op jit(solution)/shard_map/ppermute | solution.py:300
  518.1 24.2 %collective-permute-start.27 = (bf16[512,1024]{0,1:T(8,128)(2,1)}, bf16[512,1024]{0,1:T(8,128)(2,1)S(1)}, u32[]{:S(2)}, u32[]{:S(2)}) collective-permute-start(bf16[512,1024]{0,1:T(8,128)(2,1)} %pad_maximum_fusion.9), channel_id=1, source_target_pairs={{1,0},{2,1},{3,2},{5,4},{6,5},{7,6},{9,8},{10,9},{11,10},{13,12},{... | collective-permute-start | bytes 3145736 | tf_op jit(solution)/shard_map/ppermute | solution.py:300
  (117 other events, 1265.1 us)
Sparse Core Ops, SparseCore 0:
  428.4 32.1 all-gather.6
  489.5 35.0 all-gather.8

commit v3 on v2

v3 whole, which is shorter than its diff:
```python
import functools

import jax
import jax.numpy as jnp
from jax import lax
from jax.experimental import pallas as pl
from jax.experimental.pallas import tpu as pltpu
from jax.sharding import PartitionSpec as P

HEADS = 16
HD = 64
DOC_MOST = 768
QB = 256
MASKED = -1e12
SMALL = pl.CostEstimate(flops=1, bytes_accessed=1, transcendentals=1)
eps = 1e-05
f32 = jnp.float32
bf16 = jnp.bfloat16


def dot(a, b, ca, cb):
    return lax.dot_general(a, b, (((ca,), (cb,)), ((), ())), preferred_element_type=f32)


def fill_mask(segq_ref, segk_ref, mask_ref, window, halo):
    for i in range(mask_ref.shape[0]):
        key_at = lax.broadcasted_iota(jnp.int32, (window, QB), 0) + i * QB
        query_at = lax.broadcasted_iota(jnp.int32, (window, QB), 1) + (i * QB + halo)
        same = segk_ref[i * QB : i * QB + window, :] == segq_ref[:, i * QB : (i + 1) * QB]
        allowed = same & (key_at <= query_at)
        mask_ref[i] = jnp.where(allowed, (key_at - query_at).astype(f32), MASKED)


def halves(rows):
    lane = lax.broadcasted_iota(jnp.int32, (rows, 2 * HD), 1)
    return [lane < HD, lane >= HD]


def attend_kernel(halo, start, slopes, segq, segk, q_ref, k_ref, v_ref, *refs):
    o_ref, lse_ref, mask_ref = refs[-3:]
    window = halo + QB
    pair = start + pl.program_id(0)

    @pl.when(pair == start)
    def _():
        fill_mask(segq, segk, mask_ref, window, halo)

    v_t = v_ref[...].T
    pick = halves(QB)
    for i in range(mask_ref.shape[0]):
        rows = slice(i * QB, (i + 1) * QB)
        keys = slice(i * QB, i * QB + window)
        query = q_ref[rows, :] * jnp.asarray(HD**-0.5, bf16)
        key_rows = k_ref[keys, :]
        out = []
        for h in range(2):
            q_h = jnp.where(pick[h], query, jnp.zeros_like(query))
            scores = dot(key_rows, q_h, 1, 1) + slopes[2 * pair + h] * mask_ref[i]
            top = jnp.max(scores, axis=0, keepdims=True)
            expo = jnp.exp(scores - top)
            total = jnp.sum(expo, axis=0, keepdims=True)
            o_t = dot(v_t[:, keys], expo.astype(bf16), 1, 0)
            out.append(o_t[h * HD : (h + 1) * HD, :] * (1.0 / total))
            lse_ref[0, h : h + 1, rows] = top + jnp.log(total)
        o_ref[rows, :] = jnp.concatenate(out, axis=0).T.astype(bf16)


def attend_back_kernel(halo, start, slopes, segq, segk, q_ref, k_ref, v_ref, g_ref, lse_ref, *refs):
    dq_ref, dk_ref, dv_ref, mask_ref, dk_acc, dv_acc = refs[-6:]
    window = halo + QB
    pair = start + pl.program_id(0)

    @pl.when(pair == start)
    def _():
        fill_mask(segq, segk, mask_ref, window, halo)

    k_t = k_ref[...].T
    pick = halves(QB)
    dk_acc[...] = jnp.zeros_like(dk_acc)
    dv_acc[...] = jnp.zeros_like(dv_acc)
    for i in range(mask_ref.shape[0]):
        rows = slice(i * QB, (i + 1) * QB)
        keys = slice(i * QB, i * QB + window)
        query = q_ref[rows, :] * jnp.asarray(HD**-0.5, bf16)
        grad = g_ref[rows, :]
        key_rows = k_ref[keys, :]
        value_rows = v_ref[keys, :]
        out = []
        for h in range(2):
            q_h = jnp.where(pick[h], query, jnp.zeros_like(query))
            g_h = jnp.where(pick[h], grad, jnp.zeros_like(grad))
            scores = dot(key_rows, q_h, 1, 1) + slopes[2 * pair + h] * mask_ref[i]
            probs = jnp.exp(scores - lse_ref[0, h : h + 1, rows])
            grad_probs = dot(value_rows, g_h, 1, 1)
            delta = jnp.sum(probs * grad_probs, axis=0, keepdims=True)
            grad_scores = (probs * (grad_probs - delta)).astype(bf16)
            dv_acc[keys, :] += dot(probs.astype(bf16), g_h, 1, 0)
            dk_acc[keys, :] += dot(grad_scores, q_h, 1, 0)
            dq_t = dot(k_t[:, keys], grad_scores, 1, 0)
            out.append(dq_t[h * HD : (h + 1) * HD, :])
        dq_ref[rows, :] = (jnp.concatenate(out, axis=0).T * HD**-0.5).astype(bf16)
    dk_ref[...] = dk_acc[...].astype(bf16)
    dv_ref[...] = dv_acc[...].astype(bf16)


def attend(part, slopes, segq, segk, q, k, v, before=()):
    rows, wide = q.shape
    ext = k.shape[0]
    halo = ext - rows
    pairs = wide // (2 * HD)
    blocks = rows // QB
    start = part * (pairs // 2)
    col = lambda n: pl.BlockSpec((n, 2 * HD), lambda p: (0, p + start))
    return pl.pallas_call(
        functools.partial(attend_kernel, halo, start),
        grid=(pairs // 2,),
        in_specs=[
            pl.BlockSpec(memory_space=pltpu.SMEM),
            pl.BlockSpec((1, rows), lambda p: (0, 0)),
            pl.BlockSpec((ext, 1), lambda p: (0, 0)),
            col(rows),
            col(ext),
            col(ext),
        ]
        + [pl.BlockSpec(memory_space=pl.ANY)] * len(before),
        out_specs=[col(rows), pl.BlockSpec((1, 2, rows), lambda p: (p + start, 0, 0))],
        out_shape=[
            jax.ShapeDtypeStruct((rows, wide), bf16),
            jax.ShapeDtypeStruct((pairs, 2, rows), f32),
        ],
        input_output_aliases={6 + i: i for i in range(len(before))},
        scratch_shapes=[pltpu.VMEM((blocks, halo + QB, QB), f32)],
        compiler_params=pltpu.CompilerParams(vmem_limit_bytes=40 << 20),
        cost_estimate=SMALL,
    )(slopes, segq, segk, q, k, v, *before)


def attend_back(part, slopes, segq, segk, q, k, v, grad, lse, before=()):
    rows, wide = q.shape
    ext = k.shape[0]
    halo = ext - rows
    pairs = wide // (2 * HD)
    blocks = rows // QB
    start, stop = [pairs * i // 8 for i in (0, 3, 6, 8)][part : part + 2]
    col = lambda n: pl.BlockSpec((n, 2 * HD), lambda p: (0, p + start))
    return pl.pallas_call(
        functools.partial(attend_back_kernel, halo, start),
        grid=(stop - start,),
        in_specs=[
            pl.BlockSpec(memory_space=pltpu.SMEM),
            pl.BlockSpec((1, rows), lambda p: (0, 0)),
            pl.BlockSpec((ext, 1), lambda p: (0, 0)),
            col(rows),
            col(ext),
            col(ext),
            col(rows),
            pl.BlockSpec((1, 2, rows), lambda p: (p + start, 0, 0)),
        ]
        + [pl.BlockSpec(memory_space=pl.ANY)] * len(before),
        out_specs=[col(rows), col(ext), col(ext)],
        out_shape=[
            jax.ShapeDtypeStruct((rows, wide), bf16),
            jax.ShapeDtypeStruct((ext, wide), bf16),
            jax.ShapeDtypeStruct((ext, wide), bf16),
        ],
        input_output_aliases={8 + i: i for i in range(len(before))},
        scratch_shapes=[
            pltpu.VMEM((blocks, halo + QB, QB), f32),
            pltpu.VMEM((ext, 2 * HD), f32),
            pltpu.VMEM((ext, 2 * HD), f32),
        ],
        compiler_params=pltpu.CompilerParams(vmem_limit_bytes=48 << 20),
        cost_estimate=SMALL,
    )(slopes, segq, segk, q, k, v, grad, lse, *before)


def own_att_kernel(at, qkv_ref, out_ref, *own_refs):
    for t, rows in enumerate((qkv_ref[0], out_ref[...], qkv_ref[1], qkv_ref[2])):
        half = rows.shape[1] // 2
        left, right = rows[:, :half], rows[:, half:]
        own_refs[0][t, 0] = jnp.where(at[0] == 0, left, right)
        if len(own_refs) == 2:
            own_refs[1][t, 0] = jnp.where(at[0] == 0, right, left)


def own_att(halves, at, qkv_t, out_weight):
    wide = out_weight.shape[1]
    places = 4 if halves == 2 else 1
    return pl.pallas_call(
        own_att_kernel,
        grid_spec=pltpu.PrefetchScalarGridSpec(
            num_scalar_prefetch=1,
            grid=(places,),
            in_specs=[
                pl.BlockSpec((3, HD, wide), lambda p, at: (0, at[1 + p], 0)),
                pl.BlockSpec((HD, wide), lambda p, at: (at[1 + p], 0)),
            ],
            out_specs=[pl.BlockSpec((4, 1, HD, wide // 2), lambda p, at: (0, p, 0, 0))] * halves,
        ),
        cost_estimate=SMALL,
        out_shape=[jax.ShapeDtypeStruct((4, places, HD, wide // 2), bf16)] * halves,
    )(at, qkv_t, out_weight)


def me_ff_kernel(at, fc1_ref, fc2_ref, me1_ref, me2_ref):
    me1_ref[...] = fc1_ref[...].T
    me2_ref[...] = fc2_ref[...]


def me_ff(at, fc1_weight, fc2_weight):
    hidden, wide = fc2_weight.shape
    piece = hidden // 8
    return pl.pallas_call(
        me_ff_kernel,
        grid_spec=pltpu.PrefetchScalarGridSpec(
            num_scalar_prefetch=1,
            grid=(1,),
            in_specs=[
                pl.BlockSpec((wide, piece), lambda i, at: (0, at[0])),
                pl.BlockSpec((piece, wide), lambda i, at: (at[0], 0)),
            ],
            out_specs=[pl.BlockSpec((piece, wide), lambda i, at: (0, 0))] * 2,
        ),
        cost_estimate=SMALL,
        out_shape=[jax.ShapeDtypeStruct((piece, wide), bf16)] * 2,
    )(at, fc1_weight, fc2_weight)


def own_ff_kernel(at, fc1_ref, fc2_ref, o1_ref, o2_ref):
    o1_ref[...] = fc1_ref[...]
    o2_ref[...] = fc2_ref[...]


def own_ff(at, fc1_weight, fc2_weight):
    hidden, wide = fc2_weight.shape
    piece = hidden // 8
    return pl.pallas_call(
        own_ff_kernel,
        grid_spec=pltpu.PrefetchScalarGridSpec(
            num_scalar_prefetch=1,
            grid=(8,),
            in_specs=[
                pl.BlockSpec((wide, piece), lambda i, at: (0, at[i])),
                pl.BlockSpec((piece, wide), lambda i, at: (at[i], 0)),
            ],
            out_specs=[
                pl.BlockSpec((wide, piece), lambda i, at: (0, i)),
                pl.BlockSpec((piece, wide), lambda i, at: (i, 0)),
            ],
        ),
        cost_estimate=SMALL,
        out_shape=[
            jax.ShapeDtypeStruct((wide, hidden), bf16),
            jax.ShapeDtypeStruct((hidden, wide), bf16),
        ],
    )(at, fc1_weight, fc2_weight)


def join_att_kernel(exchanged, own_ref, x0_ref, x1_ref, y_ref, *out_refs):
    hops = (y_ref[0], x1_ref[...]) if exchanged else (x1_ref[...], y_ref[0])
    for t, out_ref in enumerate(out_refs):
        out_ref[:, 0] = own_ref[t]
        for place, rest in enumerate((x0_ref[...], *hops, y_ref[1])):
            out_ref[place, 1:] = rest[:, t]


def join_att(own, x0, x1, y, exchanged=False):
    rest, _, hd, half = x0.shape
    step = hd // 4
    one = pl.BlockSpec((rest, 4, step, half), lambda i: (0, 0, i, 0))
    return pl.pallas_call(
        functools.partial(join_att_kernel, exchanged),
        grid=(4,),
        in_specs=[
            pl.BlockSpec((4, 4, step, half), lambda i: (0, 0, i, 0)),
            one,
            one,
            pl.BlockSpec((2, rest, 4, step, half), lambda i: (0, 0, 0, i, 0)),
        ],
        out_specs=[pl.BlockSpec((4, rest + 1, step, half), lambda i: (0, 0, i, 0))] * 4,
        cost_estimate=SMALL,
        out_shape=[jax.ShapeDtypeStruct((4, rest + 1, hd, half), bf16)] * 4,
    )(own, x0, x1, y)


def add_att_kernel(*refs):
    mine, theirs, (hi_ref, lo_ref) = refs[:4], refs[4:8], refs[8:]
    i = pl.program_id(0)
    for t in range(4):
        total = (mine[t][...].astype(f32) + theirs[t][...].astype(f32)).astype(bf16)

        @pl.when(i < 2)
        def _():
            hi_ref[0, t] = total

        @pl.when(i >= 2)
        def _():
            lo_ref[0, t] = total


def add_att(mine, theirs):
    rows, half = mine[0].shape
    ours = pl.BlockSpec((rows // 4, half), lambda i: ((i + 2) % 4, 0))
    got = pl.BlockSpec((rows // 4, half), lambda i: ((2 * i + 1) % 4 - i // 2, 0))
    shape = jax.ShapeDtypeStruct((2, 4, rows // 4, half), bf16)
    return pl.pallas_call(
        add_att_kernel,
        grid=(4,),
        in_specs=[ours] * 4 + [got] * 4,
        out_specs=[
            pl.BlockSpec((1, 4, rows // 4, half), lambda i: (jnp.minimum(i, 1), 0, 0, 0)),
            pl.BlockSpec((1, 4, rows // 4, half), lambda i: (jnp.maximum(i - 2, 0), 0, 0, 0)),
        ],
        cost_estimate=SMALL,
        out_shape=[shape, shape],
    )(*mine, *theirs)


def last_att_kernel(at, left_ref, right_ref, out_ref, qkv_ref):
    rows = jnp.concatenate([left_ref[0], right_ref[0]], axis=-1).astype(f32)
    out_ref[...] = rows[1]
    qkv_ref[0], qkv_ref[1], qkv_ref[2] = rows[0], rows[2], rows[3]


def last_att(at, pieces):
    _, _, hd, half = pieces.shape
    block = lambda c: pl.BlockSpec((1, 4, hd, half), lambda p, at: (at[2 * p + c], 0, 0, 0))
    return pl.pallas_call(
        last_att_kernel,
        grid_spec=pltpu.PrefetchScalarGridSpec(
            num_scalar_prefetch=1,
            grid=(4,),
            in_specs=[block(0), block(1)],
            out_specs=[
                pl.BlockSpec((hd, 2 * half), lambda p, at: (p, 0)),
                pl.BlockSpec((3, hd, 2 * half), lambda p, at: (0, p, 0)),
            ],
        ),
        cost_estimate=SMALL,
        out_shape=[
            jax.ShapeDtypeStruct((4 * hd, 2 * half), f32),
            jax.ShapeDtypeStruct((3, 4 * hd, 2 * half), f32),
        ],
    )(at, pieces, pieces)


def swap(value, b):
    n = lax.axis_size("dp")
    return lax.ppermute(value, "dp", [(i, i ^ (1 << b)) for i in range(n)])


def hop(value, stage):
    n = lax.axis_size("dp")
    return lax.ppermute(
        value, "dp", [(i, i ^ (2 if (i & 1) == stage - 1 else 4)) for i in range(n)]
    )


def move(value, pairs):
    return lax.ppermute(value, "mp", pairs)


def shift(value, s):
    n = lax.axis_size("mp")
    return move(value, [(i, (i + s) % n) for i in range(n)])


def all_eight(value):
    n = lax.axis_size("dp")
    groups = None if n == 8 else [list(range(g, g + 8)) for g in range(0, n, 8)]
    return lax.all_gather(value, "dp", axis=0, axis_index_groups=groups)


def beyond(value):
    for b in range(3, lax.axis_size("dp").bit_length() - 1):
        value = value + swap(value, b)
    return value


def add(a, b):
    return (a.astype(f32) + b.astype(f32)).astype(bf16)


tie = lax.optimization_barrier


def norm_parts(rows):
    mean = jnp.mean(rows, axis=-1, keepdims=True)
    centred = rows - mean
    rstd = lax.rsqrt(jnp.mean(centred * centred, axis=-1, keepdims=True) + eps)
    return centred * rstd, rstd


def norm_back(grad, gain, xhat, rstd):
    scaled = grad * gain
    return rstd * (
        scaled
        - jnp.mean(scaled, axis=-1, keepdims=True)
        - xhat * jnp.mean(scaled * xhat, axis=-1, keepdims=True)
    )


def gelu_both(v):
    c, k = 0.7978845608028654, 0.044715
    t = jnp.tanh(c * (v + k * v * v * v))
    value = 0.5 * v * (1.0 + t)
    slope = 0.5 * (1.0 + t) + 0.5 * v * (1.0 - t * t) * (c * (1.0 + 3.0 * k * v * v))
    return value, slope


def body(
    tokens,
    segment_ids,
    norm1_gain,
    norm1_shift,
    qkv_weight,
    qv_bias,
    out_weight,
    out_bias,
    norm2_gain,
    norm2_shift,
    fc1_weight,
    fc1_bias,
    fc2_weight,
    fc2_bias,
    out_grad,
):
    rows, wide = tokens.shape
    half = wide // 2
    mp = lax.axis_size("mp")
    m = lax.axis_index("mp")
    d = lax.axis_index("dp") & 7
    core = d & 1
    ff_here = fc1_weight.shape[1]
    piece = ff_here // 8
    heads_here = qkv_weight.shape[2] // HD
    rest = mp - 1

    def slice_at(k):
        first = jnp.where((core ^ (k >> 2)) == 0, 2, 4)
        return d ^ ((k >> 2) + (k & 1) * first + ((k >> 1) & 1) * (6 - first))

    slices = slice_at(jnp.arange(8))
    place = slice_at(jnp.arange(4)) >> 1
    row = jnp.arange(mp * 8)
    other = jnp.maximum(row - 8, 0)
    shifts = jnp.where(row < 8, 0, other % rest + 1)
    lies_at = slice_at(jnp.where(row < 8, row, other // rest))
    ff_rows = (m + mp - shifts) % mp * 8 + lies_at
    ff_from = shifts * 8 + lies_at
    head = jnp.arange(mp * heads_here)
    head_place = slice_at(head // mp) >> 1
    heads = (m + mp - head % mp) % mp * heads_here + head_place
    heads_from = head % mp * heads_here + head_place
    slopes = jnp.exp2(-8.0 * (heads + 1).astype(f32) / HEADS)

    def pick(table, at):
        n = table.shape[0]
        chosen = (at[:, None] == jnp.arange(n)[None, :]).astype(f32)
        return lax.dot(chosen, table, precision=lax.Precision.HIGHEST)

    near_rows = DOC_MOST - rows
    halo = DOC_MOST
    qv_own = jnp.transpose(qv_bias.reshape(2, heads_here, HD), (1, 0, 2))
    bias_own = jnp.concatenate([fc1_bias.reshape(8, piece), qv_own.reshape(heads_here, 2 * HD)])
    bias_all = [bias_own] + [shift(bias_own, s) for s in range(1, mp)]
    qkv_t = jnp.transpose(qkv_weight, (1, 2, 0))
    att_places = jnp.concatenate([core[None], place])
    (att_me,) = own_att(1, att_places, qkv_t, out_weight)
    att_me = att_me.reshape(4, HD, half)
    att_z = [shift(att_me, s) for s in range(1, mp)]
    halo1 = move(tokens, [(i, i + 1) for i in range(mp - 1)])
    fc1_b = pick(jnp.concatenate([v[:8] for v in bias_all]), ff_from).reshape(-1)
    qv_b = pick(jnp.concatenate([v[8:] for v in bias_all]), heads_from)
    q_bias, v_bias = qv_b[:, :HD].reshape(-1), qv_b[:, HD:].reshape(-1)
    seg_row = jnp.concatenate([jnp.full((1, halo), -1, jnp.int32), segment_ids], 1)
    segk = lax.dynamic_slice_in_dim(seg_row, m * rows, halo + rows, 1)
    segq = segk[:, halo:]
    segk = segk.reshape(halo + rows, 1)

    small_ones = (fc1_b, q_bias, v_bias, segk, segq, slopes)
    att_z, halo1, small_ones, slices, att_places = tie(
        (att_z, halo1, small_ones, slices, att_places)
    )
    fc1_b, q_bias, v_bias, segk, segq, slopes = small_ones
    halo2 = move(halo1[rows - near_rows :], [(i, i + 1) for i in range(mp - 1)])
    att_x0 = jnp.stack(att_z)
    att_x1 = hop(att_x0, 1)
    me1, me2 = me_ff(slices, fc1_weight, fc2_weight)
    own = own_att(2, att_places, qkv_t, out_weight)
    own1, own2 = own_ff(slices, fc1_weight, fc2_weight)
    att_x1, halo2, me1, me2, own, own1, own2 = tie((att_x1, halo2, me1, me2, own, own1, own2))
    z1 = [shift(me1, s) for s in range(1, mp)]
    part0 = swap(att_x0, 0)
    att_y = hop(jnp.stack([att_x0, att_x1]), 2)
    part1 = swap(att_x1, 0)
    ext = jnp.concatenate([halo2, halo1, tokens], 0).astype(f32)
    xhat_ext, rstd_ext = norm_parts(ext)
    norm1 = (xhat_ext * norm1_gain + norm1_shift).astype(bf16)
    col = [core * half, (1 - core) * half]

    def cols(value):
        return [lax.dynamic_slice_in_dim(value, at, half, 1) for at in col]

    def join(own, other):
        first = core == 0
        return jnp.concatenate([jnp.where(first, own, other), jnp.where(first, other, own)], 1)

    n1 = cols(norm1)
    att_y, part0, part1, z1, n1 = tie((att_y, part0, part1, z1, n1))
    z2 = [shift(me2, s) for s in range(1, mp)]
    part_y = swap(att_y, 0)
    w_att = [
        join_att(own[0], att_x0, att_x1, att_y),
        join_att(own[1], part0, part1, part_y, True),
    ]
    w_att = [[w.reshape(HEADS * HD, half) for w in four] for four in w_att]

    def project(t, lhs):
        return dot(lhs[0], w_att[0][t], 1, 1) + dot(lhs[1], w_att[1][t], 1, 1)

    q = (project(0, [v[halo:] for v in n1]) + q_bias).astype(bf16)
    k = project(2, n1).astype(bf16)
    v = (project(3, n1) + v_bias).astype(bf16)

    cut = rest * piece

    x0_1 = jnp.concatenate(z1)
    q, x0_1, z2 = tie((q, x0_1, z2))
    x1_1 = hop(x0_1, 1)
    first = attend(0, slopes, segq, segk, q, k, v)
    first, x1_1, z2 = tie((first, x1_1, z2))
    x0_2 = jnp.concatenate(z2)
    z1 = jnp.concatenate([x0_1, x1_1])
    y1 = hop(z1, 2)
    x1_2 = hop(x0_2, 1)
    context, lse = attend(1, slopes, segq, segk, q, k, v, first)
    context, y1, x1_2 = tie((context, y1, x1_2))
    z2 = jnp.concatenate([x0_2, x1_2])
    y2 = hop(z2, 2)
    w1 = [z1, y1, swap(z1, 0), swap(y1, 0)]
    w2 = [z2, y2, swap(z2, 0), swap(y2, 0)]
    attention = join(dot(context, w_att[0][1], 1, 0), dot(context, w_att[1][1], 1, 0))
    tokens_wide = tokens.astype(f32)
    resid = attention + out_bias + tokens_wide
    xhat2, rstd2 = norm_parts(resid)
    norm2 = (xhat2 * norm2_gain + norm2_shift).astype(bf16)

    pre, at = [dot(norm2, own1, 1, 0) + fc1_b[:ff_here]], ff_here
    for w in w1:
        pre.append(dot(norm2, w, 1, 1) + fc1_b[at : at + w.shape[0]])
        at += w.shape[0]
    hidden = [gelu_both(p)[0].astype(bf16) for p in pre]

    def partials(lhs, rhs):
        send = [lhs[3], lhs[4], lhs[0][:, 4 * piece :]]
        return [dot(v, rhs, 0, 0).astype(bf16) for v in send]

    def after_core(lhs, rhs, got):
        hi = jnp.concatenate(
            [
                (dot(lhs[2], rhs, 0, 0) + got[1].astype(f32)).astype(bf16),
                (dot(lhs[0][:, 2 * piece : 4 * piece], rhs, 0, 0) + got[2][2 * piece :].astype(f32)).astype(bf16),
            ]
        )
        lo = [
            (dot(lhs[1], rhs, 0, 0) + got[0].astype(f32)).astype(bf16),
            (dot(lhs[0][:, : 2 * piece], rhs, 0, 0) + got[2][: 2 * piece].astype(f32)).astype(bf16),
        ]
        return hi, lo

    def after_hop2(lo, got):
        send = jnp.concatenate([add(lo[0][cut:], got[cut : 2 * cut]), add(lo[1][piece:], got[2 * cut + piece :])])
        keep = [add(lo[0][:cut], got[:cut]), add(lo[1][:piece], got[2 * cut : 2 * cut + piece])]
        return send, keep

    def to_mp(keep, got):
        sent = [
            shift(add(keep[0][at : at + piece], got[at : at + piece]), mp - 1 - at // piece)
            for at in range(0, cut, piece)
        ]
        return sent, keep[1].astype(f32) + got[cut:].astype(f32)

    def all_mp(sent, mine):
        for got in sent:
            mine = mine + got.astype(f32)
        return beyond(mine).astype(bf16)

    send2 = partials(hidden, out_grad)
    got2 = [swap(v, 0) for v in send2]
    mlp = sum(dot(h, w, 1, 0) for h, w in zip(hidden, [own2] + w2))
    result = (mlp + fc2_bias + resid).astype(bf16)
    grad_pre = [
        (dot(out_grad, w, 1, 1) * gelu_both(p)[1]).astype(bf16) for w, p in zip([own2] + w2, pre)
    ]
    send1 = partials(grad_pre, norm2)
    got1 = [swap(v, 0) for v in send1]
    hi2, lo2 = after_core(hidden, out_grad, got2)
    hop2_2 = hop(hi2, 2)

    grad_norm2 = dot(grad_pre[0], own1, 1, 1)
    grad_norm2 = grad_norm2 + sum(dot(g, w, 1, 0) for g, w in zip(grad_pre[1:], w1))
    out_grad_wide = out_grad.astype(f32)
    grad_resid = out_grad_wide + norm_back(grad_norm2, norm2_gain, xhat2, rstd2)
    hi1, lo1 = after_core(grad_pre, norm2, got1)
    grad_att = cols(grad_resid.astype(bf16))
    grad_context = (
        dot(grad_att[0], w_att[0][1], 1, 1) + dot(grad_att[1], w_att[1][1], 1, 1)
    ).astype(bf16)

    grad_context, hi1, hi2 = tie((grad_context, hi1, hi2))
    hop2_1 = hop(hi1, 2)
    first = attend_back(0, slopes, segq, segk, q, k, v, grad_context, lse)
    first, hop2_2 = tie((first, hop2_2))
    send2, keep2 = after_hop2(lo2, hop2_2)
    hop1_2 = hop(send2, 1)
    second = attend_back(1, slopes, segq, segk, q, k, v, grad_context, lse, first)
    second, hop2_1, hop1_2 = tie((second, hop2_1, hop1_2))
    send1, keep1 = after_hop2(lo1, hop2_1)
    hop1_1 = hop(send1, 1)
    z2, mine2 = to_mp(keep2, hop1_2)
    grads = attend_back(2, slopes, segq, segk, q, k, v, grad_context, lse, second)
    (dq, dk, dv), hop1_1, z2 = tie((grads, hop1_1, z2))
    z1, mine1 = to_mp(keep1, hop1_1)
    sum2 = all_mp(z2, mine2)

    def weights_half(i):
        return [
            dot(dq, n1[i][halo:], 0, 0).astype(bf16),
            dot(context, grad_att[i], 0, 0).astype(bf16),
            dot(dk, n1[i], 0, 0).astype(bf16),
            dot(dv, n1[i], 0, 0).astype(bf16),
        ]

    def back_half(i):
        tail = dot(dk, w_att[i][2], 1, 0) + dot(dv, w_att[i][3], 1, 0)
        return tail[:halo], tail[halo:] + dot(dq, w_att[i][0], 1, 0)

    theirs = weights_half(1)
    theirs, dk = tie((theirs, dk))
    theirs = [swap(v, 0) for v in theirs]
    back = [back_half(0), back_half(1)]
    grad_halo = join(back[0][0], back[1][0]).astype(bf16)
    grad_halo, dv, theirs, z1 = tie((grad_halo, dv, theirs, z1))
    ff_sums = all_eight(jnp.stack([all_mp(z1, mine1), sum2]))
    near = move(grad_halo[near_rows:], [(i, i - 1) for i in range(1, mp)])
    passed = move(grad_halo[:near_rows], [(i, i - 2) for i in range(2, mp)])
    mine = weights_half(0)
    att_hi, att_lo = add_att(mine, theirs)
    att_got = hop(att_hi, 2)
    grad_norm1 = join(back[0][1], back[1][1])
    att_got, near, passed, grad_norm1 = tie((att_got, near, passed, grad_norm1))
    att_hop1 = hop(add(att_lo[1], att_got[1]), 1)
    att_keep = add(att_lo[0], att_got[0])
    grad_fc1 = ff_sums[:, 0].reshape(ff_here, wide).T.astype(f32)
    grad_fc2 = ff_sums[:, 1].reshape(ff_here, wide).astype(f32)
    near = jnp.pad(passed.astype(f32), ((rows - near_rows, 0), (0, 0))) + near.astype(f32)
    grad_norm1 = grad_norm1 + near
    xhat1, rstd1 = xhat_ext[halo:], rstd_ext[halo:]
    in_grad = grad_resid + norm_back(grad_norm1, norm1_gain, xhat1, rstd1)
    att_hop1, in_grad = tie((att_hop1, in_grad))
    att_keep = add(att_keep, att_hop1).reshape(4, mp, HD, half)
    att_z = [shift(att_keep[:, s], mp - s) for s in range(1, mp)]
    ff_bias = jnp.concatenate([jnp.sum(g.astype(f32), axis=0) for g in grad_pre])
    ff_bias = ff_bias.reshape(mp * 8, piece)
    qv_sums = jnp.concatenate(
        [jnp.sum(g.astype(f32), axis=0).reshape(mp * heads_here, HD) for g in (dq, dv[:, :])], 1
    )

    def in_order(table, at):
        n = table.shape[0]
        chosen = (at[None, :] == jnp.arange(n)[:, None]).astype(f32)
        return lax.dot(chosen, table, precision=lax.Precision.HIGHEST)

    small = jnp.stack(
        [
            jnp.sum(grad_resid, axis=0),
            jnp.sum(grad_norm1 * xhat1, axis=0),
            jnp.sum(grad_norm1, axis=0),
            jnp.sum(grad_norm2 * xhat2, axis=0),
            jnp.sum(grad_norm2, axis=0),
            jnp.sum(out_grad_wide, axis=0),
        ]
    )
    n_small = wide // mp
    vectors = jnp.concatenate(
        [
            jnp.transpose(small.reshape(6, mp, n_small), (1, 0, 2)).reshape(mp, -1),
            in_order(qv_sums, heads).reshape(mp, -1),
            in_order(ff_bias, ff_rows).reshape(mp, -1),
        ],
        1,
    )
    for bit in range(lax.axis_size("dp").bit_length() - 1):
        vectors = vectors + swap(vectors, bit)
    att_z, vectors, grad_fc1, grad_fc2 = tie((att_z, vectors, grad_fc1, grad_fc2))
    att_sum = att_keep[:, 0].astype(f32)
    for got in att_z:
        att_sum = att_sum + got.astype(f32)
    att_sum = beyond(att_sum).astype(bf16)
    att_sum = jnp.stack([att_sum, hop(att_sum, 2)])
    att_sum = jnp.stack([att_sum, hop(att_sum, 1)])
    att_sum = att_sum.reshape(4, 4, HD, half)
    att_sum = jnp.stack([att_sum, swap(att_sum, 0)]).reshape(8, 4, HD, half)
    from_slice = slice_at((row[:8] & 4) + ((row[:8] & 1) << 1) + ((row[:8] >> 1) & 1))
    at = jnp.sum(jnp.where(from_slice[None] == row[:8, None], row[None, :8], 0), axis=1)
    grad_out, grad_qkv = last_att(at, att_sum)
    grad_qkv = jnp.transpose(grad_qkv, (2, 0, 1))
    for bit in range(mp.bit_length() - 1):
        vectors = vectors + move(vectors, [(i, i ^ (1 << bit)) for i in range(mp)])
    total = lax.dynamic_index_in_dim(vectors, m, 0, False)
    six = total[: 6 * n_small].reshape(6, n_small)
    n_qv = heads_here * HD
    grad_qv = total[6 * n_small : 6 * n_small + 2 * n_qv].reshape(heads_here, 2, HD)
    grad_qv = jnp.transpose(grad_qv, (1, 0, 2)).reshape(2, n_qv)
    grad_fc1_bias = total[6 * n_small + 2 * n_qv :]
    return (
        result,
        in_grad,
        six[1],
        six[2],
        grad_qkv,
        grad_qv,
        grad_out,
        six[0],
        six[3],
        six[4],
        grad_fc1,
        grad_fc1_bias,
        grad_fc2,
        six[5],
    )


def solution(mesh):
    placed = (
        P(("dp", "mp"), None),
        P("dp", None),
        P(),
        P(),
        P(None, None, "mp"),
        P(None, "mp"),
        P("mp", None),
        P(),
        P(),
        P(),
        P(None, "mp"),
        P("mp"),
        P("mp", None),
        P(),
        P(("dp", "mp"), None),
    )
    return jax.shard_map(
        body,
        mesh=mesh,
        in_specs=placed,
        out_specs=(
            P(("dp", "mp"), None),
            P(("dp", "mp"), None),
            P("mp"),
            P("mp"),
            P(None, None, "mp"),
            P(None, "mp"),
            P("mp", None),
            P("mp"),
            P("mp"),
            P("mp"),
            P(None, "mp"),
            P("mp"),
            P("mp", None),
            P("mp"),
        ),
        check_vma=False,
    )
```

time: 635 us -> 541 us (0.85)
  blocking collectives: 72.3 us -> 0 us
  Pallas kernels: 82.4 us -> 102 us
  matrix products: 110 us -> 93.9 us
  waiting for transfers between devices: 157 us -> 141 us
  local copies, waits for them, and re-layouts: 64 us -> 48.7 us
    ppermute x11 -> x14, waiting for transfers between devices: 78.7 us -> 21.2 us  [hop(): lax.ppermute(value, 'dp', [(i, i ^ (2 if i & 1 == stage - 1 else 4)) for...]
    psum x1 -> x0, blocking collectives: 39.4 us -> none  [body(): vectors = lax.psum(vectors, ('dp', 'mp'))]
    all_gather x1 -> x0, blocking collectives: 32.9 us -> none  [body(): lax.all_gather(jnp.concatenate([fc1_bias, qv_bias.reshape(-1)]), 'mp', ax...]
    ppermute x19 -> x27, waiting for transfers between devices: 78.5 us -> 107 us  [move(): return lax.ppermute(value, 'mp', pairs)]
    pallas_call x4 -> x10, Pallas kernels: 70.5 us -> 88.1 us  [the longest x3 37.2 us: attend_back(): pl.pallas_call(functools.partial(attend_back_kernel, halo, start), grid=(...]
    dot_general x58, matrix products: 110 us -> 92.6 us  [dot(): lax.dot_general(a, b, (((ca,), (cb,)), ((), ())), preferred_element_type=...]
    ppermute x15 -> x21, waiting for transfers between devices: 0.04 us -> 13.7 us  [swap(): return lax.ppermute(value, 'dp', [(i, i ^ 1 << b) for i in range(n)])]
    unnamed x225 -> x243, local copies, waits for them, and re-layouts: 39.4 us -> 30.3 us
  transfers between devices with their start and end apart: 47 -> 63, of which waited for: 16 -> 16; matrix products, arithmetic and copies ran while one was open for 30% -> 30% of each run, Pallas kernels for 11% -> 18%
where the time goes in v3:
time: 541 us; the launch traced here: 534 us
  waiting for transfers between devices  141 us (26%)
  Pallas kernels  102 us (19%)
  matrix products  93.9 us (17%)
  starting transfers between devices  80.8 us (15%)
  other arithmetic  51.2 us (9%)
  local copies, waits for them, and re-layouts  48.7 us (9%)
  between operations  16.3 us (3%)
    ppermute x27, waiting for transfers between devices, move(): return lax.ppermute(value, 'mp', pairs)  107 us
    dot_general x58, matrix products, dot(): lax.dot_general(a, b, (((ca,), (cb,)), ((), ())), preferred_element_type=...  92.6 us
    ppermute x27, starting transfers between devices, move(): return lax.ppermute(value, 'mp', pairs)  58 us
    pallas_call x3, Pallas kernels, attend_back(): pl.pallas_call(functools.partial(attend_back_kernel, halo, start), grid=(...  37.2 us
    unnamed x243, local copies, waits for them, and re-layouts  30.3 us
    pallas_call x2, Pallas kernels, attend(): pl.pallas_call(functools.partial(attend_kernel, halo, start), grid=(pairs...  27.1 us
    ppermute x14, waiting for transfers between devices, hop(): lax.ppermute(value, 'dp', [(i, i ^ (2 if i & 1 == stage - 1 else 4)) for...  21.2 us
    ppermute x14, starting transfers between devices, hop(): lax.ppermute(value, 'dp', [(i, i ^ (2 if i & 1 == stage - 1 else 4)) for...  17.2 us
  transfers between devices with their start and end apart: 63, of which 16 were waited for; matrix products, arithmetic and copies ran while one was open for 30% of the time, Pallas kernels for 18%

profile of v3, /device:TPU:0, one launch (start us, length us, event | category | flops | bytes accessed | tf_op | source)
XLA Modules:
  0.0 534.5 jit_solution(10293522184515822400)
XLA Ops:
  8.8 5.1 collective-permute-start.6
  16.4 4.4 collective-permute-start.3
  31.8 18.3 %collective-permute-done.2 = bf16[4,64,512]{2,1,0:T(8,128)(2,1)S(1)} collective-permute-done((bf16[4,64,512]{2,1,0:T(8,128)(2,1)}, bf16[4,64,512]{2,1,0:T(8,128)(2,1)S(1)}, u32[]{:S(2)}, u32[]{:S(2)}) %collective-permute-start.2) | collective-permute-done | bytes 262176 | tf_op jit(solution)/shard_map/ppermute | solution.py:360
  50.1 5.6 %collective-permute-done.1 = bf16[4,64,512]{2,1,0:T(8,128)(2,1)S(1)} collective-permute-done((bf16[4,64,512]{2,1,0:T(8,128)(2,1)}, bf16[4,64,512]{2,1,0:T(8,128)(2,1)S(1)}, u32[]{:S(2)}, u32[]{:S(2)}) %collective-permute-start.1) | collective-permute-done | bytes 262176 | tf_op jit(solution)/shard_map/ppermute | solution.py:360
  64.3 7.8 %collective-permute-start.8 = (bf16[256,1024]{0,1:T(8,128)(2,1)}, bf16[256,1024]{0,1:T(8,128)(2,1)S(1)}, u32[]{:S(2)}, u32[]{:S(2)}) collective-permute-start(bf16[256,1024]{0,1:T(8,128)(2,1)} %slice.296), channel_id=1, source_target_pairs={{0,1},{1,2},{2,3},{4,5},{5,6},{6,7},{8,9},{9,10},{10,11},{12,13},{... | collective-permute-start | bytes 1572872 | tf_op jit(solution)/shard_map/ppermute | solution.py:360
  74.8 7.3 %shard_map.257 = (bf16[1024,1024]{1,0:T(8,128)(2,1)}, bf16[1024,1024]{1,0:T(8,128)(2,1)}) custom-call(s32[8]{0:T(128)} %add_xor_fusion.1.at, bf16[1024,1024]{1,0:T(8,128)(2,1)} %fc1_ref.3, bf16[1024,1024]{1,0:T(8,128)(2,1)} %fc2_ref.3), custom_call_target="tpu_custom_call" | custom-call | flops 1 | bytes 1 | tf_op jit(solution)/shard_map/pallas_call | solution.py:237
  82.1 4.4 shard_map.256
  97.9 16.2 %collective-permute-done.13 = bf16[128,1024]{1,0:T(8,128)(2,1)S(1)} collective-permute-done((bf16[128,1024]{1,0:T(8,128)(2,1)}, bf16[128,1024]{1,0:T(8,128)(2,1)S(1)}, u32[]{:S(2)}, u32[]{:S(2)}) %collective-permute-start.13) | collective-permute-done | bytes 262176 | tf_op jit(solution)/shard_map/ppermute | solution.py:360
  117.5 5.0 shard_map.258
  124.5 4.8 shard_map.259
  132.2 7.0 %collective-permute-done.17 = bf16[128,1024]{1,0:T(8,128)(2,1)} collective-permute-done((bf16[128,1024]{1,0:T(8,128)(2,1)}, bf16[128,1024]{1,0:T(8,128)(2,1)}, u32[]{:S(2)}, u32[]{:S(2)}) %collective-permute-start.17) | collective-permute-done | bytes 262176 | tf_op jit(solution)/shard_map/ppermute | solution.py:360
  146.7 13.3 %shard_map.260 = (bf16[512,1024]{1,0:T(8,128)(2,1)S(1)}, f32[8,2,512]{2,1,0:T(2,128)S(1)}) custom-call(f32[16]{0:T(128)S(1)} %get-tuple-element.131.slopes, s32[1,512]{1,0:T(1,128)S(1)} %pad_dynamic-slice_fusion.segq, s32[1280,1]{1,0:T(8,128)S(1)} %copy.150.segk, bf16[512,1024]{1,0:T(8,128)(2,1)S(1)} %add_convert_fusion.12.q_ref, ...), custom_call_target="tpu_custom_call" | custom-call | flops 1 | bytes 1 | tf_op jit(solution)/shard_map/pallas_call | solution.py:114
  175.1 13.7 %shard_map.261 = (bf16[512,1024]{1,0:T(8,128)(2,1)S(1)}, f32[8,2,512]{2,1,0:T(2,128)S(1)}) custom-call(f32[16]{0:T(128)S(1)} %get-tuple-element.131.slopes, s32[1,512]{1,0:T(1,128)S(1)} %pad_dynamic-slice_fusion.segq, s32[1280,1]{1,0:T(8,128)S(1)} %copy.150.segk, bf16[512,1024]{1,0:T(8,128)(2,1)S(1)} %copy-done.4, ...), custom_call_target="tpu_custom_call", output_to_operand_aliasing={{0}: (6, {}), {1}: (7, {})} | custom-call | flops 1 | bytes 1 | tf_op jit(solution)/shard_map/pallas_call | solution.py:114
  251.3 13.9 %shard_map.262 = (bf16[512,1024]{1,0:T(8,128)(2,1)S(1)}, bf16[1280,1024]{1,0:T(8,128)(2,1)}, bf16[1280,1024]{1,0:T(8,128)(2,1)}) custom-call(f32[16]{0:T(128)S(1)} %get-tuple-element.131.slopes, s32[1,512]{1,0:T(1,128)S(1)} %pad_dynamic-slice_fusion.segq, s32[1280,1]{1,0:T(8,128)S(1)} %copy.150.segk, bf16[512,1024]{1,0:T(8,128)(2,1)S(1)} %copy-done.5, ...), custom_call_target="tpu_custom_call" | custom-call | flops 1 | bytes 1 | tf_op jit(solution)/shard_map/pallas_call | solution.py:146
  270.5 13.5 %shard_map.263 = (bf16[512,1024]{1,0:T(8,128)(2,1)S(1)}, bf16[1280,1024]{1,0:T(8,128)(2,1)}, bf16[1280,1024]{1,0:T(8,128)(2,1)}) custom-call(f32[16]{0:T(128)S(1)} %get-tuple-element.131.slopes, s32[1,512]{1,0:T(1,128)S(1)} %pad_dynamic-slice_fusion.segq, s32[1280,1]{1,0:T(8,128)S(1)} %copy.150.segk, ...), custom_call_target="tpu_custom_call", output_to_operand_aliasing={{0}: (8, {}), {1}: (9, {}), {2}: (10, {})} | custom-call | flops 1 | bytes 1 | tf_op jit(solution)/shard_map/pallas_call | solution.py:146
  284.0 8.1 %collective-permute-done.34 = bf16[512,1024]{1,0:T(8,128)(2,1)S(1)} collective-permute-done((bf16[512,1024]{1,0:T(8,128)(2,1)S(1)}, bf16[512,1024]{1,0:T(8,128)(2,1)S(1)}, u32[]{:S(2)}, u32[]{:S(2)}) %collective-permute-start.34) | collective-permute-done | bytes 1048608 | tf_op jit(solution)/shard_map/ppermute | solution.py:354
  292.1 5.9 %collective-permute-done.32 = bf16[1024,1024]{1,0:T(8,128)(2,1)S(1)} collective-permute-done((bf16[1024,1024]{1,0:T(8,128)(2,1)}, bf16[1024,1024]{1,0:T(8,128)(2,1)S(1)}, u32[]{:S(2)}, u32[]{:S(2)}) %collective-permute-start.32) | collective-permute-done | bytes 2097184 | tf_op jit(solution)/shard_map/ppermute | solution.py:354
  309.6 9.8 %shard_map.264 = (bf16[512,1024]{1,0:T(8,128)(2,1)S(1)}, bf16[1280,1024]{1,0:T(8,128)(2,1)}, bf16[1280,1024]{1,0:T(8,128)(2,1)}) custom-call(f32[16]{0:T(128)S(1)} %get-tuple-element.131.slopes, s32[1,512]{1,0:T(1,128)S(1)} %pad_dynamic-slice_fusion.segq, s32[1280,1]{1,0:T(8,128)S(1)} %copy.150.segk, ...), custom_call_target="tpu_custom_call", output_to_operand_aliasing={{0}: (8, {}), {1}: (9, {}), {2}: (10, {})} | custom-call | flops 1 | bytes 1 | tf_op jit(solution)/shard_map/pallas_call | solution.py:146
  322.2 3.9 convolution_convert_fusion.6
  328.0 6.3 %collective-permute-start.46 = (bf16[128,1024]{1,0:T(8,128)(2,1)S(1)}, bf16[128,1024]{1,0:T(8,128)(2,1)S(1)}, u32[]{:S(2)}, u32[]{:S(2)}) collective-permute-start(bf16[128,1024]{1,0:T(8,128)(2,1)S(1)} %get-tuple-element.349), channel_id=1, source_target_pairs={{0,1},{1,2},{2,3},{3,0},{4,5},{5,6},{6,7},{7,4},{8,9},{9,10},{10,1... | collective-permute-start | bytes 786440 | tf_op jit(solution)/shard_map/ppermute | solution.py:360
  346.6 10.6 %collective-permute-done.45 = bf16[128,1024]{1,0:T(8,128)(2,1)S(1)} collective-permute-done((bf16[128,1024]{1,0:T(8,128)(2,1)S(1)}, bf16[128,1024]{1,0:T(8,128)(2,1)S(1)}, u32[]{:S(2)}, u32[]{:S(2)}) %collective-permute-start.45) | collective-permute-done | bytes 262176 | tf_op jit(solution)/shard_map/ppermute | solution.py:360
  361.2 4.6 collective-permute-done.44
  370.2 4.7 fusion.143
  383.9 6.6 %shard_map.265 = (bf16[2,4,256,512]{3,2,1,0:T(8,128)(2,1)}, bf16[2,4,256,512]{3,2,1,0:T(8,128)(2,1)}) custom-call(bf16[1024,512]{1,0:T(8,128)(2,1)} %convolution_convert_fusion.11.refs_0_, bf16[1024,512]{1,0:T(8,128)(2,1)} %convolution_convert_fusion.10.refs_1_, bf16[1024,512]{1,0:T(8,128)(2,1)} %convolution_convert_fusion.5.refs_2_, ...), custom_call_target="tpu_custom_call" | custom-call | flops 1 | bytes 1 | tf_op jit(solution)/shard_map/pallas_call | solution.py:306
  404.9 36.9 %collective-permute-done.49 = bf16[256,1024]{0,1:T(8,128)(2,1)} collective-permute-done((bf16[256,1024]{0,1:T(8,128)(2,1)}, bf16[256,1024]{0,1:T(8,128)(2,1)}, u32[]{:S(2)}, u32[]{:S(2)}) %collective-permute-start.49) | collective-permute-done | bytes 524320 | tf_op jit(solution)/shard_map/ppermute | solution.py:360
  451.0 12.4 %collective-permute-done.55 = f32[4,3072]{1,0:T(4,128)S(1)} collective-permute-done((f32[4,3072]{1,0:T(4,128)S(1)}, f32[4,3072]{1,0:T(4,128)S(1)}, u32[]{:S(2)}, u32[]{:S(2)}) %collective-permute-start.55) | collective-permute-done | bytes 49184 | tf_op jit(solution)/shard_map/ppermute | solution.py:349
  464.3 4.2 multiply_add_fusion.5
  471.1 3.8 collective-permute-start.51
  480.3 5.3 copy.184
  492.0 5.5 %collective-permute-done.59 = bf16[4,64,512]{2,1,0:T(8,128)(2,1)S(1)} collective-permute-done((bf16[4,64,512]{2,1,0:T(8,128)(2,1)S(1)}, bf16[4,64,512]{2,1,0:T(8,128)(2,1)S(1)}, u32[]{:S(2)}, u32[]{:S(2)}) %collective-permute-start.59) | collective-permute-done | bytes 262176 | tf_op jit(solution)/shard_map/ppermute | solution.py:354
  503.5 3.9 collective-permute-start.58
  519.0 4.9 shard_map.266
  (516 shorter events, 240.3 us)
Async XLA Ops:
  7.2 467.7 %all-gather.3.cloned.1.call-start = ((), (), s32[]{:S(2)}) async-start(), calls=%async_computation | async-start | bytes 4718592 | tf_op jit(solution)/shard_map/all_gather | solution.py:371
  16.4 43.0 %collective-permute-start.3 = (bf16[512,1024]{0,1:T(8,128)(2,1)S(1)}, bf16[512,1024]{0,1:T(8,128)(2,1)S(1)}, u32[]{:S(2)}, u32[]{:S(2)}) collective-permute-start(bf16[512,1024]{0,1:T(8,128)(2,1)S(1)} %copy.146), channel_id=1, source_target_pairs={{0,1},{1,2},{2,3},{4,5},{5,6},{6,7},{8,9},{9,10},{10,11},{12,13},{... | collective-permute-start | bytes 3145736 | tf_op jit(solution)/shard_map/ppermute | solution.py:360
  26.4 23.6 %collective-permute-start.2 = (bf16[4,64,512]{2,1,0:T(8,128)(2,1)}, bf16[4,64,512]{2,1,0:T(8,128)(2,1)S(1)}, u32[]{:S(2)}, u32[]{:S(2)}) collective-permute-start(bf16[4,64,512]{2,1,0:T(8,128)(2,1)} %bitcast.220), channel_id=1, source_target_pairs={{0,3},{1,0},{2,1},{3,2},{4,7},{5,4},{6,5},{7,6},{8,11},{9,8},{10,9... | collective-permute-start | bytes 786440 | tf_op jit(solution)/shard_map/ppermute | solution.py:360
  27.6 28.1 %collective-permute-start.1 = (bf16[4,64,512]{2,1,0:T(8,128)(2,1)}, bf16[4,64,512]{2,1,0:T(8,128)(2,1)S(1)}, u32[]{:S(2)}, u32[]{:S(2)}) collective-permute-start(bf16[4,64,512]{2,1,0:T(8,128)(2,1)} %bitcast.221), channel_id=1, source_target_pairs={{0,2},{1,3},{2,0},{3,1},{4,6},{5,7},{6,4},{7,5},{8,10},{9,11},{10,... | collective-permute-start | bytes 786440 | tf_op jit(solution)/shard_map/ppermute | solution.py:360
  29.1 30.2 %collective-permute-start = (bf16[4,64,512]{2,1,0:T(8,128)(2,1)}, bf16[4,64,512]{2,1,0:T(8,128)(2,1)S(1)}, u32[]{:S(2)}, u32[]{:S(2)}) collective-permute-start(bf16[4,64,512]{2,1,0:T(8,128)(2,1)} %bitcast.222), channel_id=1, source_target_pairs={{0,1},{1,2},{2,3},{3,0},{4,5},{5,6},{6,7},{7,4},{8,9},{9,10},{10,1... | collective-permute-start | bytes 786440 | tf_op jit(solution)/shard_map/ppermute | solution.py:360
  62.0 24.5 %collective-permute-start.7 = (bf16[3,4,64,512]{3,2,1,0:T(8,128)(2,1)S(1)}, bf16[3,4,64,512]{3,2,1,0:T(8,128)(2,1)}, u32[]{:S(2)}, u32[]{:S(2)}) collective-permute-start(bf16[3,4,64,512]{3,2,1,0:T(8,128)(2,1)S(1)} %get-tuple-element.360.x0_ref), channel_id=1, source_target_pairs={{0,8},{4,20},{8,0},{12,28},{16,24},{20,4},{24,16},{28,12},{1,9},{5... | collective-permute-start | bytes 2359304 | tf_op jit(solution)/shard_map/ppermute | solution.py:354
  64.3 22.2 %collective-permute-start.8 = (bf16[256,1024]{0,1:T(8,128)(2,1)}, bf16[256,1024]{0,1:T(8,128)(2,1)S(1)}, u32[]{:S(2)}, u32[]{:S(2)}) collective-permute-start(bf16[256,1024]{0,1:T(8,128)(2,1)} %slice.296), channel_id=1, source_target_pairs={{0,1},{1,2},{2,3},{4,5},{5,6},{6,7},{8,9},{9,10},{10,11},{12,13},{... | collective-permute-start | bytes 1572872 | tf_op jit(solution)/shard_map/ppermute | solution.py:360
  72.1 25.4 %collective-permute-start.10 = (bf16[3,4,64,512]{3,2,1,0:T(8,128)(2,1)S(1)}, bf16[3,4,64,512]{3,2,1,0:T(8,128)(2,1)}, u32[]{:S(2)}, u32[]{:S(2)}) collective-permute-start(bf16[3,4,64,512]{3,2,1,0:T(8,128)(2,1)S(1)} %get-tuple-element.360.x0_ref), channel_id=1, source_target_pairs={{0,4},{4,0},{8,12},{12,8},{16,20},{20,16},{24,28},{28,24},{1,5},{5... | collective-permute-start | bytes 2359304 | tf_op jit(solution)/shard_map/ppermute | solution.py:349
  86.6 27.5 %collective-permute-start.13 = (bf16[128,1024]{1,0:T(8,128)(2,1)}, bf16[128,1024]{1,0:T(8,128)(2,1)S(1)}, u32[]{:S(2)}, u32[]{:S(2)}) collective-permute-start(bf16[128,1024]{1,0:T(8,128)(2,1)} %get-tuple-element.147), channel_id=1, source_target_pairs={{0,2},{1,3},{2,0},{3,1},{4,6},{5,7},{6,4},{7,5},{8,10},{9,11},{10,... | collective-permute-start | bytes 786440 | tf_op jit(solution)/shard_map/ppermute | solution.py:360
  90.8 23.3 %collective-permute-start.11 = (bf16[3,4,64,512]{3,2,1,0:T(8,128)(2,1)}, bf16[3,4,64,512]{3,2,1,0:T(8,128)(2,1)S(1)}, u32[]{:S(2)}, u32[]{:S(2)}) collective-permute-start(bf16[3,4,64,512]{3,2,1,0:T(8,128)(2,1)} %collective-permute-done.7.x1_ref), channel_id=1, source_target_pairs={{0,4},{4,0},{8,12},{12,8},{16,20},{20,16},{24,28},{28,24},{1,5},{5... | collective-permute-start | bytes 2359304 | tf_op jit(solution)/shard_map/ppermute | solution.py:349
  92.2 21.9 %collective-permute-start.9 = (bf16[2,3,4,64,512]{4,3,2,1,0:T(8,128)(2,1)S(1)}, bf16[2,3,4,64,512]{4,3,2,1,0:T(8,128)(2,1)}, u32[]{:S(2)}, u32[]{:S(2)}) collective-permute-start(bf16[2,3,4,64,512]{4,3,2,1,0:T(8,128)(2,1)S(1)} %pad_maximum_fusion.5), channel_id=1, source_target_pairs={{0,16},{4,12},{8,24},{12,4},{16,0},{20,28},{24,8},{28,20},{1,17},{... | collective-permute-start | bytes 4718600 | tf_op jit(solution)/shard_map/ppermute | solution.py:354
  115.5 23.8 %collective-permute-start.17 = (bf16[128,1024]{1,0:T(8,128)(2,1)}, bf16[128,1024]{1,0:T(8,128)(2,1)}, u32[]{:S(2)}, u32[]{:S(2)}) collective-permute-start(bf16[128,1024]{1,0:T(8,128)(2,1)} %get-tuple-element.162), channel_id=1, source_target_pairs={{0,2},{1,3},{2,0},{3,1},{4,6},{5,7},{6,4},{7,5},{8,10},{9,11},{10,... | collective-permute-start | bytes 786440 | tf_op jit(solution)/shard_map/ppermute | solution.py:360
  115.6 23.7 %collective-permute-start.16 = (bf16[128,1024]{1,0:T(8,128)(2,1)}, bf16[128,1024]{1,0:T(8,128)(2,1)}, u32[]{:S(2)}, u32[]{:S(2)}) collective-permute-start(bf16[128,1024]{1,0:T(8,128)(2,1)} %get-tuple-element.162), channel_id=1, source_target_pairs={{0,1},{1,2},{2,3},{3,0},{4,5},{5,6},{6,7},{7,4},{8,9},{9,10},{10,1... | collective-permute-start | bytes 786440 | tf_op jit(solution)/shard_map/ppermute | solution.py:360
  139.3 23.3 %collective-permute-start.19 = (bf16[384,1024]{1,0:T(8,128)(2,1)}, bf16[384,1024]{1,0:T(8,128)(2,1)S(1)}, u32[]{:S(2)}, u32[]{:S(2)}) collective-permute-start(bf16[384,1024]{1,0:T(8,128)(2,1)} %pad_maximum_fusion.11), channel_id=1, source_target_pairs={{0,8},{4,20},{8,0},{12,28},{16,24},{20,4},{24,16},{28,12},{1,9},{5... | collective-permute-start | bytes 2359304 | tf_op jit(solution)/shard_map/ppermute | solution.py:354
  163.5 29.2 %collective-permute-start.20 = (bf16[768,1024]{1,0:T(8,128)(2,1)}, bf16[768,1024]{1,0:T(8,128)(2,1)}, u32[]{:S(2)}, u32[]{:S(2)}) collective-permute-start(bf16[768,1024]{1,0:T(8,128)(2,1)} %constant_dynamic-update-slice_fusion), channel_id=1, source_target_pairs={{0,16},{4,12},{8,24},{12,4},{16,0},{20,28},{24,8},{28,20},{1,17},{... | collective-permute-start | bytes 4718600 | tf_op jit(solution)/shard_map/ppermute | solution.py:354
  167.0 24.1 %collective-permute-start.21 = (bf16[384,1024]{1,0:T(8,128)(2,1)}, bf16[384,1024]{1,0:T(8,128)(2,1)}, u32[]{:S(2)}, u32[]{:S(2)}) collective-permute-start(bf16[384,1024]{1,0:T(8,128)(2,1)} %pad_maximum_fusion.12), channel_id=1, source_target_pairs={{0,8},{4,20},{8,0},{12,28},{16,24},{20,4},{24,16},{28,12},{1,9},{5... | collective-permute-start | bytes 2359304 | tf_op jit(solution)/shard_map/ppermute | solution.py:354
  170.8 45.0 %collective-permute-start.23 = (bf16[768,1024]{1,0:T(8,128)(2,1)}, bf16[768,1024]{1,0:T(8,128)(2,1)S(1)}, u32[]{:S(2)}, u32[]{:S(2)}) collective-permute-start(bf16[768,1024]{1,0:T(8,128)(2,1)} %constant_dynamic-update-slice_fusion), channel_id=1, source_target_pairs={{0,4},{4,0},{8,12},{12,8},{16,20},{20,16},{24,28},{28,24},{1,5},{5... | collective-permute-start | bytes 4718600 | tf_op jit(solution)/shard_map/ppermute | solution.py:349
  193.9 26.3 %collective-permute-start.24 = (bf16[768,1024]{1,0:T(8,128)(2,1)S(1)}, bf16[768,1024]{1,0:T(8,128)(2,1)S(1)}, u32[]{:S(2)}, u32[]{:S(2)}) collective-permute-start(bf16[768,1024]{1,0:T(8,128)(2,1)S(1)} %constant_dynamic-update-slice_fusion.2), channel_id=1, source_target_pairs={{0,4},{4,0},{8,12},{12,8},{16,20},{20,16},{24,28},{28,24},{1,5},{5... | collective-permute-start | bytes 4718600 | tf_op jit(solution)/shard_map/ppermute | solution.py:349
  193.9 30.5 %collective-permute-start.22 = (bf16[768,1024]{1,0:T(8,128)(2,1)S(1)}, bf16[768,1024]{1,0:T(8,128)(2,1)S(1)}, u32[]{:S(2)}, u32[]{:S(2)}) collective-permute-start(bf16[768,1024]{1,0:T(8,128)(2,1)S(1)} %constant_dynamic-update-slice_fusion.2), channel_id=1, source_target_pairs={{0,16},{4,12},{8,24},{12,4},{16,0},{20,28},{24,8},{28,20},{1,17},{... | collective-permute-start | bytes 4718600 | tf_op jit(solution)/shard_map/ppermute | solution.py:354
  218.4 31.6 %collective-permute-start.33 = (bf16[768,1024]{1,0:T(8,128)(2,1)S(1)}, bf16[768,1024]{1,0:T(8,128)(2,1)S(1)}, u32[]{:S(2)}, u32[]{:S(2)}) collective-permute-start(bf16[768,1024]{1,0:T(8,128)(2,1)S(1)} %convolution_convert_fusion.1), channel_id=1, source_target_pairs={{0,4},{4,0},{8,12},{12,8},{16,20},{20,16},{24,28},{28,24},{1,5},{5... | collective-permute-start | bytes 4718600 | tf_op jit(solution)/shard_map/ppermute | solution.py:349
  224.1 43.9 %collective-permute-start.35 = (bf16[768,1024]{1,0:T(8,128)(2,1)}, bf16[768,1024]{1,0:T(8,128)(2,1)}, u32[]{:S(2)}, u32[]{:S(2)}) collective-permute-start(bf16[768,1024]{1,0:T(8,128)(2,1)} %convolution_convert_fusion), channel_id=1, source_target_pairs={{0,4},{4,0},{8,12},{12,8},{16,20},{20,16},{24,28},{28,24},{1,5},{5... | collective-permute-start | bytes 4718600 | tf_op jit(solution)/shard_map/ppermute | solution.py:349
  238.2 26.9 %collective-permute-start.31 = (bf16[1024,1024]{1,0:T(8,128)(2,1)S(1)}, bf16[1024,1024]{1,0:T(8,128)(2,1)S(1)}, u32[]{:S(2)}, u32[]{:S(2)}) collective-permute-start(bf16[1024,1024]{1,0:T(8,128)(2,1)S(1)} %pad_maximum_fusion.2), channel_id=1, source_target_pairs={{0,16},{4,12},{8,24},{12,4},{16,0},{20,28},{24,8},{28,20},{1,17},{... | collective-permute-start | bytes 6291464 | tf_op jit(solution)/shard_map/ppermute | solution.py:354
  249.4 48.6 %collective-permute-start.32 = (bf16[1024,1024]{1,0:T(8,128)(2,1)}, bf16[1024,1024]{1,0:T(8,128)(2,1)S(1)}, u32[]{:S(2)}, u32[]{:S(2)}) collective-permute-start(bf16[1024,1024]{1,0:T(8,128)(2,1)} %pad_maximum_fusion.1), channel_id=1, source_target_pairs={{0,16},{4,12},{8,24},{12,4},{16,0},{20,28},{24,8},{28,20},{1,17},{... | collective-permute-start | bytes 6291464 | tf_op jit(solution)/shard_map/ppermute | solution.py:354
  266.0 26.1 %collective-permute-start.34 = (bf16[512,1024]{1,0:T(8,128)(2,1)S(1)}, bf16[512,1024]{1,0:T(8,128)(2,1)S(1)}, u32[]{:S(2)}, u32[]{:S(2)}) collective-permute-start(bf16[512,1024]{1,0:T(8,128)(2,1)S(1)} %pad_maximum_fusion.7), channel_id=1, source_target_pairs={{0,8},{4,20},{8,0},{12,28},{16,24},{20,4},{24,16},{28,12},{1,9},{5... | collective-permute-start | bytes 3145736 | tf_op jit(solution)/shard_map/ppermute | solution.py:354
  298.9 23.2 %collective-permute-start.36 = (bf16[512,1024]{1,0:T(8,128)(2,1)S(1)}, bf16[512,1024]{1,0:T(8,128)(2,1)S(1)}, u32[]{:S(2)}, u32[]{:S(2)}) collective-permute-start(bf16[512,1024]{1,0:T(8,128)(2,1)S(1)} %pad_maximum_fusion.8), channel_id=1, source_target_pairs={{0,8},{4,20},{8,0},{12,28},{16,24},{20,4},{24,16},{28,12},{1,9},{5... | collective-permute-start | bytes 3145736 | tf_op jit(solution)/shard_map/ppermute | solution.py:354
  336.6 29.1 %collective-permute-start.40 = (bf16[1024,512]{1,0:T(8,128)(2,1)S(1)}, bf16[1024,512]{1,0:T(8,128)(2,1)S(1)}, u32[]{:S(2)}, u32[]{:S(2)}) collective-permute-start(bf16[1024,512]{1,0:T(8,128)(2,1)S(1)} %convolution_convert_fusion.9), channel_id=1, source_target_pairs={{0,4},{4,0},{8,12},{12,8},{16,20},{20,16},{24,28},{28,24},{1,5},{5... | collective-permute-start | bytes 3145736 | tf_op jit(solution)/shard_map/ppermute | solution.py:349
  337.1 28.7 %collective-permute-start.41 = (bf16[1024,512]{1,0:T(8,128)(2,1)S(1)}, bf16[1024,512]{1,0:T(8,128)(2,1)S(1)}, u32[]{:S(2)}, u32[]{:S(2)}) collective-permute-start(bf16[1024,512]{1,0:T(8,128)(2,1)S(1)} %copy-done.101), channel_id=1, source_target_pairs={{0,4},{4,0},{8,12},{12,8},{16,20},{20,16},{24,28},{28,24},{1,5},{5... | collective-permute-start | bytes 3145736 | tf_op jit(solution)/shard_map/ppermute | solution.py:349
  337.2 28.6 %collective-permute-start.42 = (bf16[1024,512]{1,0:T(8,128)(2,1)S(1)}, bf16[1024,512]{1,0:T(8,128)(2,1)S(1)}, u32[]{:S(2)}, u32[]{:S(2)}) collective-permute-start(bf16[1024,512]{1,0:T(8,128)(2,1)S(1)} %convolution_convert_fusion.7), channel_id=1, source_target_pairs={{0,4},{4,0},{8,12},{12,8},{16,20},{20,16},{24,28},{28,24},{1,5},{5... | collective-permute-start | bytes 3145736 | tf_op jit(solution)/shard_map/ppermute | solution.py:349
  337.6 28.3 %collective-permute-start.43 = (bf16[1024,512]{1,0:T(8,128)(2,1)S(1)}, bf16[1024,512]{1,0:T(8,128)(2,1)S(1)}, u32[]{:S(2)}, u32[]{:S(2)}) collective-permute-start(bf16[1024,512]{1,0:T(8,128)(2,1)S(1)} %convolution_convert_fusion.6), channel_id=1, source_target_pairs={{0,4},{4,0},{8,12},{12,8},{16,20},{20,16},{24,28},{28,24},{1,5},{5... | collective-permute-start | bytes 3145736 | tf_op jit(solution)/shard_map/ppermute | solution.py:349
  390.6 51.3 %collective-permute-start.47 = (bf16[2,4,256,512]{3,2,1,0:T(8,128)(2,1)}, bf16[2,4,256,512]{3,2,1,0:T(8,128)(2,1)}, u32[]{:S(2)}, u32[]{:S(2)}) collective-permute-start(bf16[2,4,256,512]{3,2,1,0:T(8,128)(2,1)} %get-tuple-element.226), channel_id=1, source_target_pairs={{0,16},{4,12},{8,24},{12,4},{16,0},{20,28},{24,8},{28,20},{1,17},{... | collective-permute-start | bytes 6291464 | tf_op jit(solution)/shard_map/ppermute | solution.py:354
  394.5 47.3 %collective-permute-start.48 = (bf16[512,1024]{0,1:T(8,128)(2,1)}, bf16[512,1024]{0,1:T(8,128)(2,1)S(1)}, u32[]{:S(2)}, u32[]{:S(2)}) collective-permute-start(bf16[512,1024]{0,1:T(8,128)(2,1)} %slice.341), channel_id=1, source_target_pairs={{1,0},{2,1},{3,2},{5,4},{6,5},{7,6},{9,8},{10,9},{11,10},{13,12},{... | collective-permute-start | bytes 3145736 | tf_op jit(solution)/shard_map/ppermute | solution.py:360
  400.5 41.3 %collective-permute-start.49 = (bf16[256,1024]{0,1:T(8,128)(2,1)}, bf16[256,1024]{0,1:T(8,128)(2,1)}, u32[]{:S(2)}, u32[]{:S(2)}) collective-permute-start(bf16[256,1024]{0,1:T(8,128)(2,1)} %slice.342), channel_id=1, source_target_pairs={{2,0},{3,1},{6,4},{7,5},{10,8},{11,9},{14,12},{15,13},{18,16},{19,... | collective-permute-start | bytes 1572872 | tf_op jit(solution)/shard_map/ppermute | solution.py:360
  (144 other events, 1349.4 us)
Sparse Core Ops, SparseCore 0:
  368.8 42.6 all-gather.2

commit v4 on v3

--- a/solution.py
+++ b/solution.py
@@ -256,31 +256,43 @@
     )(at, fc1_weight, fc2_weight)
 
 
-def join_att_kernel(exchanged, own_ref, x0_ref, x1_ref, y_ref, *out_refs):
-    hops = (y_ref[0], x1_ref[...]) if exchanged else (x1_ref[...], y_ref[0])
+def join_att_kernel(core, *refs):
+    mine, other, out_refs = refs[:4], refs[4:8], refs[8:]
+    left_mine = core[0] == 0
+
+    def places(t, own_ref, x0_ref, x1_ref, y_ref, exchanged):
+        hops = (y_ref[0, :, t], x1_ref[:, t]) if exchanged else (x1_ref[:, t], y_ref[0, :, t])
+        return own_ref[t], (x0_ref[:, t], *hops, y_ref[1, :, t])
+
     for t, out_ref in enumerate(out_refs):
-        out_ref[:, 0] = own_ref[t]
-        for place, rest in enumerate((x0_ref[...], *hops, y_ref[1])):
-            out_ref[place, 1:] = rest[:, t]
-
-
-def join_att(own, x0, x1, y, exchanged=False):
-    rest, _, hd, half = x0.shape
+        own_a, rest_a = places(t, *mine, False)
+        own_b, rest_b = places(t, *other, True)
+        half = own_a.shape[-1]
+        out_ref[:, 0, :, :half] = jnp.where(left_mine, own_a, own_b)
+        out_ref[:, 0, :, half:] = jnp.where(left_mine, own_b, own_a)
+        for place, (a, b) in enumerate(zip(rest_a, rest_b)):
+            out_ref[place, 1:, :, :half] = jnp.where(left_mine, a, b)
+            out_ref[place, 1:, :, half:] = jnp.where(left_mine, b, a)
+
+
+def join_att(core, mine, other):
+    rest, _, hd, half = mine[1].shape
     step = hd // 4
     one = pl.BlockSpec((rest, 4, step, half), lambda i: (0, 0, i, 0))
+    side = [
+        pl.BlockSpec((4, 4, step, half), lambda i: (0, 0, i, 0)),
+        one,
+        one,
+        pl.BlockSpec((2, rest, 4, step, half), lambda i: (0, 0, 0, i, 0)),
+    ]
     return pl.pallas_call(
-        functools.partial(join_att_kernel, exchanged),
+        join_att_kernel,
         grid=(4,),
-        in_specs=[
-            pl.BlockSpec((4, 4, step, half), lambda i: (0, 0, i, 0)),
-            one,
-            one,
-            pl.BlockSpec((2, rest, 4, step, half), lambda i: (0, 0, 0, i, 0)),
-        ],
-        out_specs=[pl.BlockSpec((4, rest + 1, step, half), lambda i: (0, 0, i, 0))] * 4,
+        in_specs=[pl.BlockSpec(memory_space=pltpu.SMEM)] + side + side,
+        out_specs=[pl.BlockSpec((4, rest + 1, step, 2 * half), lambda i: (0, 0, i, 0))] * 4,
         cost_estimate=SMALL,
-        out_shape=[jax.ShapeDtypeStruct((4, rest + 1, hd, half), bf16)] * 4,
-    )(own, x0, x1, y)
+        out_shape=[jax.ShapeDtypeStruct((4, rest + 1, hd, 2 * half), bf16)] * 4,
+    )(core, *mine, *other)
 
 
 def add_att_kernel(*refs):
@@ -316,15 +328,20 @@
     )(*mine, *theirs)
 
 
-def last_att_kernel(at, left_ref, right_ref, out_ref, qkv_ref):
-    rows = jnp.concatenate([left_ref[0], right_ref[0]], axis=-1).astype(f32)
-    out_ref[...] = rows[1]
-    qkv_ref[0], qkv_ref[1], qkv_ref[2] = rows[0], rows[2], rows[3]
-
-
-def last_att(at, pieces):
+def last_att_kernel(at, mine_ref, other_ref, out_ref, qkv_ref):
+    mine, other = mine_ref[0].astype(f32), other_ref[0].astype(f32)
+    half = mine.shape[-1]
+    left, right = jnp.where(at[0] == 0, mine, other), jnp.where(at[0] == 0, other, mine)
+    out_ref[:, :half] = left[1]
+    out_ref[:, half:] = right[1]
+    for i, t in enumerate((0, 2, 3)):
+        qkv_ref[i, :, :half] = left[t]
+        qkv_ref[i, :, half:] = right[t]
+
+
+def last_att(at, pieces, others):
     _, _, hd, half = pieces.shape
-    block = lambda c: pl.BlockSpec((1, 4, hd, half), lambda p, at: (at[2 * p + c], 0, 0, 0))
+    block = lambda c: pl.BlockSpec((1, 4, hd, half), lambda p, at: (at[1 + 4 * c + p], 0, 0, 0))
     return pl.pallas_call(
         last_att_kernel,
         grid_spec=pltpu.PrefetchScalarGridSpec(
@@ -341,7 +358,7 @@
             jax.ShapeDtypeStruct((4 * hd, 2 * half), f32),
             jax.ShapeDtypeStruct((3, 4 * hd, 2 * half), f32),
         ],
-    )(at, pieces, pieces)
+    )(at, pieces, others)
 
 
 def swap(value, b):
@@ -446,8 +463,8 @@
     other = jnp.maximum(row - 8, 0)
     shifts = jnp.where(row < 8, 0, other % rest + 1)
     lies_at = slice_at(jnp.where(row < 8, row, other // rest))
-    ff_rows = (m + mp - shifts) % mp * 8 + lies_at
-    ff_from = shifts * 8 + lies_at
+    ff_rows = (m + shifts) % mp * 8 + lies_at
+    ff_from = (mp - shifts) % mp * 8 + lies_at
     head = jnp.arange(mp * heads_here)
     head_place = slice_at(head // mp) >> 1
     heads = (m + mp - head % mp) % mp * heads_here + head_place
@@ -463,13 +480,17 @@
     halo = DOC_MOST
     qv_own = jnp.transpose(qv_bias.reshape(2, heads_here, HD), (1, 0, 2))
     bias_own = jnp.concatenate([fc1_bias.reshape(8, piece), qv_own.reshape(heads_here, 2 * HD)])
-    bias_all = [bias_own] + [shift(bias_own, s) for s in range(1, mp)]
     qkv_t = jnp.transpose(qkv_weight, (1, 2, 0))
     att_places = jnp.concatenate([core[None], place])
     (att_me,) = own_att(1, att_places, qkv_t, out_weight)
     att_me = att_me.reshape(4, HD, half)
     att_z = [shift(att_me, s) for s in range(1, mp)]
-    halo1 = move(tokens, [(i, i + 1) for i in range(mp - 1)])
+    bias_own, _ = tie((bias_own, att_me))
+    bias_all = [bias_own] + [shift(bias_own, s) for s in range(1, mp)]
+    me1, me2 = me_ff(slices, fc1_weight, fc2_weight)
+    up = [(i, i + 1) for i in range(mp - 1)]
+    tokens_late, _ = tie((tokens, att_me))
+    halo1 = move(tokens_late[rows - near_rows :], up)
     fc1_b = pick(jnp.concatenate([v[:8] for v in bias_all]), ff_from).reshape(-1)
     qv_b = pick(jnp.concatenate([v[8:] for v in bias_all]), heads_from)
     q_bias, v_bias = qv_b[:, :HD].reshape(-1), qv_b[:, HD:].reshape(-1)
@@ -478,23 +499,25 @@
     segq = segk[:, halo:]
     segk = segk.reshape(halo + rows, 1)
 
-    small_ones = (fc1_b, q_bias, v_bias, segk, segq, slopes)
-    att_z, halo1, small_ones, slices, att_places = tie(
-        (att_z, halo1, small_ones, slices, att_places)
-    )
-    fc1_b, q_bias, v_bias, segk, segq, slopes = small_ones
-    halo2 = move(halo1[rows - near_rows :], [(i, i + 1) for i in range(mp - 1)])
+    fc1_b, slices, att_places = tie((fc1_b, slices, att_places))
+    own = own_att(2, att_places, qkv_t, out_weight)
+    own1, own2 = own_ff(slices, fc1_weight, fc2_weight)
+    small_ones = (fc1_b, q_bias, v_bias, segk, segq, slopes, own, own1, own2)
+    att_z, small_ones = tie((att_z, small_ones))
+    fc1_b, q_bias, v_bias, segk, segq, slopes, own, own1, own2 = small_ones
     att_x0 = jnp.stack(att_z)
     att_x1 = hop(att_x0, 1)
-    me1, me2 = me_ff(slices, fc1_weight, fc2_weight)
-    own = own_att(2, att_places, qkv_t, out_weight)
-    own1, own2 = own_ff(slices, fc1_weight, fc2_weight)
-    att_x1, halo2, me1, me2, own, own1, own2 = tie((att_x1, halo2, me1, me2, own, own1, own2))
-    z1 = [shift(me1, s) for s in range(1, mp)]
+    att_x1, halo1 = tie((att_x1, halo1))
+    halo2 = move(halo1, up)
+    halo3 = move(tokens_late[: rows - near_rows], up)
     part0 = swap(att_x0, 0)
     att_y = hop(jnp.stack([att_x0, att_x1]), 2)
     part1 = swap(att_x1, 0)
-    ext = jnp.concatenate([halo2, halo1, tokens], 0).astype(f32)
+    att_y, part0, part1, halo2, halo3, me1, me2 = tie(
+        (att_y, part0, part1, halo2, halo3, me1, me2)
+    )
+    z1 = [shift(me1, mp - s) for s in range(1, mp)]
+    ext = jnp.concatenate([halo2, halo3, halo1, tokens], 0).astype(f32)
     xhat_ext, rstd_ext = norm_parts(ext)
     norm1 = (xhat_ext * norm1_gain + norm1_shift).astype(bf16)
     col = [core * half, (1 - core) * half]
@@ -502,31 +525,22 @@
     def cols(value):
         return [lax.dynamic_slice_in_dim(value, at, half, 1) for at in col]
 
-    def join(own, other):
-        first = core == 0
-        return jnp.concatenate([jnp.where(first, own, other), jnp.where(first, other, own)], 1)
-
     n1 = cols(norm1)
-    att_y, part0, part1, z1, n1 = tie((att_y, part0, part1, z1, n1))
-    z2 = [shift(me2, s) for s in range(1, mp)]
     part_y = swap(att_y, 0)
-    w_att = [
-        join_att(own[0], att_x0, att_x1, att_y),
-        join_att(own[1], part0, part1, part_y, True),
-    ]
-    w_att = [[w.reshape(HEADS * HD, half) for w in four] for four in w_att]
-
-    def project(t, lhs):
-        return dot(lhs[0], w_att[0][t], 1, 1) + dot(lhs[1], w_att[1][t], 1, 1)
-
-    q = (project(0, [v[halo:] for v in n1]) + q_bias).astype(bf16)
-    k = project(2, n1).astype(bf16)
-    v = (project(3, n1) + v_bias).astype(bf16)
+    weights = join_att(
+        core[None], (own[0], att_x0, att_x1, att_y), (own[1], part0, part1, part_y)
+    )
+    w_q, w_o, w_k, w_v = [w.reshape(HEADS * HD, wide) for w in weights]
+
+    q = (dot(norm1[halo:], w_q, 1, 1) + q_bias).astype(bf16)
+    k = dot(norm1, w_k, 1, 1).astype(bf16)
+    v = (dot(norm1, w_v, 1, 1) + v_bias).astype(bf16)
 
     cut = rest * piece
 
+    q, z1, me2 = tie((q, z1, me2))
     x0_1 = jnp.concatenate(z1)
-    q, x0_1, z2 = tie((q, x0_1, z2))
+    z2 = [shift(me2, mp - s) for s in range(1, mp)]
     x1_1 = hop(x0_1, 1)
     first = attend(0, slopes, segq, segk, q, k, v)
     first, x1_1, z2 = tie((first, x1_1, z2))
@@ -540,7 +554,7 @@
     y2 = hop(z2, 2)
     w1 = [z1, y1, swap(z1, 0), swap(y1, 0)]
     w2 = [z2, y2, swap(z2, 0), swap(y2, 0)]
-    attention = join(dot(context, w_att[0][1], 1, 0), dot(context, w_att[1][1], 1, 0))
+    attention = dot(context, w_o, 1, 0)
     tokens_wide = tokens.astype(f32)
     resid = attention + out_bias + tokens_wide
     xhat2, rstd2 = norm_parts(resid)
@@ -574,17 +588,12 @@
         keep = [add(lo[0][:cut], got[:cut]), add(lo[1][:piece], got[2 * cut : 2 * cut + piece])]
         return send, keep
 
-    def to_mp(keep, got):
-        sent = [
-            shift(add(keep[0][at : at + piece], got[at : at + piece]), mp - 1 - at // piece)
-            for at in range(0, cut, piece)
-        ]
-        return sent, keep[1].astype(f32) + got[cut:].astype(f32)
-
-    def all_mp(sent, mine):
-        for got in sent:
-            mine = mine + got.astype(f32)
-        return beyond(mine).astype(bf16)
+    def along_mp(keep, got):
+        mine = add(keep[1], got[cut:])
+        others = add(keep[0], got[:cut])
+        blocks = jnp.concatenate([mine, others, mine, others])
+        blocks = lax.dynamic_slice_in_dim(blocks, (mp - m) * piece, mp * piece, 0)
+        return lax.psum_scatter(blocks, "mp", scatter_dimension=0, tiled=True)
 
     send2 = partials(hidden, out_grad)
     got2 = [swap(v, 0) for v in send2]
@@ -603,26 +612,24 @@
     out_grad_wide = out_grad.astype(f32)
     grad_resid = out_grad_wide + norm_back(grad_norm2, norm2_gain, xhat2, rstd2)
     hi1, lo1 = after_core(grad_pre, norm2, got1)
-    grad_att = cols(grad_resid.astype(bf16))
-    grad_context = (
-        dot(grad_att[0], w_att[0][1], 1, 1) + dot(grad_att[1], w_att[1][1], 1, 1)
-    ).astype(bf16)
+    grad_attention = grad_resid.astype(bf16)
+    grad_att = cols(grad_attention)
+    grad_context = dot(grad_attention, w_o, 1, 1).astype(bf16)
 
     grad_context, hi1, hi2 = tie((grad_context, hi1, hi2))
     hop2_1 = hop(hi1, 2)
     first = attend_back(0, slopes, segq, segk, q, k, v, grad_context, lse)
-    first, hop2_2 = tie((first, hop2_2))
+    first, hop2_2, result = tie((first, hop2_2, result))
     send2, keep2 = after_hop2(lo2, hop2_2)
     hop1_2 = hop(send2, 1)
     second = attend_back(1, slopes, segq, segk, q, k, v, grad_context, lse, first)
     second, hop2_1, hop1_2 = tie((second, hop2_1, hop1_2))
     send1, keep1 = after_hop2(lo1, hop2_1)
     hop1_1 = hop(send1, 1)
-    z2, mine2 = to_mp(keep2, hop1_2)
+    sum2 = all_eight(beyond(along_mp(keep2, hop1_2)))
     grads = attend_back(2, slopes, segq, segk, q, k, v, grad_context, lse, second)
-    (dq, dk, dv), hop1_1, z2 = tie((grads, hop1_1, z2))
-    z1, mine1 = to_mp(keep1, hop1_1)
-    sum2 = all_mp(z2, mine2)
+    (dq, dk, dv), hop1_1 = tie((grads, hop1_1))
+    sum1 = along_mp(keep1, hop1_1)
 
     def weights_half(i):
         return [
@@ -632,33 +639,27 @@
             dot(dv, n1[i], 0, 0).astype(bf16),
         ]
 
-    def back_half(i):
-        tail = dot(dk, w_att[i][2], 1, 0) + dot(dv, w_att[i][3], 1, 0)
-        return tail[:halo], tail[halo:] + dot(dq, w_att[i][0], 1, 0)
-
+    grad_ext = dot(dk, w_k, 1, 0) + dot(dv, w_v, 1, 0)
+    grad_halo = grad_ext[:halo].astype(bf16)
+    grad_halo, dk, dv, dq = tie((grad_halo, dk, dv, dq))
+    passed = move(grad_halo[:near_rows], [(i, i - 2) for i in range(2, mp)])
     theirs = weights_half(1)
-    theirs, dk = tie((theirs, dk))
+    theirs, dk, dv, dq = tie((theirs, dk, dv, dq))
     theirs = [swap(v, 0) for v in theirs]
-    back = [back_half(0), back_half(1)]
-    grad_halo = join(back[0][0], back[1][0]).astype(bf16)
-    grad_halo, dv, theirs, z1 = tie((grad_halo, dv, theirs, z1))
-    ff_sums = all_eight(jnp.stack([all_mp(z1, mine1), sum2]))
-    near = move(grad_halo[near_rows:], [(i, i - 1) for i in range(1, mp)])
-    passed = move(grad_halo[:near_rows], [(i, i - 2) for i in range(2, mp)])
     mine = weights_half(0)
     att_hi, att_lo = add_att(mine, theirs)
+    att_hi, passed, grad_halo, grad_ext, dq_late = tie((att_hi, passed, grad_halo, grad_ext, dq))
     att_got = hop(att_hi, 2)
-    grad_norm1 = join(back[0][1], back[1][1])
-    att_got, near, passed, grad_norm1 = tie((att_got, near, passed, grad_norm1))
+    near = move(grad_halo[near_rows:], [(i, i - 1) for i in range(1, mp)])
+    grad_norm1 = grad_ext[halo:] + dot(dq_late, w_q, 1, 0)
+    att_got, grad_norm1, sum1 = tie((att_got, grad_norm1, sum1))
+    sum1 = all_eight(beyond(sum1))
     att_hop1 = hop(add(att_lo[1], att_got[1]), 1)
     att_keep = add(att_lo[0], att_got[0])
-    grad_fc1 = ff_sums[:, 0].reshape(ff_here, wide).T.astype(f32)
-    grad_fc2 = ff_sums[:, 1].reshape(ff_here, wide).astype(f32)
     near = jnp.pad(passed.astype(f32), ((rows - near_rows, 0), (0, 0))) + near.astype(f32)
     grad_norm1 = grad_norm1 + near
     xhat1, rstd1 = xhat_ext[halo:], rstd_ext[halo:]
     in_grad = grad_resid + norm_back(grad_norm1, norm1_gain, xhat1, rstd1)
-    att_hop1, in_grad = tie((att_hop1, in_grad))
     att_keep = add(att_keep, att_hop1).reshape(4, mp, HD, half)
     att_z = [shift(att_keep[:, s], mp - s) for s in range(1, mp)]
     ff_bias = jnp.concatenate([jnp.sum(g.astype(f32), axis=0) for g in grad_pre])
@@ -691,20 +692,25 @@
         ],
         1,
     )
+    grad_fc1 = sum1.reshape(ff_here, wide).T.astype(f32)
+    grad_fc2 = sum2.reshape(ff_here, wide).astype(f32)
+
+    att_z, vectors, grad_fc2, in_grad = tie((att_z, vectors, grad_fc2, in_grad))
     for bit in range(lax.axis_size("dp").bit_length() - 1):
         vectors = vectors + swap(vectors, bit)
-    att_z, vectors, grad_fc1, grad_fc2 = tie((att_z, vectors, grad_fc1, grad_fc2))
     att_sum = att_keep[:, 0].astype(f32)
     for got in att_z:
         att_sum = att_sum + got.astype(f32)
     att_sum = beyond(att_sum).astype(bf16)
     att_sum = jnp.stack([att_sum, hop(att_sum, 2)])
-    att_sum = jnp.stack([att_sum, hop(att_sum, 1)])
+    att_sum, grad_fc1 = tie((jnp.stack([att_sum, hop(att_sum, 1)]), grad_fc1))
     att_sum = att_sum.reshape(4, 4, HD, half)
-    att_sum = jnp.stack([att_sum, swap(att_sum, 0)]).reshape(8, 4, HD, half)
-    from_slice = slice_at((row[:8] & 4) + ((row[:8] & 1) << 1) + ((row[:8] >> 1) & 1))
-    at = jnp.sum(jnp.where(from_slice[None] == row[:8, None], row[None, :8], 0), axis=1)
-    grad_out, grad_qkv = last_att(at, att_sum)
+    number = row[:4]
+    order = jnp.stack([number * 0, number * 0 + 1])
+    lies = (slice_at(4 * order + ((number & 1) << 1) + (number >> 1))) >> 1
+    at = jnp.sum(jnp.where(lies[:, None] == number[:, None], number[None, None], 0), axis=2)
+    at = jnp.concatenate([core[None], at.reshape(-1)])
+    grad_out, grad_qkv = last_att(at, att_sum, swap(att_sum, 0))
     grad_qkv = jnp.transpose(grad_qkv, (2, 0, 1))
     for bit in range(mp.bit_length() - 1):
         vectors = vectors + move(vectors, [(i, i ^ (1 << bit)) for i in range(mp)])

time: 541 us -> 504 us (0.932)
  waiting for transfers between devices: 141 us -> 123 us
  local copies, waits for them, and re-layouts: 48.7 us -> 31.1 us
  other arithmetic: 51.2 us -> 64.2 us
  starting transfers between devices: 80.8 us -> 69.2 us
    ppermute x27 -> x22, waiting for transfers between devices: 107 us -> 62.6 us  [move(): return lax.ppermute(value, 'mp', pairs)]
    ppermute x14, waiting for transfers between devices: 21.2 us -> 52.1 us  [hop(): lax.ppermute(value, 'dp', [(i, i ^ (2 if i & 1 == stage - 1 else 4)) for...]
    ppermute x27 -> x22, starting transfers between devices: 58 us -> 46.1 us  [move(): return lax.ppermute(value, 'mp', pairs)]
    convert_element_type x8 -> x10, other arithmetic: 6.47 us -> 15.6 us  [add(): return (a.astype(f32) + b.astype(f32)).astype(bf16)]
    convert_element_type x3 -> x4, other arithmetic: 5.36 us -> 13.6 us  [the longest x1 4.92 us: body(): norm1 = (xhat_ext * norm1_gain + norm1_shift).astype(bf16)]
    another operation x7 -> x2, other arithmetic: 6.52 us -> 0.17 us  [body(): att_sum, grad_fc1 = tie((jnp.stack([att_sum, hop(att_sum, 1)]), grad_fc1))]
    ppermute x21, waiting for transfers between devices: 13.7 us -> 8.16 us  [swap(): return lax.ppermute(value, 'dp', [(i, i ^ 1 << b) for i in range(n)])]
    unnamed x243 -> x156, local copies, waits for them, and re-layouts: 30.3 us -> 25.1 us
  transfers between devices with their start and end apart: 63 -> 61, of which waited for: 16 -> 20; matrix products, arithmetic and copies ran while one was open for 30% -> 33% of each run, Pallas kernels for 18% -> 19%
where the time goes in v4:
time: 504 us; the launch traced here: 496 us
  waiting for transfers between devices  123 us (24%)
  Pallas kernels  99.3 us (20%)
  matrix products  93.5 us (19%)
  starting transfers between devices  69.2 us (14%)
  other arithmetic  64.2 us (13%)
  local copies, waits for them, and re-layouts  31.1 us (6%)
  between operations  15.7 us (3%)
    dot_general x50, matrix products, dot(): lax.dot_general(a, b, (((ca,), (cb,)), ((), ())), preferred_element_type=...  92.8 us
    ppermute x22, waiting for transfers between devices, move(): return lax.ppermute(value, 'mp', pairs)  62.6 us
    ppermute x14, waiting for transfers between devices, hop(): lax.ppermute(value, 'dp', [(i, i ^ (2 if i & 1 == stage - 1 else 4)) for...  52.1 us
    ppermute x22, starting transfers between devices, move(): return lax.ppermute(value, 'mp', pairs)  46.1 us
    pallas_call x3, Pallas kernels, attend_back(): pl.pallas_call(functools.partial(attend_back_kernel, halo, start), grid=(...  37.1 us
    pallas_call x2, Pallas kernels, attend(): pl.pallas_call(functools.partial(attend_kernel, halo, start), grid=(pairs...  27.1 us
    unnamed x156, local copies, waits for them, and re-layouts  25.1 us
    ppermute x14, starting transfers between devices, hop(): lax.ppermute(value, 'dp', [(i, i ^ (2 if i & 1 == stage - 1 else 4)) for...  16.4 us
  transfers between devices with their start and end apart: 61, of which 20 were waited for; matrix products, arithmetic and copies ran while one was open for 33% of the time, Pallas kernels for 19%

profile of v4, /device:TPU:0, one launch (start us, length us, event | category | flops | bytes accessed | tf_op | source)
XLA Modules:
  0.0 496.1 jit_solution(15006900009105951893)
XLA Ops:
  25.5 4.4 shard_map.255
  29.9 7.3 %shard_map.256 = (bf16[1024,1024]{1,0:T(8,128)(2,1)}, bf16[1024,1024]{1,0:T(8,128)(2,1)}) custom-call(s32[8]{0:T(128)} %add_xor_fusion.at, bf16[1024,1024]{1,0:T(8,128)(2,1)} %fc1_ref.3, bf16[1024,1024]{1,0:T(8,128)(2,1)} %fc2_ref.3), custom_call_target="tpu_custom_call" | custom-call | flops 1 | bytes 1 | tf_op jit(solution)/shard_map/pallas_call | solution.py:237
  44.0 7.5 %collective-permute-start.7 = (bf16[256,1024]{1,0:T(8,128)(2,1)S(1)}, bf16[256,1024]{1,0:T(8,128)(2,1)S(1)}, u32[]{:S(2)}, u32[]{:S(2)}) collective-permute-start(bf16[256,1024]{1,0:T(8,128)(2,1)S(1)} %get-tuple-element.312), channel_id=1, source_target_pairs={{0,1},{1,2},{2,3},{4,5},{5,6},{6,7},{8,9},{9,10},{10,11},{12,13},{... | collective-permute-start | bytes 1572872 | tf_op jit(solution)/shard_map/ppermute | solution.py:377
  51.5 10.6 %collective-permute-done.7 = bf16[256,1024]{1,0:T(8,128)(2,1)S(1)} collective-permute-done((bf16[256,1024]{1,0:T(8,128)(2,1)S(1)}, bf16[256,1024]{1,0:T(8,128)(2,1)S(1)}, u32[]{:S(2)}, u32[]{:S(2)}) %collective-permute-start.7) | collective-permute-done | bytes 524320 | tf_op jit(solution)/shard_map/ppermute | solution.py:377
  65.5 4.4 collective-permute-start.12
  74.9 7.6 %collective-permute-done.12 = bf16[256,1024]{1,0:T(8,128)(2,1)S(1)} collective-permute-done((bf16[256,1024]{1,0:T(8,128)(2,1)}, bf16[256,1024]{1,0:T(8,128)(2,1)S(1)}, u32[]{:S(2)}, u32[]{:S(2)}) %collective-permute-start.12) | collective-permute-done | bytes 524320 | tf_op jit(solution)/shard_map/ppermute | solution.py:377
  82.5 10.2 %collective-permute-done.11 = bf16[256,1024]{1,0:T(8,128)(2,1)S(1)} collective-permute-done((bf16[256,1024]{1,0:T(8,128)(2,1)S(1)}, bf16[256,1024]{1,0:T(8,128)(2,1)S(1)}, u32[]{:S(2)}, u32[]{:S(2)}) %collective-permute-start.11) | collective-permute-done | bytes 524320 | tf_op jit(solution)/shard_map/ppermute | solution.py:377
  100.7 4.9 add_convert_fusion.1
  105.6 7.1 %shard_map.258 = (bf16[4,4,64,1024]{3,2,1,0:T(8,128)(2,1)}, bf16[4,4,64,1024]{3,2,1,0:T(8,128)(2,1)}, bf16[4,4,64,1024]{3,2,1,0:T(8,128)(2,1)}, bf16[4,4,64,1024]{3,2,1,0:T(8,128)(2,1)}) custom-call(s32[1]{0:T(128)} %bitcast.core, bf16[4,4,64,512]{3,2,1,0:T(8,128)(2,1)} %get-tuple-element.146.refs_0_, bf16[3,4,64,512]{3,2,1,0:T(8,128)(2,1)} %get-tuple-element.314.refs_1_, ...), custom_call_target="tpu_custom_call" | custom-call | flops 1 | bytes 1 | tf_op jit(solution)/shard_map/pallas_call | solution.py:288
  133.0 13.3 %shard_map.259 = (bf16[512,1024]{1,0:T(8,128)(2,1)S(1)}, f32[8,2,512]{2,1,0:T(2,128)S(1)}) custom-call(f32[16]{0:T(128)S(1)} %get-tuple-element.133.slopes, s32[1,512]{1,0:T(1,128)S(1)} %pad_dynamic-slice_fusion.8.segq, s32[1280,1]{1,0:T(8,128)S(1)} %copy.75.segk, bf16[512,1024]{1,0:T(8,128)(2,1)S(1)} %add_convert_fusion.10.q_ref, ...), custom_call_target="tpu_custom_call" | custom-call | flops 1 | bytes 1 | tf_op jit(solution)/shard_map/pallas_call | solution.py:114
  150.6 13.8 %shard_map.260 = (bf16[512,1024]{1,0:T(8,128)(2,1)S(1)}, f32[8,2,512]{2,1,0:T(2,128)S(1)}) custom-call(f32[16]{0:T(128)S(1)} %get-tuple-element.133.slopes, s32[1,512]{1,0:T(1,128)S(1)} %pad_dynamic-slice_fusion.8.segq, s32[1280,1]{1,0:T(8,128)S(1)} %copy.75.segk, ...), custom_call_target="tpu_custom_call", output_to_operand_aliasing={{0}: (6, {}), {1}: (7, {})} | custom-call | flops 1 | bytes 1 | tf_op jit(solution)/shard_map/pallas_call | solution.py:114
  164.5 6.0 %collective-permute-done.22 = bf16[384,1024]{1,0:T(8,128)(2,1)S(1)} collective-permute-done((bf16[384,1024]{1,0:T(8,128)(2,1)S(1)}, bf16[384,1024]{1,0:T(8,128)(2,1)S(1)}, u32[]{:S(2)}, u32[]{:S(2)}) %collective-permute-start.22) | collective-permute-done | bytes 786464 | tf_op jit(solution)/shard_map/ppermute | solution.py:371
  170.5 6.1 %collective-permute-done.21 = bf16[768,1024]{1,0:T(8,128)(2,1)S(1)} collective-permute-done((bf16[768,1024]{1,0:T(8,128)(2,1)S(1)}, bf16[768,1024]{1,0:T(8,128)(2,1)S(1)}, u32[]{:S(2)}, u32[]{:S(2)}) %collective-permute-start.21) | collective-permute-done | bytes 1572896 | tf_op jit(solution)/shard_map/ppermute | solution.py:371
  237.6 13.5 %shard_map.261 = (bf16[512,1024]{1,0:T(8,128)(2,1)S(1)}, bf16[1280,1024]{1,0:T(8,128)(2,1)}, bf16[1280,1024]{1,0:T(8,128)(2,1)}) custom-call(f32[16]{0:T(128)S(1)} %get-tuple-element.133.slopes, s32[1,512]{1,0:T(1,128)S(1)} %pad_dynamic-slice_fusion.8.segq, s32[1280,1]{1,0:T(8,128)S(1)} %copy.75.segk, bf16[512,1024]{1,0:T(8,128)(2,1)S(1)} %add_convert_fusion.10.q_ref, ...), custom_call_target="tpu_custom_call" | custom-call | flops 1 | bytes 1 | tf_op jit(solution)/shard_map/pallas_call | solution.py:146
  262.8 13.8 %shard_map.262 = (bf16[512,1024]{1,0:T(8,128)(2,1)S(1)}, bf16[1280,1024]{1,0:T(8,128)(2,1)}, bf16[1280,1024]{1,0:T(8,128)(2,1)}) custom-call(f32[16]{0:T(128)S(1)} %get-tuple-element.133.slopes, s32[1,512]{1,0:T(1,128)S(1)} %pad_dynamic-slice_fusion.8.segq, s32[1280,1]{1,0:T(8,128)S(1)} %copy.75.segk, ...), custom_call_target="tpu_custom_call", output_to_operand_aliasing={{0}: (8, {}), {1}: (9, {}), {2}: (10, {})} | custom-call | flops 1 | bytes 1 | tf_op jit(solution)/shard_map/pallas_call | solution.py:146
  294.8 9.8 %shard_map.263 = (bf16[512,1024]{1,0:T(8,128)(2,1)S(1)}, bf16[1280,1024]{1,0:T(8,128)(2,1)}, bf16[1280,1024]{1,0:T(8,128)(2,1)}) custom-call(f32[16]{0:T(128)S(1)} %get-tuple-element.133.slopes, s32[1,512]{1,0:T(1,128)S(1)} %pad_dynamic-slice_fusion.8.segq, s32[1280,1]{1,0:T(8,128)S(1)} %copy.75.segk, ...), custom_call_target="tpu_custom_call", output_to_operand_aliasing={{0}: (8, {}), {1}: (9, {}), {2}: (10, {})} | custom-call | flops 1 | bytes 1 | tf_op jit(solution)/shard_map/pallas_call | solution.py:146
  313.7 4.6 fusion.149
  341.8 6.5 %shard_map.264 = (bf16[2,4,256,512]{3,2,1,0:T(8,128)(2,1)}, bf16[2,4,256,512]{3,2,1,0:T(8,128)(2,1)}) custom-call(bf16[1024,512]{1,0:T(8,128)(2,1)} %convolution_convert_fusion.11.refs_0_, bf16[1024,512]{1,0:T(8,128)(2,1)} %convolution_convert_fusion.10.refs_1_, bf16[1024,512]{1,0:T(8,128)(2,1)} %convolution_convert_fusion.6.refs_2_, ...), custom_call_target="tpu_custom_call" | custom-call | flops 1 | bytes 1 | tf_op jit(solution)/shard_map/pallas_call | solution.py:318
  348.3 13.6 %collective-permute-done.42 = bf16[256,1024]{1,0:T(8,128)(2,1)} collective-permute-done((bf16[256,1024]{1,0:T(8,128)(2,1)S(1)}, bf16[256,1024]{1,0:T(8,128)(2,1)}, u32[]{:S(2)}, u32[]{:S(2)}) %collective-permute-start.42) | collective-permute-done | bytes 524320 | tf_op jit(solution)/shard_map/ppermute | solution.py:377
  369.4 5.0 %slice_add_fusion = f32[512,1024]{1,0:T(8,128)} fusion(f32[1280,1024]{1,0:T(8,128)} %copy-done.39, bf16[512,1024]{1,0:T(8,128)(2,1)S(1)} %copy-done.9, bf16[1024,1024]{1,0:T(8,128)(2,1)} %bitcast.199), kind=kOutput, calls=%fused_computation.58 | convolution fusion | flops 1074266112 | bytes 7340032 | tf_op jit(solution)/shard_map/dot_general | solution.py:22
  374.4 18.9 %collective-permute-done.43 = bf16[2,4,256,512]{3,2,1,0:T(8,128)(2,1)} collective-permute-done((bf16[2,4,256,512]{3,2,1,0:T(8,128)(2,1)}, bf16[2,4,256,512]{3,2,1,0:T(8,128)(2,1)}, u32[]{:S(2)}, u32[]{:S(2)}) %collective-permute-start.43) | collective-permute-done | bytes 2097184 | tf_op jit(solution)/shard_map/ppermute | solution.py:371
  397.5 4.5 multiply_reduce_fusion
  402.1 4.2 multiply_add_fusion.5
  406.3 12.0 %collective-permute-done.44 = bf16[4,256,512]{2,1,0:T(8,128)(2,1)S(1)} collective-permute-done((bf16[4,256,512]{2,1,0:T(8,128)(2,1)}, bf16[4,256,512]{2,1,0:T(8,128)(2,1)S(1)}, u32[]{:S(2)}, u32[]{:S(2)}) %collective-permute-start.44) | collective-permute-done | bytes 1048608 | tf_op jit(solution)/shard_map/ppermute | solution.py:371
  422.2 4.1 convert_element_type.490
  429.3 7.7 %collective-permute-done.46 = bf16[4,64,512]{2,1,0:T(8,128)(2,1)S(1)} collective-permute-done((bf16[4,64,512]{2,1,0:T(8,128)(2,1)S(1)}, bf16[4,64,512]{2,1,0:T(8,128)(2,1)S(1)}, u32[]{:S(2)}, u32[]{:S(2)}) %collective-permute-start.46) | collective-permute-done | bytes 262176 | tf_op jit(solution)/shard_map/ppermute | solution.py:377
  438.8 4.8 collective-permute-done.54
  447.1 6.9 %collective-permute-done.50 = f32[4,3072]{1,0:T(4,128)S(1)} collective-permute-done((f32[4,3072]{1,0:T(4,128)S(1)}, f32[4,3072]{1,0:T(4,128)S(1)}, u32[]{:S(2)}, u32[]{:S(2)}) %collective-permute-start.50) | collective-permute-done | bytes 49184 | tf_op jit(solution)/shard_map/ppermute | solution.py:366
  455.8 4.4 convert_bitcast_fusion
  460.3 4.0 collective-permute-start.52
  474.4 5.3 %copy.84 = f32[1024,1024]{1,0:T(8,128)} copy(f32[1024,1024]{0,1:T(8,128)} %convert_bitcast_fusion) | data formatting | bytes 8388608
  480.8 4.8 shard_map.265
  (418 shorter events, 228.9 us)
Async XLA Ops:
  7.2 320.7 %reduce-scatter.5.cloned.1.call-start = ((), (), s32[]{:S(2)}) async-start(), calls=%async_computation.3 | async-start | bytes 1310720 | tf_op jit(solution)/shard_map/reduce_scatter | solution.py:596
  20.7 19.9 %collective-permute-start.1 = (bf16[4,64,512]{2,1,0:T(8,128)(2,1)}, bf16[4,64,512]{2,1,0:T(8,128)(2,1)S(1)}, u32[]{:S(2)}, u32[]{:S(2)}) collective-permute-start(bf16[4,64,512]{2,1,0:T(8,128)(2,1)} %bitcast.174), channel_id=1, source_target_pairs={{0,2},{1,3},{2,0},{3,1},{4,6},{5,7},{6,4},{7,5},{8,10},{9,11},{10,... | collective-permute-start | bytes 786440 | tf_op jit(solution)/shard_map/ppermute | solution.py:377
  22.2 18.4 %collective-permute-start.2 = (bf16[4,64,512]{2,1,0:T(8,128)(2,1)}, bf16[4,64,512]{2,1,0:T(8,128)(2,1)S(1)}, u32[]{:S(2)}, u32[]{:S(2)}) collective-permute-start(bf16[4,64,512]{2,1,0:T(8,128)(2,1)} %bitcast.175), channel_id=1, source_target_pairs={{0,3},{1,0},{2,1},{3,2},{4,7},{5,4},{6,5},{7,6},{8,11},{9,8},{10,9... | collective-permute-start | bytes 786440 | tf_op jit(solution)/shard_map/ppermute | solution.py:377
  41.6 20.4 %collective-permute-start.6 = (bf16[3,4,64,512]{3,2,1,0:T(8,128)(2,1)}, bf16[3,4,64,512]{3,2,1,0:T(8,128)(2,1)}, u32[]{:S(2)}, u32[]{:S(2)}) collective-permute-start(bf16[3,4,64,512]{3,2,1,0:T(8,128)(2,1)} %get-tuple-element.314.refs_1_), channel_id=1, source_target_pairs={{0,8},{4,20},{8,0},{12,28},{16,24},{20,4},{24,16},{28,12},{1,9},{5... | collective-permute-start | bytes 2359304 | tf_op jit(solution)/shard_map/ppermute | solution.py:371
  44.0 18.1 %collective-permute-start.7 = (bf16[256,1024]{1,0:T(8,128)(2,1)S(1)}, bf16[256,1024]{1,0:T(8,128)(2,1)S(1)}, u32[]{:S(2)}, u32[]{:S(2)}) collective-permute-start(bf16[256,1024]{1,0:T(8,128)(2,1)S(1)} %get-tuple-element.312), channel_id=1, source_target_pairs={{0,1},{1,2},{2,3},{4,5},{5,6},{6,7},{8,9},{9,10},{10,11},{12,13},{... | collective-permute-start | bytes 1572872 | tf_op jit(solution)/shard_map/ppermute | solution.py:377
  64.5 28.2 %collective-permute-start.8 = (bf16[2,3,4,64,512]{4,3,2,1,0:T(8,128)(2,1)}, bf16[2,3,4,64,512]{4,3,2,1,0:T(8,128)(2,1)}, u32[]{:S(2)}, u32[]{:S(2)}) collective-permute-start(bf16[2,3,4,64,512]{4,3,2,1,0:T(8,128)(2,1)} %pad_maximum_fusion.3), channel_id=1, source_target_pairs={{0,16},{4,12},{8,24},{12,4},{16,0},{20,28},{24,8},{28,20},{1,17},{... | collective-permute-start | bytes 4718600 | tf_op jit(solution)/shard_map/ppermute | solution.py:371
  65.1 27.7 %collective-permute-start.10 = (bf16[3,4,64,512]{3,2,1,0:T(8,128)(2,1)}, bf16[3,4,64,512]{3,2,1,0:T(8,128)(2,1)}, u32[]{:S(2)}, u32[]{:S(2)}) collective-permute-start(bf16[3,4,64,512]{3,2,1,0:T(8,128)(2,1)} %collective-permute-done.6.refs_2_), channel_id=1, source_target_pairs={{0,4},{4,0},{8,12},{12,8},{16,20},{20,16},{24,28},{28,24},{1,5},{5... | collective-permute-start | bytes 2359304 | tf_op jit(solution)/shard_map/ppermute | solution.py:366
  69.9 22.8 %collective-permute-start.11 = (bf16[256,1024]{1,0:T(8,128)(2,1)S(1)}, bf16[256,1024]{1,0:T(8,128)(2,1)S(1)}, u32[]{:S(2)}, u32[]{:S(2)}) collective-permute-start(bf16[256,1024]{1,0:T(8,128)(2,1)S(1)} %collective-permute-done.7), channel_id=1, source_target_pairs={{0,1},{1,2},{2,3},{4,5},{5,6},{6,7},{8,9},{9,10},{10,11},{12,13},{... | collective-permute-start | bytes 1572872 | tf_op jit(solution)/shard_map/ppermute | solution.py:377
  92.7 23.4 %collective-permute-start.14 = (bf16[128,1024]{1,0:T(8,128)(2,1)}, bf16[128,1024]{1,0:T(8,128)(2,1)}, u32[]{:S(2)}, u32[]{:S(2)}) collective-permute-start(bf16[128,1024]{1,0:T(8,128)(2,1)} %get-tuple-element.153), channel_id=1, source_target_pairs={{0,3},{1,0},{2,1},{3,2},{4,7},{5,4},{6,5},{7,6},{8,11},{9,8},{10,9... | collective-permute-start | bytes 786440 | tf_op jit(solution)/shard_map/ppermute | solution.py:377
  95.0 24.3 %collective-permute-start.15 = (bf16[128,1024]{1,0:T(8,128)(2,1)}, bf16[128,1024]{1,0:T(8,128)(2,1)}, u32[]{:S(2)}, u32[]{:S(2)}) collective-permute-start(bf16[128,1024]{1,0:T(8,128)(2,1)} %get-tuple-element.153), channel_id=1, source_target_pairs={{0,2},{1,3},{2,0},{3,1},{4,6},{5,7},{6,4},{7,5},{8,10},{9,11},{10,... | collective-permute-start | bytes 786440 | tf_op jit(solution)/shard_map/ppermute | solution.py:377
  96.7 22.6 %collective-permute-start.16 = (bf16[128,1024]{1,0:T(8,128)(2,1)}, bf16[128,1024]{1,0:T(8,128)(2,1)}, u32[]{:S(2)}, u32[]{:S(2)}) collective-permute-start(bf16[128,1024]{1,0:T(8,128)(2,1)} %get-tuple-element.153), channel_id=1, source_target_pairs={{0,1},{1,2},{2,3},{3,0},{4,5},{5,6},{6,7},{7,4},{8,9},{9,10},{10,1... | collective-permute-start | bytes 786440 | tf_op jit(solution)/shard_map/ppermute | solution.py:377
  119.3 28.9 %collective-permute-start.18 = (bf16[128,1024]{1,0:T(8,128)(2,1)S(1)}, bf16[128,1024]{1,0:T(8,128)(2,1)S(1)}, u32[]{:S(2)}, u32[]{:S(2)}) collective-permute-start(bf16[128,1024]{1,0:T(8,128)(2,1)S(1)} %copy-done.63), channel_id=1, source_target_pairs={{0,3},{1,0},{2,1},{3,2},{4,7},{5,4},{6,5},{7,6},{8,11},{9,8},{10,9... | collective-permute-start | bytes 786440 | tf_op jit(solution)/shard_map/ppermute | solution.py:377
  119.5 28.8 %collective-permute-start.19 = (bf16[128,1024]{1,0:T(8,128)(2,1)S(1)}, bf16[128,1024]{1,0:T(8,128)(2,1)S(1)}, u32[]{:S(2)}, u32[]{:S(2)}) collective-permute-start(bf16[128,1024]{1,0:T(8,128)(2,1)S(1)} %copy-done.63), channel_id=1, source_target_pairs={{0,2},{1,3},{2,0},{3,1},{4,6},{5,7},{6,4},{7,5},{8,10},{9,11},{10,... | collective-permute-start | bytes 786440 | tf_op jit(solution)/shard_map/ppermute | solution.py:377
  121.1 27.2 %collective-permute-start.20 = (bf16[128,1024]{1,0:T(8,128)(2,1)S(1)}, bf16[128,1024]{1,0:T(8,128)(2,1)S(1)}, u32[]{:S(2)}, u32[]{:S(2)}) collective-permute-start(bf16[128,1024]{1,0:T(8,128)(2,1)S(1)} %copy-done.63), channel_id=1, source_target_pairs={{0,1},{1,2},{2,3},{3,0},{4,5},{5,6},{6,7},{7,4},{8,9},{9,10},{10,1... | collective-permute-start | bytes 786440 | tf_op jit(solution)/shard_map/ppermute | solution.py:377
  124.5 23.8 %collective-permute-start.17 = (bf16[384,1024]{1,0:T(8,128)(2,1)S(1)}, bf16[384,1024]{1,0:T(8,128)(2,1)S(1)}, u32[]{:S(2)}, u32[]{:S(2)}) collective-permute-start(bf16[384,1024]{1,0:T(8,128)(2,1)S(1)} %pad_maximum_fusion.8), channel_id=1, source_target_pairs={{0,8},{4,20},{8,0},{12,28},{16,24},{20,4},{24,16},{28,12},{1,9},{5... | collective-permute-start | bytes 2359304 | tf_op jit(solution)/shard_map/ppermute | solution.py:371
  148.3 28.2 %collective-permute-start.21 = (bf16[768,1024]{1,0:T(8,128)(2,1)S(1)}, bf16[768,1024]{1,0:T(8,128)(2,1)S(1)}, u32[]{:S(2)}, u32[]{:S(2)}) collective-permute-start(bf16[768,1024]{1,0:T(8,128)(2,1)S(1)} %constant_dynamic-update-slice_fusion), channel_id=1, source_target_pairs={{0,16},{4,12},{8,24},{12,4},{16,0},{20,28},{24,8},{28,20},{1,17},{... | collective-permute-start | bytes 4718600 | tf_op jit(solution)/shard_map/ppermute | solution.py:371
  150.0 20.5 %collective-permute-start.22 = (bf16[384,1024]{1,0:T(8,128)(2,1)S(1)}, bf16[384,1024]{1,0:T(8,128)(2,1)S(1)}, u32[]{:S(2)}, u32[]{:S(2)}) collective-permute-start(bf16[384,1024]{1,0:T(8,128)(2,1)S(1)} %pad_maximum_fusion.9), channel_id=1, source_target_pairs={{0,8},{4,20},{8,0},{12,28},{16,24},{20,4},{24,16},{28,12},{1,9},{5... | collective-permute-start | bytes 2359304 | tf_op jit(solution)/shard_map/ppermute | solution.py:371
  150.6 33.2 %collective-permute-start.25 = (bf16[768,1024]{1,0:T(8,128)(2,1)S(1)}, bf16[768,1024]{1,0:T(8,128)(2,1)S(1)}, u32[]{:S(2)}, u32[]{:S(2)}) collective-permute-start(bf16[768,1024]{1,0:T(8,128)(2,1)S(1)} %constant_dynamic-update-slice_fusion), channel_id=1, source_target_pairs={{0,4},{4,0},{8,12},{12,8},{16,20},{20,16},{24,28},{28,24},{1,5},{5... | collective-permute-start | bytes 4718600 | tf_op jit(solution)/shard_map/ppermute | solution.py:366
  176.6 23.1 %collective-permute-start.24 = (bf16[768,1024]{1,0:T(8,128)(2,1)S(1)}, bf16[768,1024]{1,0:T(8,128)(2,1)S(1)}, u32[]{:S(2)}, u32[]{:S(2)}) collective-permute-start(bf16[768,1024]{1,0:T(8,128)(2,1)S(1)} %constant_dynamic-update-slice_fusion.4), channel_id=1, source_target_pairs={{0,4},{4,0},{8,12},{12,8},{16,20},{20,16},{24,28},{28,24},{1,5},{5... | collective-permute-start | bytes 4718600 | tf_op jit(solution)/shard_map/ppermute | solution.py:366
  176.7 29.8 %collective-permute-start.23 = (bf16[768,1024]{1,0:T(8,128)(2,1)S(1)}, bf16[768,1024]{1,0:T(8,128)(2,1)S(1)}, u32[]{:S(2)}, u32[]{:S(2)}) collective-permute-start(bf16[768,1024]{1,0:T(8,128)(2,1)S(1)} %constant_dynamic-update-slice_fusion.4), channel_id=1, source_target_pairs={{0,16},{4,12},{8,24},{12,4},{16,0},{20,28},{24,8},{28,20},{1,17},{... | collective-permute-start | bytes 4718600 | tf_op jit(solution)/shard_map/ppermute | solution.py:371
  203.6 55.3 %collective-permute-start.36 = (bf16[768,1024]{1,0:T(8,128)(2,1)}, bf16[768,1024]{1,0:T(8,128)(2,1)}, u32[]{:S(2)}, u32[]{:S(2)}) collective-permute-start(bf16[768,1024]{1,0:T(8,128)(2,1)} %convolution_convert_fusion.1), channel_id=1, source_target_pairs={{0,4},{4,0},{8,12},{12,8},{16,20},{20,16},{24,28},{28,24},{1,5},{5... | collective-permute-start | bytes 4718600 | tf_op jit(solution)/shard_map/ppermute | solution.py:366
  220.2 30.9 %collective-permute-start.32 = (bf16[1024,1024]{1,0:T(8,128)(2,1)}, bf16[1024,1024]{1,0:T(8,128)(2,1)}, u32[]{:S(2)}, u32[]{:S(2)}) collective-permute-start(bf16[1024,1024]{1,0:T(8,128)(2,1)} %pad_maximum_fusion.2), channel_id=1, source_target_pairs={{0,16},{4,12},{8,24},{12,4},{16,0},{20,28},{24,8},{28,20},{1,17},{... | collective-permute-start | bytes 6291464 | tf_op jit(solution)/shard_map/ppermute | solution.py:371
  234.2 46.0 %collective-permute-start.33 = (bf16[1024,1024]{1,0:T(8,128)(2,1)}, bf16[1024,1024]{1,0:T(8,128)(2,1)}, u32[]{:S(2)}, u32[]{:S(2)}) collective-permute-start(bf16[1024,1024]{1,0:T(8,128)(2,1)} %pad_maximum_fusion.1), channel_id=1, source_target_pairs={{0,16},{4,12},{8,24},{12,4},{16,0},{20,28},{24,8},{28,20},{1,17},{... | collective-permute-start | bytes 6291464 | tf_op jit(solution)/shard_map/ppermute | solution.py:371
  254.8 24.6 %collective-permute-start.35 = (bf16[512,1024]{1,0:T(8,128)(2,1)}, bf16[512,1024]{1,0:T(8,128)(2,1)}, u32[]{:S(2)}, u32[]{:S(2)}) collective-permute-start(bf16[512,1024]{1,0:T(8,128)(2,1)} %pad_maximum_fusion.4), channel_id=1, source_target_pairs={{0,8},{4,20},{8,0},{12,28},{16,24},{20,4},{24,16},{28,12},{1,9},{5... | collective-permute-start | bytes 3145736 | tf_op jit(solution)/shard_map/ppermute | solution.py:371
  286.4 88.0 %reduce-scatter.3.cloned.1.call-start = ((), (), s32[]{:S(2)}) async-start(), calls=%async_computation.2 | async-start | bytes 1310720 | tf_op jit(solution)/shard_map/reduce_scatter | solution.py:596
  311.5 110.6 %all-gather.5.cloned.1.call-start = ((), (), s32[]{:S(2)}) async-start(), calls=%async_computation.4 | async-start | bytes 2359296 | tf_op jit(solution)/shard_map/all_gather | solution.py:388
  327.9 127.8 %all-gather.7.cloned.1.call-start = ((), (), s32[]{:S(2)}) async-start(), calls=%async_computation.5 | async-start | bytes 2359296 | tf_op jit(solution)/shard_map/all_gather | solution.py:388
  333.4 28.5 %collective-permute-start.42 = (bf16[256,1024]{1,0:T(8,128)(2,1)S(1)}, bf16[256,1024]{1,0:T(8,128)(2,1)}, u32[]{:S(2)}, u32[]{:S(2)}) collective-permute-start(bf16[256,1024]{1,0:T(8,128)(2,1)S(1)} %slice.293), channel_id=1, source_target_pairs={{2,0},{3,1},{6,4},{7,5},{10,8},{11,9},{14,12},{15,13},{18,16},{19,... | collective-permute-start | bytes 1572872 | tf_op jit(solution)/shard_map/ppermute | solution.py:377
  361.9 31.4 %collective-permute-start.43 = (bf16[2,4,256,512]{3,2,1,0:T(8,128)(2,1)}, bf16[2,4,256,512]{3,2,1,0:T(8,128)(2,1)}, u32[]{:S(2)}, u32[]{:S(2)}) collective-permute-start(bf16[2,4,256,512]{3,2,1,0:T(8,128)(2,1)} %get-tuple-element.216), channel_id=1, source_target_pairs={{0,16},{4,12},{8,24},{12,4},{16,0},{20,28},{24,8},{28,20},{1,17},{... | collective-permute-start | bytes 6291464 | tf_op jit(solution)/shard_map/ppermute | solution.py:371
  367.5 29.9 %collective-permute-start.48 = (bf16[512,1024]{1,0:T(8,128)(2,1)}, bf16[512,1024]{1,0:T(8,128)(2,1)}, u32[]{:S(2)}, u32[]{:S(2)}) collective-permute-start(bf16[512,1024]{1,0:T(8,128)(2,1)} %slice.307), channel_id=1, source_target_pairs={{1,0},{2,1},{3,2},{5,4},{6,5},{7,6},{9,8},{10,9},{11,10},{13,12},{... | collective-permute-start | bytes 3145736 | tf_op jit(solution)/shard_map/ppermute | solution.py:377
  395.9 22.4 %collective-permute-start.44 = (bf16[4,256,512]{2,1,0:T(8,128)(2,1)}, bf16[4,256,512]{2,1,0:T(8,128)(2,1)S(1)}, u32[]{:S(2)}, u32[]{:S(2)}) collective-permute-start(bf16[4,256,512]{2,1,0:T(8,128)(2,1)} %fusion.49), channel_id=1, source_target_pairs={{0,8},{4,20},{8,0},{12,28},{16,24},{20,4},{24,16},{28,12},{1,9},{5... | collective-permute-start | bytes 3145736 | tf_op jit(solution)/shard_map/ppermute | solution.py:371
  460.2 19.6 %collective-permute-start.56 = (bf16[4,4,64,512]{3,2,1,0:T(8,128)(2,1)S(1)}, bf16[4,4,64,512]{3,2,1,0:T(8,128)(2,1)S(1)}, u32[]{:S(2)}, u32[]{:S(2)}) collective-permute-start(bf16[4,4,64,512]{3,2,1,0:T(8,128)(2,1)S(1)} %bitcast.166), channel_id=1, source_target_pairs={{0,4},{4,0},{8,12},{12,8},{16,20},{20,16},{24,28},{28,24},{1,5},{5... | collective-permute-start | bytes 3145736 | tf_op jit(solution)/shard_map/ppermute | solution.py:366
  (100 other events, 888.9 us)
Sparse Core Ops, SparseCore 0:
  286.5 26.0 reduce-scatter.4
  314.9 25.9 reduce-scatter.2
  342.8 32.2 all-gather.4
  393.4 27.4 all-gather.6

commit v5 on v4

--- a/solution.py
+++ b/solution.py
@@ -328,6 +328,23 @@
     )(*mine, *theirs)
 
 
+def widen_t_kernel(in_ref, out_ref):
+    out_ref[...] = in_ref[...].T.astype(f32)
+
+
+def widen_t(value):
+    rows, cols = value.shape
+    step = 256
+    return pl.pallas_call(
+        widen_t_kernel,
+        grid=(cols // step,),
+        in_specs=[pl.BlockSpec((rows, step), lambda i: (0, i))],
+        out_specs=pl.BlockSpec((step, rows), lambda i: (i, 0)),
+        cost_estimate=SMALL,
+        out_shape=jax.ShapeDtypeStruct((cols, rows), f32),
+    )(value)
+
+
 def last_att_kernel(at, mine_ref, other_ref, out_ref, qkv_ref):
     mine, other = mine_ref[0].astype(f32), other_ref[0].astype(f32)
     half = mine.shape[-1]
@@ -648,7 +665,7 @@
     theirs = [swap(v, 0) for v in theirs]
     mine = weights_half(0)
     att_hi, att_lo = add_att(mine, theirs)
-    att_hi, passed, grad_halo, grad_ext, dq_late = tie((att_hi, passed, grad_halo, grad_ext, dq))
+    att_hi, grad_ext, dq_late = tie((att_hi, grad_ext, dq))
     att_got = hop(att_hi, 2)
     near = move(grad_halo[near_rows:], [(i, i - 1) for i in range(1, mp)])
     grad_norm1 = grad_ext[halo:] + dot(dq_late, w_q, 1, 0)
@@ -660,8 +677,6 @@
     grad_norm1 = grad_norm1 + near
     xhat1, rstd1 = xhat_ext[halo:], rstd_ext[halo:]
     in_grad = grad_resid + norm_back(grad_norm1, norm1_gain, xhat1, rstd1)
-    att_keep = add(att_keep, att_hop1).reshape(4, mp, HD, half)
-    att_z = [shift(att_keep[:, s], mp - s) for s in range(1, mp)]
     ff_bias = jnp.concatenate([jnp.sum(g.astype(f32), axis=0) for g in grad_pre])
     ff_bias = ff_bias.reshape(mp * 8, piece)
     qv_sums = jnp.concatenate(
@@ -692,12 +707,15 @@
         ],
         1,
     )
-    grad_fc1 = sum1.reshape(ff_here, wide).T.astype(f32)
+    grad_fc1 = widen_t(sum1.reshape(ff_here, wide))
     grad_fc2 = sum2.reshape(ff_here, wide).astype(f32)
 
-    att_z, vectors, grad_fc2, in_grad = tie((att_z, vectors, grad_fc2, in_grad))
+    att_hop1, vectors = tie((att_hop1, vectors))
+    att_keep = add(att_keep, att_hop1).reshape(4, mp, HD, half)
+    att_z = [shift(att_keep[:, s], mp - s) for s in range(1, mp)]
     for bit in range(lax.axis_size("dp").bit_length() - 1):
         vectors = vectors + swap(vectors, bit)
+    att_z, vectors, grad_fc2, in_grad = tie((att_z, vectors, grad_fc2, in_grad))
     att_sum = att_keep[:, 0].astype(f32)
     for got in att_z:
         att_sum = att_sum + got.astype(f32)

time: 504 us -> 495 us (0.982)
  starting transfers between devices: 69.2 us -> 63 us
    ppermute x21, waiting for transfers between devices: 8.16 us -> 0.06 us  [swap(): return lax.ppermute(value, 'dp', [(i, i ^ 1 << b) for i in range(n)])]
    ppermute x22, waiting for transfers between devices: 62.6 us -> 68.7 us  [move(): return lax.ppermute(value, 'mp', pairs)]
    ppermute x22, starting transfers between devices: 46.1 us -> 41.1 us  [move(): return lax.ppermute(value, 'mp', pairs)]
    unnamed x156 -> x151, local copies, waits for them, and re-layouts: 25.1 us -> 20.6 us
  transfers between devices with their start and end apart: 61 -> 61, of which waited for: 20 -> 17; matrix products, arithmetic and copies ran while one was open for 33% -> 32% of each run, Pallas kernels for 19% -> 19%
where the time goes in v5:
time: 495 us; the launch traced here: 487 us
  waiting for transfers between devices  120 us (24%)
  Pallas kernels  104 us (21%)
  matrix products  96.5 us (19%)
  starting transfers between devices  63 us (13%)
  other arithmetic  59.3 us (12%)
  local copies, waits for them, and re-layouts  28.2 us (6%)
  between operations  15.7 us (3%)
    dot_general x50, matrix products, dot(): lax.dot_general(a, b, (((ca,), (cb,)), ((), ())), preferred_element_type=...  95.8 us
    ppermute x22, waiting for transfers between devices, move(): return lax.ppermute(value, 'mp', pairs)  68.7 us
    ppermute x14, waiting for transfers between devices, hop(): lax.ppermute(value, 'dp', [(i, i ^ (2 if i & 1 == stage - 1 else 4)) for...  50.8 us
    ppermute x22, starting transfers between devices, move(): return lax.ppermute(value, 'mp', pairs)  41.1 us
    pallas_call x3, Pallas kernels, attend_back(): pl.pallas_call(functools.partial(attend_back_kernel, halo, start), grid=(...  37 us
    pallas_call x2, Pallas kernels, attend(): pl.pallas_call(functools.partial(attend_kernel, halo, start), grid=(pairs...  27.1 us
    unnamed x151, local copies, waits for them, and re-layouts  20.6 us
    convert_element_type x10, other arithmetic, add(): return (a.astype(f32) + b.astype(f32)).astype(bf16)  16.3 us
  transfers between devices with their start and end apart: 61, of which 17 were waited for; matrix products, arithmetic and copies ran while one was open for 32% of the time, Pallas kernels for 19%

profile of v5, /device:TPU:0, one launch (start us, length us, event | category | flops | bytes accessed | tf_op | source)
XLA Modules:
  0.0 486.5 jit_solution(14517005048843068109)
XLA Ops:
  25.5 4.4 shard_map.255
  29.9 7.3 %shard_map.256 = (bf16[1024,1024]{1,0:T(8,128)(2,1)}, bf16[1024,1024]{1,0:T(8,128)(2,1)}) custom-call(s32[8]{0:T(128)} %add_xor_fusion.at, bf16[1024,1024]{1,0:T(8,128)(2,1)} %fc1_ref.3, bf16[1024,1024]{1,0:T(8,128)(2,1)} %fc2_ref.3), custom_call_target="tpu_custom_call" | custom-call | flops 1 | bytes 1 | tf_op jit(solution)/shard_map/pallas_call | solution.py:237
  44.0 7.5 %collective-permute-start.7 = (bf16[256,1024]{1,0:T(8,128)(2,1)S(1)}, bf16[256,1024]{1,0:T(8,128)(2,1)S(1)}, u32[]{:S(2)}, u32[]{:S(2)}) collective-permute-start(bf16[256,1024]{1,0:T(8,128)(2,1)S(1)} %get-tuple-element.312), channel_id=1, source_target_pairs={{0,1},{1,2},{2,3},{4,5},{5,6},{6,7},{8,9},{9,10},{10,11},{12,13},{... | collective-permute-start | bytes 1572872 | tf_op jit(solution)/shard_map/ppermute | solution.py:394
  51.5 10.6 %collective-permute-done.7 = bf16[256,1024]{1,0:T(8,128)(2,1)S(1)} collective-permute-done((bf16[256,1024]{1,0:T(8,128)(2,1)S(1)}, bf16[256,1024]{1,0:T(8,128)(2,1)S(1)}, u32[]{:S(2)}, u32[]{:S(2)}) %collective-permute-start.7) | collective-permute-done | bytes 524320 | tf_op jit(solution)/shard_map/ppermute | solution.py:394
  65.5 4.4 collective-permute-start.12
  74.9 7.6 %collective-permute-done.12 = bf16[256,1024]{1,0:T(8,128)(2,1)S(1)} collective-permute-done((bf16[256,1024]{1,0:T(8,128)(2,1)}, bf16[256,1024]{1,0:T(8,128)(2,1)S(1)}, u32[]{:S(2)}, u32[]{:S(2)}) %collective-permute-start.12) | collective-permute-done | bytes 524320 | tf_op jit(solution)/shard_map/ppermute | solution.py:394
  82.5 10.2 %collective-permute-done.11 = bf16[256,1024]{1,0:T(8,128)(2,1)S(1)} collective-permute-done((bf16[256,1024]{1,0:T(8,128)(2,1)S(1)}, bf16[256,1024]{1,0:T(8,128)(2,1)S(1)}, u32[]{:S(2)}, u32[]{:S(2)}) %collective-permute-start.11) | collective-permute-done | bytes 524320 | tf_op jit(solution)/shard_map/ppermute | solution.py:394
  100.7 4.9 %add_convert_fusion.1 = (bf16[1280,1024]{1,0:T(8,128)(2,1)}, f32[1280,1024]{1,0:T(8,128)}) fusion(f32[1024]{0:T(1024)S(1)} %copy-done.45, f32[1024]{0:T(1024)S(1)} %copy-done.42, f32[1280]{0:T(1024)S(1)} %add_rsqrt_fusion, f32[1280]{0:T(1024)S(1)} %broadcast_multiply_fusion, bf16[512,1024]{1,0:T(8,128)(2,1)S(1)} %copy-done.16, ...), kind=kLoop, calls=%fused_computation.7 | loop fusion | flops 17039360 | bytes 10504192 | tf_op jit(solution)/shard_map/convert_element_type | solution.py:539
  105.6 7.1 %shard_map.258 = (bf16[4,4,64,1024]{3,2,1,0:T(8,128)(2,1)}, bf16[4,4,64,1024]{3,2,1,0:T(8,128)(2,1)}, bf16[4,4,64,1024]{3,2,1,0:T(8,128)(2,1)}, bf16[4,4,64,1024]{3,2,1,0:T(8,128)(2,1)}) custom-call(s32[1]{0:T(128)} %bitcast.core, bf16[4,4,64,512]{3,2,1,0:T(8,128)(2,1)} %get-tuple-element.146.refs_0_, bf16[3,4,64,512]{3,2,1,0:T(8,128)(2,1)} %get-tuple-element.314.refs_1_, ...), custom_call_target="tpu_custom_call" | custom-call | flops 1 | bytes 1 | tf_op jit(solution)/shard_map/pallas_call | solution.py:288
  112.8 3.3 add_convert_fusion.10.q_ref
  133.0 13.3 %shard_map.259 = (bf16[512,1024]{1,0:T(8,128)(2,1)S(1)}, f32[8,2,512]{2,1,0:T(2,128)S(1)}) custom-call(f32[16]{0:T(128)S(1)} %get-tuple-element.133.slopes, s32[1,512]{1,0:T(1,128)S(1)} %pad_dynamic-slice_fusion.8.segq, s32[1280,1]{1,0:T(8,128)S(1)} %copy.72.segk, bf16[512,1024]{1,0:T(8,128)(2,1)S(1)} %add_convert_fusion.10.q_ref, ...), custom_call_target="tpu_custom_call" | custom-call | flops 1 | bytes 1 | tf_op jit(solution)/shard_map/pallas_call | solution.py:114
  150.6 13.8 %shard_map.260 = (bf16[512,1024]{1,0:T(8,128)(2,1)S(1)}, f32[8,2,512]{2,1,0:T(2,128)S(1)}) custom-call(f32[16]{0:T(128)S(1)} %get-tuple-element.133.slopes, s32[1,512]{1,0:T(1,128)S(1)} %pad_dynamic-slice_fusion.8.segq, s32[1280,1]{1,0:T(8,128)S(1)} %copy.72.segk, ...), custom_call_target="tpu_custom_call", output_to_operand_aliasing={{0}: (6, {}), {1}: (7, {})} | custom-call | flops 1 | bytes 1 | tf_op jit(solution)/shard_map/pallas_call | solution.py:114
  164.5 6.0 %collective-permute-done.22 = bf16[384,1024]{1,0:T(8,128)(2,1)S(1)} collective-permute-done((bf16[384,1024]{1,0:T(8,128)(2,1)S(1)}, bf16[384,1024]{1,0:T(8,128)(2,1)S(1)}, u32[]{:S(2)}, u32[]{:S(2)}) %collective-permute-start.22) | collective-permute-done | bytes 786464 | tf_op jit(solution)/shard_map/ppermute | solution.py:388
  170.5 6.2 %collective-permute-done.21 = bf16[768,1024]{1,0:T(8,128)(2,1)} collective-permute-done((bf16[768,1024]{1,0:T(8,128)(2,1)S(1)}, bf16[768,1024]{1,0:T(8,128)(2,1)}, u32[]{:S(2)}, u32[]{:S(2)}) %collective-permute-start.21) | collective-permute-done | bytes 1572896 | tf_op jit(solution)/shard_map/ppermute | solution.py:388
  240.6 13.5 %shard_map.261 = (bf16[512,1024]{1,0:T(8,128)(2,1)S(1)}, bf16[1280,1024]{1,0:T(8,128)(2,1)}, bf16[1280,1024]{1,0:T(8,128)(2,1)}) custom-call(f32[16]{0:T(128)S(1)} %get-tuple-element.133.slopes, s32[1,512]{1,0:T(1,128)S(1)} %pad_dynamic-slice_fusion.8.segq, s32[1280,1]{1,0:T(8,128)S(1)} %copy.72.segk, bf16[512,1024]{1,0:T(8,128)(2,1)S(1)} %add_convert_fusion.10.q_ref, ...), custom_call_target="tpu_custom_call" | custom-call | flops 1 | bytes 1 | tf_op jit(solution)/shard_map/pallas_call | solution.py:146
  261.9 3.8 add_convert_fusion.2
  265.7 13.8 %shard_map.262 = (bf16[512,1024]{1,0:T(8,128)(2,1)S(1)}, bf16[1280,1024]{1,0:T(8,128)(2,1)}, bf16[1280,1024]{1,0:T(8,128)(2,1)}) custom-call(f32[16]{0:T(128)S(1)} %get-tuple-element.133.slopes, s32[1,512]{1,0:T(1,128)S(1)} %pad_dynamic-slice_fusion.8.segq, s32[1280,1]{1,0:T(8,128)S(1)} %copy.72.segk, ...), custom_call_target="tpu_custom_call", output_to_operand_aliasing={{0}: (8, {}), {1}: (9, {}), {2}: (10, {})} | custom-call | flops 1 | bytes 1 | tf_op jit(solution)/shard_map/pallas_call | solution.py:146
  297.7 9.8 %shard_map.263 = (bf16[512,1024]{1,0:T(8,128)(2,1)S(1)}, bf16[1280,1024]{1,0:T(8,128)(2,1)}, bf16[1280,1024]{1,0:T(8,128)(2,1)}) custom-call(f32[16]{0:T(128)S(1)} %get-tuple-element.133.slopes, s32[1,512]{1,0:T(1,128)S(1)} %pad_dynamic-slice_fusion.8.segq, s32[1280,1]{1,0:T(8,128)S(1)} %copy.72.segk, ...), custom_call_target="tpu_custom_call", output_to_operand_aliasing={{0}: (8, {}), {1}: (9, {}), {2}: (10, {})} | custom-call | flops 1 | bytes 1 | tf_op jit(solution)/shard_map/pallas_call | solution.py:146
  316.6 4.6 fusion.149
  343.4 6.5 %shard_map.264 = (bf16[2,4,256,512]{3,2,1,0:T(8,128)(2,1)}, bf16[2,4,256,512]{3,2,1,0:T(8,128)(2,1)}) custom-call(bf16[1024,512]{1,0:T(8,128)(2,1)} %convolution_convert_fusion.11.refs_0_, bf16[1024,512]{1,0:T(8,128)(2,1)} %convolution_convert_fusion.10.refs_1_, bf16[1024,512]{1,0:T(8,128)(2,1)} %convolution_convert_fusion.6.refs_2_, ...), custom_call_target="tpu_custom_call" | custom-call | flops 1 | bytes 1 | tf_op jit(solution)/shard_map/pallas_call | solution.py:318
  359.7 5.0 %slice_add_fusion = f32[512,1024]{1,0:T(8,128)} fusion(f32[1280,1024]{1,0:T(8,128)} %copy-done.39, bf16[512,1024]{1,0:T(8,128)(2,1)S(1)} %copy-done.9, bf16[1024,1024]{1,0:T(8,128)(2,1)} %bitcast.197), kind=kOutput, calls=%fused_computation.57 | convolution fusion | flops 1074266112 | bytes 7340032 | tf_op jit(solution)/shard_map/dot_general | solution.py:22
  364.6 20.1 %collective-permute-done.42 = bf16[2,4,256,512]{3,2,1,0:T(8,128)(2,1)} collective-permute-done((bf16[2,4,256,512]{3,2,1,0:T(8,128)(2,1)}, bf16[2,4,256,512]{3,2,1,0:T(8,128)(2,1)}, u32[]{:S(2)}, u32[]{:S(2)}) %collective-permute-start.42) | collective-permute-done | bytes 2097184 | tf_op jit(solution)/shard_map/ppermute | solution.py:388
  388.7 14.5 %collective-permute-done.44 = bf16[256,1024]{1,0:T(8,128)(2,1)} collective-permute-done((bf16[256,1024]{1,0:T(8,128)(2,1)}, bf16[256,1024]{1,0:T(8,128)(2,1)}, u32[]{:S(2)}, u32[]{:S(2)}) %collective-permute-start.44) | collective-permute-done | bytes 524320 | tf_op jit(solution)/shard_map/ppermute | solution.py:394
  415.7 3.4 multiply_add_fusion.5
  419.1 4.1 convert_element_type.476
  423.2 13.4 %collective-permute-done.47 = bf16[4,64,512]{2,1,0:T(8,128)(2,1)} collective-permute-done((bf16[4,64,512]{2,1,0:T(8,128)(2,1)}, bf16[4,64,512]{2,1,0:T(8,128)(2,1)}, u32[]{:S(2)}, u32[]{:S(2)}) %collective-permute-start.47) | collective-permute-done | bytes 262176 | tf_op jit(solution)/shard_map/ppermute | solution.py:394
  438.6 5.6 %collective-permute-done.54 = bf16[4,64,512]{2,1,0:T(8,128)(2,1)S(1)} collective-permute-done((bf16[4,64,512]{2,1,0:T(8,128)(2,1)S(1)}, bf16[4,64,512]{2,1,0:T(8,128)(2,1)S(1)}, u32[]{:S(2)}, u32[]{:S(2)}) %collective-permute-start.54) | collective-permute-done | bytes 262176 | tf_op jit(solution)/shard_map/ppermute | solution.py:388
  445.2 8.4 %collective-permute-done.55 = bf16[2,4,64,512]{3,2,1,0:T(8,128)(2,1)S(1)} collective-permute-done((bf16[2,4,64,512]{3,2,1,0:T(8,128)(2,1)S(1)}, bf16[2,4,64,512]{3,2,1,0:T(8,128)(2,1)S(1)}, u32[]{:S(2)}, u32[]{:S(2)}) %collective-permute-start.55) | collective-permute-done | bytes 524320 | tf_op jit(solution)/shard_map/ppermute | solution.py:388
  453.8 4.8 shard_map.265
  459.2 3.7 collective-permute-done.52
  471.1 4.8 shard_map.266
  475.9 3.5 copy.80
  (413 shorter events, 220.8 us)
Async XLA Ops:
  7.2 323.7 %reduce-scatter.5.cloned.1.call-start = ((), (), s32[]{:S(2)}) async-start(), calls=%async_computation.3 | async-start | bytes 1310720 | tf_op jit(solution)/shard_map/reduce_scatter | solution.py:613
  20.7 19.9 %collective-permute-start.1 = (bf16[4,64,512]{2,1,0:T(8,128)(2,1)}, bf16[4,64,512]{2,1,0:T(8,128)(2,1)S(1)}, u32[]{:S(2)}, u32[]{:S(2)}) collective-permute-start(bf16[4,64,512]{2,1,0:T(8,128)(2,1)} %bitcast.172), channel_id=1, source_target_pairs={{0,2},{1,3},{2,0},{3,1},{4,6},{5,7},{6,4},{7,5},{8,10},{9,11},{10,... | collective-permute-start | bytes 786440 | tf_op jit(solution)/shard_map/ppermute | solution.py:394
  41.6 20.4 %collective-permute-start.6 = (bf16[3,4,64,512]{3,2,1,0:T(8,128)(2,1)}, bf16[3,4,64,512]{3,2,1,0:T(8,128)(2,1)}, u32[]{:S(2)}, u32[]{:S(2)}) collective-permute-start(bf16[3,4,64,512]{3,2,1,0:T(8,128)(2,1)} %get-tuple-element.314.refs_1_), channel_id=1, source_target_pairs={{0,8},{4,20},{8,0},{12,28},{16,24},{20,4},{24,16},{28,12},{1,9},{5... | collective-permute-start | bytes 2359304 | tf_op jit(solution)/shard_map/ppermute | solution.py:388
  64.5 28.2 %collective-permute-start.8 = (bf16[2,3,4,64,512]{4,3,2,1,0:T(8,128)(2,1)}, bf16[2,3,4,64,512]{4,3,2,1,0:T(8,128)(2,1)}, u32[]{:S(2)}, u32[]{:S(2)}) collective-permute-start(bf16[2,3,4,64,512]{4,3,2,1,0:T(8,128)(2,1)} %pad_maximum_fusion.3), channel_id=1, source_target_pairs={{0,16},{4,12},{8,24},{12,4},{16,0},{20,28},{24,8},{28,20},{1,17},{... | collective-permute-start | bytes 4718600 | tf_op jit(solution)/shard_map/ppermute | solution.py:388
  65.1 27.7 %collective-permute-start.10 = (bf16[3,4,64,512]{3,2,1,0:T(8,128)(2,1)}, bf16[3,4,64,512]{3,2,1,0:T(8,128)(2,1)}, u32[]{:S(2)}, u32[]{:S(2)}) collective-permute-start(bf16[3,4,64,512]{3,2,1,0:T(8,128)(2,1)} %collective-permute-done.6.refs_2_), channel_id=1, source_target_pairs={{0,4},{4,0},{8,12},{12,8},{16,20},{20,16},{24,28},{28,24},{1,5},{5... | collective-permute-start | bytes 2359304 | tf_op jit(solution)/shard_map/ppermute | solution.py:383
  69.9 22.8 %collective-permute-start.11 = (bf16[256,1024]{1,0:T(8,128)(2,1)S(1)}, bf16[256,1024]{1,0:T(8,128)(2,1)S(1)}, u32[]{:S(2)}, u32[]{:S(2)}) collective-permute-start(bf16[256,1024]{1,0:T(8,128)(2,1)S(1)} %collective-permute-done.7), channel_id=1, source_target_pairs={{0,1},{1,2},{2,3},{4,5},{5,6},{6,7},{8,9},{9,10},{10,11},{12,13},{... | collective-permute-start | bytes 1572872 | tf_op jit(solution)/shard_map/ppermute | solution.py:394
  92.7 23.4 %collective-permute-start.14 = (bf16[128,1024]{1,0:T(8,128)(2,1)}, bf16[128,1024]{1,0:T(8,128)(2,1)}, u32[]{:S(2)}, u32[]{:S(2)}) collective-permute-start(bf16[128,1024]{1,0:T(8,128)(2,1)} %get-tuple-element.153), channel_id=1, source_target_pairs={{0,3},{1,0},{2,1},{3,2},{4,7},{5,4},{6,5},{7,6},{8,11},{9,8},{10,9... | collective-permute-start | bytes 786440 | tf_op jit(solution)/shard_map/ppermute | solution.py:394
  95.0 24.3 %collective-permute-start.15 = (bf16[128,1024]{1,0:T(8,128)(2,1)}, bf16[128,1024]{1,0:T(8,128)(2,1)}, u32[]{:S(2)}, u32[]{:S(2)}) collective-permute-start(bf16[128,1024]{1,0:T(8,128)(2,1)} %get-tuple-element.153), channel_id=1, source_target_pairs={{0,2},{1,3},{2,0},{3,1},{4,6},{5,7},{6,4},{7,5},{8,10},{9,11},{10,... | collective-permute-start | bytes 786440 | tf_op jit(solution)/shard_map/ppermute | solution.py:394
  96.7 22.6 %collective-permute-start.16 = (bf16[128,1024]{1,0:T(8,128)(2,1)}, bf16[128,1024]{1,0:T(8,128)(2,1)}, u32[]{:S(2)}, u32[]{:S(2)}) collective-permute-start(bf16[128,1024]{1,0:T(8,128)(2,1)} %get-tuple-element.153), channel_id=1, source_target_pairs={{0,1},{1,2},{2,3},{3,0},{4,5},{5,6},{6,7},{7,4},{8,9},{9,10},{10,1... | collective-permute-start | bytes 786440 | tf_op jit(solution)/shard_map/ppermute | solution.py:394
  119.3 28.9 %collective-permute-start.18 = (bf16[128,1024]{1,0:T(8,128)(2,1)S(1)}, bf16[128,1024]{1,0:T(8,128)(2,1)S(1)}, u32[]{:S(2)}, u32[]{:S(2)}) collective-permute-start(bf16[128,1024]{1,0:T(8,128)(2,1)S(1)} %copy-done.63), channel_id=1, source_target_pairs={{0,3},{1,0},{2,1},{3,2},{4,7},{5,4},{6,5},{7,6},{8,11},{9,8},{10,9... | collective-permute-start | bytes 786440 | tf_op jit(solution)/shard_map/ppermute | solution.py:394
  119.5 28.8 %collective-permute-start.19 = (bf16[128,1024]{1,0:T(8,128)(2,1)S(1)}, bf16[128,1024]{1,0:T(8,128)(2,1)S(1)}, u32[]{:S(2)}, u32[]{:S(2)}) collective-permute-start(bf16[128,1024]{1,0:T(8,128)(2,1)S(1)} %copy-done.63), channel_id=1, source_target_pairs={{0,2},{1,3},{2,0},{3,1},{4,6},{5,7},{6,4},{7,5},{8,10},{9,11},{10,... | collective-permute-start | bytes 786440 | tf_op jit(solution)/shard_map/ppermute | solution.py:394
  121.1 27.2 %collective-permute-start.20 = (bf16[128,1024]{1,0:T(8,128)(2,1)S(1)}, bf16[128,1024]{1,0:T(8,128)(2,1)S(1)}, u32[]{:S(2)}, u32[]{:S(2)}) collective-permute-start(bf16[128,1024]{1,0:T(8,128)(2,1)S(1)} %copy-done.63), channel_id=1, source_target_pairs={{0,1},{1,2},{2,3},{3,0},{4,5},{5,6},{6,7},{7,4},{8,9},{9,10},{10,1... | collective-permute-start | bytes 786440 | tf_op jit(solution)/shard_map/ppermute | solution.py:394
  124.5 23.8 %collective-permute-start.17 = (bf16[384,1024]{1,0:T(8,128)(2,1)S(1)}, bf16[384,1024]{1,0:T(8,128)(2,1)S(1)}, u32[]{:S(2)}, u32[]{:S(2)}) collective-permute-start(bf16[384,1024]{1,0:T(8,128)(2,1)S(1)} %pad_maximum_fusion.8), channel_id=1, source_target_pairs={{0,8},{4,20},{8,0},{12,28},{16,24},{20,4},{24,16},{28,12},{1,9},{5... | collective-permute-start | bytes 2359304 | tf_op jit(solution)/shard_map/ppermute | solution.py:388
  148.3 28.3 %collective-permute-start.21 = (bf16[768,1024]{1,0:T(8,128)(2,1)S(1)}, bf16[768,1024]{1,0:T(8,128)(2,1)}, u32[]{:S(2)}, u32[]{:S(2)}) collective-permute-start(bf16[768,1024]{1,0:T(8,128)(2,1)S(1)} %constant_dynamic-update-slice_fusion), channel_id=1, source_target_pairs={{0,16},{4,12},{8,24},{12,4},{16,0},{20,28},{24,8},{28,20},{1,17},{... | collective-permute-start | bytes 4718600 | tf_op jit(solution)/shard_map/ppermute | solution.py:388
  150.0 20.5 %collective-permute-start.22 = (bf16[384,1024]{1,0:T(8,128)(2,1)S(1)}, bf16[384,1024]{1,0:T(8,128)(2,1)S(1)}, u32[]{:S(2)}, u32[]{:S(2)}) collective-permute-start(bf16[384,1024]{1,0:T(8,128)(2,1)S(1)} %pad_maximum_fusion.9), channel_id=1, source_target_pairs={{0,8},{4,20},{8,0},{12,28},{16,24},{20,4},{24,16},{28,12},{1,9},{5... | collective-permute-start | bytes 2359304 | tf_op jit(solution)/shard_map/ppermute | solution.py:388
  150.6 33.3 %collective-permute-start.25 = (bf16[768,1024]{1,0:T(8,128)(2,1)S(1)}, bf16[768,1024]{1,0:T(8,128)(2,1)S(1)}, u32[]{:S(2)}, u32[]{:S(2)}) collective-permute-start(bf16[768,1024]{1,0:T(8,128)(2,1)S(1)} %constant_dynamic-update-slice_fusion), channel_id=1, source_target_pairs={{0,4},{4,0},{8,12},{12,8},{16,20},{20,16},{24,28},{28,24},{1,5},{5... | collective-permute-start | bytes 4718600 | tf_op jit(solution)/shard_map/ppermute | solution.py:383
  176.7 24.5 %collective-permute-start.24 = (bf16[768,1024]{1,0:T(8,128)(2,1)S(1)}, bf16[768,1024]{1,0:T(8,128)(2,1)S(1)}, u32[]{:S(2)}, u32[]{:S(2)}) collective-permute-start(bf16[768,1024]{1,0:T(8,128)(2,1)S(1)} %constant_dynamic-update-slice_fusion.4), channel_id=1, source_target_pairs={{0,4},{4,0},{8,12},{12,8},{16,20},{20,16},{24,28},{28,24},{1,5},{5... | collective-permute-start | bytes 4718600 | tf_op jit(solution)/shard_map/ppermute | solution.py:383
  176.8 31.1 %collective-permute-start.23 = (bf16[768,1024]{1,0:T(8,128)(2,1)S(1)}, bf16[768,1024]{1,0:T(8,128)(2,1)S(1)}, u32[]{:S(2)}, u32[]{:S(2)}) collective-permute-start(bf16[768,1024]{1,0:T(8,128)(2,1)S(1)} %constant_dynamic-update-slice_fusion.4), channel_id=1, source_target_pairs={{0,16},{4,12},{8,24},{12,4},{16,0},{20,28},{24,8},{28,20},{1,17},{... | collective-permute-start | bytes 4718600 | tf_op jit(solution)/shard_map/ppermute | solution.py:388
  186.5 18.8 %collective-permute-start.27 = (bf16[768,1024]{1,0:T(8,128)(2,1)}, bf16[768,1024]{1,0:T(8,128)(2,1)S(1)}, u32[]{:S(2)}, u32[]{:S(2)}) collective-permute-start(bf16[768,1024]{1,0:T(8,128)(2,1)} %collective-permute-done.21), channel_id=1, source_target_pairs={{0,4},{4,0},{8,12},{12,8},{16,20},{20,16},{24,28},{28,24},{1,5},{5... | collective-permute-start | bytes 4718600 | tf_op jit(solution)/shard_map/ppermute | solution.py:383
  205.1 56.7 %collective-permute-start.36 = (bf16[768,1024]{1,0:T(8,128)(2,1)}, bf16[768,1024]{1,0:T(8,128)(2,1)}, u32[]{:S(2)}, u32[]{:S(2)}) collective-permute-start(bf16[768,1024]{1,0:T(8,128)(2,1)} %convolution_convert_fusion.1), channel_id=1, source_target_pairs={{0,4},{4,0},{8,12},{12,8},{16,20},{20,16},{24,28},{28,24},{1,5},{5... | collective-permute-start | bytes 4718600 | tf_op jit(solution)/shard_map/ppermute | solution.py:383
  223.2 30.9 %collective-permute-start.32 = (bf16[1024,1024]{1,0:T(8,128)(2,1)}, bf16[1024,1024]{1,0:T(8,128)(2,1)}, u32[]{:S(2)}, u32[]{:S(2)}) collective-permute-start(bf16[1024,1024]{1,0:T(8,128)(2,1)} %pad_maximum_fusion.2), channel_id=1, source_target_pairs={{0,16},{4,12},{8,24},{12,4},{16,0},{20,28},{24,8},{28,20},{1,17},{... | collective-permute-start | bytes 6291464 | tf_op jit(solution)/shard_map/ppermute | solution.py:388
  237.2 46.1 %collective-permute-start.33 = (bf16[1024,1024]{1,0:T(8,128)(2,1)}, bf16[1024,1024]{1,0:T(8,128)(2,1)}, u32[]{:S(2)}, u32[]{:S(2)}) collective-permute-start(bf16[1024,1024]{1,0:T(8,128)(2,1)} %pad_maximum_fusion.1), channel_id=1, source_target_pairs={{0,16},{4,12},{8,24},{12,4},{16,0},{20,28},{24,8},{28,20},{1,17},{... | collective-permute-start | bytes 6291464 | tf_op jit(solution)/shard_map/ppermute | solution.py:388
  257.8 24.7 %collective-permute-start.35 = (bf16[512,1024]{1,0:T(8,128)(2,1)}, bf16[512,1024]{1,0:T(8,128)(2,1)}, u32[]{:S(2)}, u32[]{:S(2)}) collective-permute-start(bf16[512,1024]{1,0:T(8,128)(2,1)} %pad_maximum_fusion.4), channel_id=1, source_target_pairs={{0,8},{4,20},{8,0},{12,28},{16,24},{20,4},{24,16},{28,12},{1,9},{5... | collective-permute-start | bytes 3145736 | tf_op jit(solution)/shard_map/ppermute | solution.py:388
  289.4 75.3 %reduce-scatter.3.cloned.1.call-start = ((), (), s32[]{:S(2)}) async-start(), calls=%async_computation.2 | async-start | bytes 1310720 | tf_op jit(solution)/shard_map/reduce_scatter | solution.py:613
  314.5 104.6 %all-gather.5.cloned.1.call-start = ((), (), s32[]{:S(2)}) async-start(), calls=%async_computation.4 | async-start | bytes 2359296 | tf_op jit(solution)/shard_map/all_gather | solution.py:405
  330.9 122.9 %all-gather.7.cloned.1.call-start = ((), (), s32[]{:S(2)}) async-start(), calls=%async_computation.5 | async-start | bytes 2359296 | tf_op jit(solution)/shard_map/all_gather | solution.py:405
  349.9 34.8 %collective-permute-start.42 = (bf16[2,4,256,512]{3,2,1,0:T(8,128)(2,1)}, bf16[2,4,256,512]{3,2,1,0:T(8,128)(2,1)}, u32[]{:S(2)}, u32[]{:S(2)}) collective-permute-start(bf16[2,4,256,512]{3,2,1,0:T(8,128)(2,1)} %get-tuple-element.215), channel_id=1, source_target_pairs={{0,16},{4,12},{8,24},{12,4},{16,0},{20,28},{24,8},{28,20},{1,17},{... | collective-permute-start | bytes 6291464 | tf_op jit(solution)/shard_map/ppermute | solution.py:388
  353.4 49.8 %collective-permute-start.45 = (bf16[512,1024]{1,0:T(8,128)(2,1)}, bf16[512,1024]{1,0:T(8,128)(2,1)}, u32[]{:S(2)}, u32[]{:S(2)}) collective-permute-start(bf16[512,1024]{1,0:T(8,128)(2,1)} %slice.304), channel_id=1, source_target_pairs={{1,0},{2,1},{3,2},{5,4},{6,5},{7,6},{9,8},{10,9},{11,10},{13,12},{... | collective-permute-start | bytes 3145736 | tf_op jit(solution)/shard_map/ppermute | solution.py:394
  358.0 45.2 %collective-permute-start.44 = (bf16[256,1024]{1,0:T(8,128)(2,1)}, bf16[256,1024]{1,0:T(8,128)(2,1)}, u32[]{:S(2)}, u32[]{:S(2)}) collective-permute-start(bf16[256,1024]{1,0:T(8,128)(2,1)} %slice.303), channel_id=1, source_target_pairs={{2,0},{3,1},{6,4},{7,5},{10,8},{11,9},{14,12},{15,13},{18,16},{19,... | collective-permute-start | bytes 1572872 | tf_op jit(solution)/shard_map/ppermute | solution.py:394
  387.4 19.0 %collective-permute-start.43 = (bf16[4,256,512]{2,1,0:T(8,128)(2,1)}, bf16[4,256,512]{2,1,0:T(8,128)(2,1)S(1)}, u32[]{:S(2)}, u32[]{:S(2)}) collective-permute-start(bf16[4,256,512]{2,1,0:T(8,128)(2,1)} %fusion.49), channel_id=1, source_target_pairs={{0,8},{4,20},{8,0},{12,28},{16,24},{20,4},{24,16},{28,12},{1,9},{5... | collective-permute-start | bytes 3145736 | tf_op jit(solution)/shard_map/ppermute | solution.py:388
  412.7 24.0 %collective-permute-start.47 = (bf16[4,64,512]{2,1,0:T(8,128)(2,1)}, bf16[4,64,512]{2,1,0:T(8,128)(2,1)}, u32[]{:S(2)}, u32[]{:S(2)}) collective-permute-start(bf16[4,64,512]{2,1,0:T(8,128)(2,1)} %get-tuple-element.308), channel_id=1, source_target_pairs={{0,2},{1,3},{2,0},{3,1},{4,6},{5,7},{6,4},{7,5},{8,10},{9,11},{10,... | collective-permute-start | bytes 786440 | tf_op jit(solution)/shard_map/ppermute | solution.py:394
  413.1 23.6 %collective-permute-start.48 = (bf16[4,64,512]{2,1,0:T(8,128)(2,1)}, bf16[4,64,512]{2,1,0:T(8,128)(2,1)}, u32[]{:S(2)}, u32[]{:S(2)}) collective-permute-start(bf16[4,64,512]{2,1,0:T(8,128)(2,1)} %get-tuple-element.307), channel_id=1, source_target_pairs={{0,1},{1,2},{2,3},{3,0},{4,5},{5,6},{6,7},{7,4},{8,9},{9,10},{10,1... | collective-permute-start | bytes 786440 | tf_op jit(solution)/shard_map/ppermute | solution.py:394
  (98 other events, 907.6 us)
Sparse Core Ops, SparseCore 0:
  289.5 26.0 reduce-scatter.4
  317.9 25.7 reduce-scatter.2
  345.6 30.7 all-gather.4
  384.8 27.9 all-gather.6

commit v6 on v5

--- a/solution.py
+++ b/solution.py
@@ -507,7 +507,7 @@
     me1, me2 = me_ff(slices, fc1_weight, fc2_weight)
     up = [(i, i + 1) for i in range(mp - 1)]
     tokens_late, _ = tie((tokens, att_me))
-    halo1 = move(tokens_late[rows - near_rows :], up)
+    halo1 = move(tokens_late, up)
     fc1_b = pick(jnp.concatenate([v[:8] for v in bias_all]), ff_from).reshape(-1)
     qv_b = pick(jnp.concatenate([v[8:] for v in bias_all]), heads_from)
     q_bias, v_bias = qv_b[:, :HD].reshape(-1), qv_b[:, HD:].reshape(-1)
@@ -525,16 +525,13 @@
     att_x0 = jnp.stack(att_z)
     att_x1 = hop(att_x0, 1)
     att_x1, halo1 = tie((att_x1, halo1))
-    halo2 = move(halo1, up)
-    halo3 = move(tokens_late[: rows - near_rows], up)
+    halo2 = move(halo1[rows - near_rows :], up)
     part0 = swap(att_x0, 0)
     att_y = hop(jnp.stack([att_x0, att_x1]), 2)
     part1 = swap(att_x1, 0)
-    att_y, part0, part1, halo2, halo3, me1, me2 = tie(
-        (att_y, part0, part1, halo2, halo3, me1, me2)
-    )
+    att_y, part0, part1, halo2, me1, me2 = tie((att_y, part0, part1, halo2, me1, me2))
     z1 = [shift(me1, mp - s) for s in range(1, mp)]
-    ext = jnp.concatenate([halo2, halo3, halo1, tokens], 0).astype(f32)
+    ext = jnp.concatenate([halo2, halo1, tokens], 0).astype(f32)
     xhat_ext, rstd_ext = norm_parts(ext)
     norm1 = (xhat_ext * norm1_gain + norm1_shift).astype(bf16)
     col = [core * half, (1 - core) * half]

time: 495 us -> 487 us (0.984)
    ppermute x22 -> x21, waiting for transfers between devices: 68.7 us -> 51.3 us  [move(): return lax.ppermute(value, 'mp', pairs)]
    ppermute x14, waiting for transfers between devices: 50.8 us -> 63.9 us  [hop(): lax.ppermute(value, 'dp', [(i, i ^ (2 if i & 1 == stage - 1 else 4)) for...]
    ppermute x22 -> x21, starting transfers between devices: 41.1 us -> 41.2 us  [move(): return lax.ppermute(value, 'mp', pairs)]
  transfers between devices with their start and end apart: 61 -> 60, of which waited for: 17 -> 18; matrix products, arithmetic and copies ran while one was open for 32% -> 33% of each run, Pallas kernels for 19% -> 19%
where the time goes in v6:
time: 487 us; the launch traced here: 480 us
  waiting for transfers between devices  116 us (24%)
  Pallas kernels  104 us (21%)
  matrix products  96.5 us (20%)
  starting transfers between devices  60.5 us (12%)
  other arithmetic  58.6 us (12%)
  local copies, waits for them, and re-layouts  28.4 us (6%)
  between operations  15.7 us (3%)
    dot_general x50, matrix products, dot(): lax.dot_general(a, b, (((ca,), (cb,)), ((), ())), preferred_element_type=...  95.8 us
    ppermute x14, waiting for transfers between devices, hop(): lax.ppermute(value, 'dp', [(i, i ^ (2 if i & 1 == stage - 1 else 4)) for...  63.9 us
    ppermute x21, waiting for transfers between devices, move(): return lax.ppermute(value, 'mp', pairs)  51.3 us
    ppermute x21, starting transfers between devices, move(): return lax.ppermute(value, 'mp', pairs)  41.2 us
    pallas_call x3, Pallas kernels, attend_back(): pl.pallas_call(functools.partial(attend_back_kernel, halo, start), grid=(...  37 us
    pallas_call x2, Pallas kernels, attend(): pl.pallas_call(functools.partial(attend_kernel, halo, start), grid=(pairs...  27.1 us
    unnamed x151, local copies, waits for them, and re-layouts  20.8 us
    convert_element_type x10, other arithmetic, add(): return (a.astype(f32) + b.astype(f32)).astype(bf16)  16.3 us
  transfers between devices with their start and end apart: 60, of which 18 were waited for; matrix products, arithmetic and copies ran while one was open for 33% of the time, Pallas kernels for 19%

profile of v6, /device:TPU:0, one launch (start us, length us, event | category | flops | bytes accessed | tf_op | source)
XLA Modules:
  0.0 479.6 jit_solution(18351412140599934800)
XLA Ops:
  28.2 4.4 shard_map.255
  32.6 7.3 %shard_map.256 = (bf16[1024,1024]{1,0:T(8,128)(2,1)}, bf16[1024,1024]{1,0:T(8,128)(2,1)}) custom-call(s32[8]{0:T(128)} %add_xor_fusion.at, bf16[1024,1024]{1,0:T(8,128)(2,1)} %fc1_ref.3, bf16[1024,1024]{1,0:T(8,128)(2,1)} %fc2_ref.3), custom_call_target="tpu_custom_call" | custom-call | flops 1 | bytes 1 | tf_op jit(solution)/shard_map/pallas_call | solution.py:237
  43.2 10.8 %collective-permute-done.6.refs_2_ = bf16[3,4,64,512]{3,2,1,0:T(8,128)(2,1)} collective-permute-done((bf16[3,4,64,512]{3,2,1,0:T(8,128)(2,1)}, bf16[3,4,64,512]{3,2,1,0:T(8,128)(2,1)}, u32[]{:S(2)}, u32[]{:S(2)}) %collective-permute-start.6) | collective-permute-done | bytes 786464 | tf_op jit(solution)/shard_map/ppermute | solution.py:388
  54.0 5.6 %collective-permute-done.7 = bf16[512,1024]{1,0:T(8,128)(2,1)S(1)} collective-permute-done((bf16[512,1024]{1,0:T(8,128)(2,1)S(1)}, bf16[512,1024]{1,0:T(8,128)(2,1)S(1)}, u32[]{:S(2)}, u32[]{:S(2)}) %collective-permute-start.7) | collective-permute-done | bytes 1048608 | tf_op jit(solution)/shard_map/ppermute | solution.py:394
  64.9 8.0 %collective-permute-start.11 = (bf16[256,1024]{1,0:T(8,128)(2,1)}, bf16[256,1024]{1,0:T(8,128)(2,1)S(1)}, u32[]{:S(2)}, u32[]{:S(2)}) collective-permute-start(bf16[256,1024]{1,0:T(8,128)(2,1)} %slice.260), channel_id=1, source_target_pairs={{0,1},{1,2},{2,3},{4,5},{5,6},{6,7},{8,9},{9,10},{10,11},{12,13},{... | collective-permute-start | bytes 1572872 | tf_op jit(solution)/shard_map/ppermute | solution.py:394
  75.7 8.8 %collective-permute-done.11 = bf16[256,1024]{1,0:T(8,128)(2,1)S(1)} collective-permute-done((bf16[256,1024]{1,0:T(8,128)(2,1)}, bf16[256,1024]{1,0:T(8,128)(2,1)S(1)}, u32[]{:S(2)}, u32[]{:S(2)}) %collective-permute-start.11) | collective-permute-done | bytes 524320 | tf_op jit(solution)/shard_map/ppermute | solution.py:394
  84.5 4.1 collective-permute-start.13
  95.7 4.5 fusion
  100.2 7.1 %shard_map.258 = (bf16[4,4,64,1024]{3,2,1,0:T(8,128)(2,1)}, bf16[4,4,64,1024]{3,2,1,0:T(8,128)(2,1)}, bf16[4,4,64,1024]{3,2,1,0:T(8,128)(2,1)}, bf16[4,4,64,1024]{3,2,1,0:T(8,128)(2,1)}) custom-call(s32[1]{0:T(128)} %bitcast.core, bf16[4,4,64,512]{3,2,1,0:T(8,128)(2,1)} %get-tuple-element.144.refs_0_, bf16[3,4,64,512]{3,2,1,0:T(8,128)(2,1)} %get-tuple-element.310.refs_1_, ...), custom_call_target="tpu_custom_call" | custom-call | flops 1 | bytes 1 | tf_op jit(solution)/shard_map/pallas_call | solution.py:288
  126.9 13.3 %shard_map.259 = (bf16[512,1024]{1,0:T(8,128)(2,1)S(1)}, f32[8,2,512]{2,1,0:T(2,128)S(1)}) custom-call(f32[16]{0:T(128)S(1)} %get-tuple-element.132.slopes, s32[1,512]{1,0:T(1,128)S(1)} %pad_dynamic-slice_fusion.8.segq, s32[1280,1]{1,0:T(8,128)S(1)} %copy.72.segk, bf16[512,1024]{1,0:T(8,128)(2,1)S(1)} %add_convert_fusion.10.q_ref, ...), custom_call_target="tpu_custom_call" | custom-call | flops 1 | bytes 1 | tf_op jit(solution)/shard_map/pallas_call | solution.py:114
  143.5 13.8 %shard_map.260 = (bf16[512,1024]{1,0:T(8,128)(2,1)S(1)}, f32[8,2,512]{2,1,0:T(2,128)S(1)}) custom-call(f32[16]{0:T(128)S(1)} %get-tuple-element.132.slopes, s32[1,512]{1,0:T(1,128)S(1)} %pad_dynamic-slice_fusion.8.segq, s32[1280,1]{1,0:T(8,128)S(1)} %copy.72.segk, ...), custom_call_target="tpu_custom_call", output_to_operand_aliasing={{0}: (6, {}), {1}: (7, {})} | custom-call | flops 1 | bytes 1 | tf_op jit(solution)/shard_map/pallas_call | solution.py:114
  157.4 6.0 %collective-permute-done.21 = bf16[384,1024]{1,0:T(8,128)(2,1)S(1)} collective-permute-done((bf16[384,1024]{1,0:T(8,128)(2,1)S(1)}, bf16[384,1024]{1,0:T(8,128)(2,1)S(1)}, u32[]{:S(2)}, u32[]{:S(2)}) %collective-permute-start.21) | collective-permute-done | bytes 786464 | tf_op jit(solution)/shard_map/ppermute | solution.py:388
  163.4 6.2 %collective-permute-done.20 = bf16[768,1024]{1,0:T(8,128)(2,1)} collective-permute-done((bf16[768,1024]{1,0:T(8,128)(2,1)S(1)}, bf16[768,1024]{1,0:T(8,128)(2,1)}, u32[]{:S(2)}, u32[]{:S(2)}) %collective-permute-start.20) | collective-permute-done | bytes 1572896 | tf_op jit(solution)/shard_map/ppermute | solution.py:388
  234.5 13.5 %shard_map.261 = (bf16[512,1024]{1,0:T(8,128)(2,1)S(1)}, bf16[1280,1024]{1,0:T(8,128)(2,1)}, bf16[1280,1024]{1,0:T(8,128)(2,1)}) custom-call(f32[16]{0:T(128)S(1)} %get-tuple-element.132.slopes, s32[1,512]{1,0:T(1,128)S(1)} %pad_dynamic-slice_fusion.8.segq, s32[1280,1]{1,0:T(8,128)S(1)} %copy.72.segk, bf16[512,1024]{1,0:T(8,128)(2,1)S(1)} %add_convert_fusion.10.q_ref, ...), custom_call_target="tpu_custom_call" | custom-call | flops 1 | bytes 1 | tf_op jit(solution)/shard_map/pallas_call | solution.py:146
  255.0 3.8 add_convert_fusion.2
  258.9 13.7 %shard_map.262 = (bf16[512,1024]{1,0:T(8,128)(2,1)S(1)}, bf16[1280,1024]{1,0:T(8,128)(2,1)}, bf16[1280,1024]{1,0:T(8,128)(2,1)}) custom-call(f32[16]{0:T(128)S(1)} %get-tuple-element.132.slopes, s32[1,512]{1,0:T(1,128)S(1)} %pad_dynamic-slice_fusion.8.segq, s32[1280,1]{1,0:T(8,128)S(1)} %copy.72.segk, ...), custom_call_target="tpu_custom_call", output_to_operand_aliasing={{0}: (8, {}), {1}: (9, {}), {2}: (10, {})} | custom-call | flops 1 | bytes 1 | tf_op jit(solution)/shard_map/pallas_call | solution.py:146
  272.6 3.7 collective-permute-done.34
  290.9 9.8 %shard_map.263 = (bf16[512,1024]{1,0:T(8,128)(2,1)S(1)}, bf16[1280,1024]{1,0:T(8,128)(2,1)}, bf16[1280,1024]{1,0:T(8,128)(2,1)}) custom-call(f32[16]{0:T(128)S(1)} %get-tuple-element.132.slopes, s32[1,512]{1,0:T(1,128)S(1)} %pad_dynamic-slice_fusion.8.segq, s32[1280,1]{1,0:T(8,128)S(1)} %copy.72.segk, ...), custom_call_target="tpu_custom_call", output_to_operand_aliasing={{0}: (8, {}), {1}: (9, {}), {2}: (10, {})} | custom-call | flops 1 | bytes 1 | tf_op jit(solution)/shard_map/pallas_call | solution.py:146
  310.5 4.6 fusion.147
  337.3 6.5 %shard_map.264 = (bf16[2,4,256,512]{3,2,1,0:T(8,128)(2,1)}, bf16[2,4,256,512]{3,2,1,0:T(8,128)(2,1)}) custom-call(bf16[1024,512]{1,0:T(8,128)(2,1)} %convolution_convert_fusion.11.refs_0_, bf16[1024,512]{1,0:T(8,128)(2,1)} %convolution_convert_fusion.10.refs_1_, bf16[1024,512]{1,0:T(8,128)(2,1)} %convolution_convert_fusion.6.refs_2_, ...), custom_call_target="tpu_custom_call" | custom-call | flops 1 | bytes 1 | tf_op jit(solution)/shard_map/pallas_call | solution.py:318
  352.6 5.0 %slice_add_fusion = f32[512,1024]{1,0:T(8,128)} fusion(f32[1280,1024]{1,0:T(8,128)} %copy-done.39, bf16[512,1024]{1,0:T(8,128)(2,1)S(1)} %copy-done.9, bf16[1024,1024]{1,0:T(8,128)(2,1)} %bitcast.197), kind=kOutput, calls=%fused_computation.57 | convolution fusion | flops 1074266112 | bytes 7340032 | tf_op jit(solution)/shard_map/dot_general | solution.py:22
  357.5 21.0 %collective-permute-done.41 = bf16[2,4,256,512]{3,2,1,0:T(8,128)(2,1)} collective-permute-done((bf16[2,4,256,512]{3,2,1,0:T(8,128)(2,1)}, bf16[2,4,256,512]{3,2,1,0:T(8,128)(2,1)}, u32[]{:S(2)}, u32[]{:S(2)}) %collective-permute-start.41) | collective-permute-done | bytes 2097184 | tf_op jit(solution)/shard_map/ppermute | solution.py:388
  381.8 14.6 %collective-permute-done.43 = bf16[256,1024]{1,0:T(8,128)(2,1)} collective-permute-done((bf16[256,1024]{1,0:T(8,128)(2,1)}, bf16[256,1024]{1,0:T(8,128)(2,1)}, u32[]{:S(2)}, u32[]{:S(2)}) %collective-permute-start.43) | collective-permute-done | bytes 524320 | tf_op jit(solution)/shard_map/ppermute | solution.py:394
  408.4 3.4 multiply_add_fusion.5
  411.9 4.1 convert_element_type.476
  416.0 13.8 %collective-permute-done.46 = bf16[4,64,512]{2,1,0:T(8,128)(2,1)} collective-permute-done((bf16[4,64,512]{2,1,0:T(8,128)(2,1)}, bf16[4,64,512]{2,1,0:T(8,128)(2,1)}, u32[]{:S(2)}, u32[]{:S(2)}) %collective-permute-start.46) | collective-permute-done | bytes 262176 | tf_op jit(solution)/shard_map/ppermute | solution.py:394
  431.9 5.5 %collective-permute-done.53 = bf16[4,64,512]{2,1,0:T(8,128)(2,1)S(1)} collective-permute-done((bf16[4,64,512]{2,1,0:T(8,128)(2,1)S(1)}, bf16[4,64,512]{2,1,0:T(8,128)(2,1)S(1)}, u32[]{:S(2)}, u32[]{:S(2)}) %collective-permute-start.53) | collective-permute-done | bytes 262176 | tf_op jit(solution)/shard_map/ppermute | solution.py:388
  438.4 8.3 %collective-permute-done.54 = bf16[2,4,64,512]{3,2,1,0:T(8,128)(2,1)S(1)} collective-permute-done((bf16[2,4,64,512]{3,2,1,0:T(8,128)(2,1)S(1)}, bf16[2,4,64,512]{3,2,1,0:T(8,128)(2,1)S(1)}, u32[]{:S(2)}, u32[]{:S(2)}) %collective-permute-start.54) | collective-permute-done | bytes 524320 | tf_op jit(solution)/shard_map/ppermute | solution.py:388
  446.9 4.8 %shard_map.265 = f32[1024,1024]{1,0:T(8,128)} custom-call(bf16[1024,1024]{1,0:T(8,128)(2,1)} %all-gather.7.cloned.1.call-done.in_ref), custom_call_target="tpu_custom_call" | custom-call | flops 1 | bytes 1 | tf_op jit(solution)/shard_map/pallas_call | solution.py:338
  452.1 3.9 collective-permute-done.51
  464.3 4.8 shard_map.266
  469.0 3.5 copy.80
  (411 shorter events, 215.6 us)
Async XLA Ops:
  7.2 317.6 %reduce-scatter.5.cloned.1.call-start = ((), (), s32[]{:S(2)}) async-start(), calls=%async_computation.3 | async-start | bytes 1310720 | tf_op jit(solution)/shard_map/reduce_scatter | solution.py:610
  20.1 20.1 %collective-permute-start = (bf16[4,64,512]{2,1,0:T(8,128)(2,1)}, bf16[4,64,512]{2,1,0:T(8,128)(2,1)S(1)}, u32[]{:S(2)}, u32[]{:S(2)}) collective-permute-start(bf16[4,64,512]{2,1,0:T(8,128)(2,1)} %bitcast.171), channel_id=1, source_target_pairs={{0,1},{1,2},{2,3},{3,0},{4,5},{5,6},{6,7},{7,4},{8,9},{9,10},{10,1... | collective-permute-start | bytes 786440 | tf_op jit(solution)/shard_map/ppermute | solution.py:394
  20.8 19.9 %collective-permute-start.1 = (bf16[4,64,512]{2,1,0:T(8,128)(2,1)}, bf16[4,64,512]{2,1,0:T(8,128)(2,1)S(1)}, u32[]{:S(2)}, u32[]{:S(2)}) collective-permute-start(bf16[4,64,512]{2,1,0:T(8,128)(2,1)} %bitcast.172), channel_id=1, source_target_pairs={{0,2},{1,3},{2,0},{3,1},{4,6},{5,7},{6,4},{7,5},{8,10},{9,11},{10,... | collective-permute-start | bytes 786440 | tf_op jit(solution)/shard_map/ppermute | solution.py:394
  25.2 34.4 %collective-permute-start.7 = (bf16[512,1024]{1,0:T(8,128)(2,1)S(1)}, bf16[512,1024]{1,0:T(8,128)(2,1)S(1)}, u32[]{:S(2)}, u32[]{:S(2)}) collective-permute-start(bf16[512,1024]{1,0:T(8,128)(2,1)S(1)} %copy-done.18), channel_id=1, source_target_pairs={{0,1},{1,2},{2,3},{4,5},{5,6},{6,7},{8,9},{9,10},{10,11},{12,13},{... | collective-permute-start | bytes 3145736 | tf_op jit(solution)/shard_map/ppermute | solution.py:394
  62.0 22.5 %collective-permute-start.8 = (bf16[2,3,4,64,512]{4,3,2,1,0:T(8,128)(2,1)}, bf16[2,3,4,64,512]{4,3,2,1,0:T(8,128)(2,1)}, u32[]{:S(2)}, u32[]{:S(2)}) collective-permute-start(bf16[2,3,4,64,512]{4,3,2,1,0:T(8,128)(2,1)} %pad_maximum_fusion.3), channel_id=1, source_target_pairs={{0,16},{4,12},{8,24},{12,4},{16,0},{20,28},{24,8},{28,20},{1,17},{... | collective-permute-start | bytes 4718600 | tf_op jit(solution)/shard_map/ppermute | solution.py:388
  63.5 21.0 %collective-permute-start.10 = (bf16[3,4,64,512]{3,2,1,0:T(8,128)(2,1)}, bf16[3,4,64,512]{3,2,1,0:T(8,128)(2,1)}, u32[]{:S(2)}, u32[]{:S(2)}) collective-permute-start(bf16[3,4,64,512]{3,2,1,0:T(8,128)(2,1)} %collective-permute-done.6.refs_2_), channel_id=1, source_target_pairs={{0,4},{4,0},{8,12},{12,8},{16,20},{20,16},{24,28},{28,24},{1,5},{5... | collective-permute-start | bytes 2359304 | tf_op jit(solution)/shard_map/ppermute | solution.py:383
  64.9 19.6 %collective-permute-start.11 = (bf16[256,1024]{1,0:T(8,128)(2,1)}, bf16[256,1024]{1,0:T(8,128)(2,1)S(1)}, u32[]{:S(2)}, u32[]{:S(2)}) collective-permute-start(bf16[256,1024]{1,0:T(8,128)(2,1)} %slice.260), channel_id=1, source_target_pairs={{0,1},{1,2},{2,3},{4,5},{5,6},{6,7},{8,9},{9,10},{10,11},{12,13},{... | collective-permute-start | bytes 1572872 | tf_op jit(solution)/shard_map/ppermute | solution.py:394
  84.5 26.1 %collective-permute-start.13 = (bf16[128,1024]{1,0:T(8,128)(2,1)}, bf16[128,1024]{1,0:T(8,128)(2,1)}, u32[]{:S(2)}, u32[]{:S(2)}) collective-permute-start(bf16[128,1024]{1,0:T(8,128)(2,1)} %get-tuple-element.151), channel_id=1, source_target_pairs={{0,3},{1,0},{2,1},{3,2},{4,7},{5,4},{6,5},{7,6},{8,11},{9,8},{10,9... | collective-permute-start | bytes 786440 | tf_op jit(solution)/shard_map/ppermute | solution.py:394
  88.6 23.5 %collective-permute-start.14 = (bf16[128,1024]{1,0:T(8,128)(2,1)}, bf16[128,1024]{1,0:T(8,128)(2,1)}, u32[]{:S(2)}, u32[]{:S(2)}) collective-permute-start(bf16[128,1024]{1,0:T(8,128)(2,1)} %get-tuple-element.151), channel_id=1, source_target_pairs={{0,2},{1,3},{2,0},{3,1},{4,6},{5,7},{6,4},{7,5},{8,10},{9,11},{10,... | collective-permute-start | bytes 786440 | tf_op jit(solution)/shard_map/ppermute | solution.py:394
  90.8 21.3 %collective-permute-start.15 = (bf16[128,1024]{1,0:T(8,128)(2,1)}, bf16[128,1024]{1,0:T(8,128)(2,1)}, u32[]{:S(2)}, u32[]{:S(2)}) collective-permute-start(bf16[128,1024]{1,0:T(8,128)(2,1)} %get-tuple-element.151), channel_id=1, source_target_pairs={{0,1},{1,2},{2,3},{3,0},{4,5},{5,6},{6,7},{7,4},{8,9},{9,10},{10,1... | collective-permute-start | bytes 786440 | tf_op jit(solution)/shard_map/ppermute | solution.py:394
  112.1 30.0 %collective-permute-start.17 = (bf16[128,1024]{1,0:T(8,128)(2,1)S(1)}, bf16[128,1024]{1,0:T(8,128)(2,1)S(1)}, u32[]{:S(2)}, u32[]{:S(2)}) collective-permute-start(bf16[128,1024]{1,0:T(8,128)(2,1)S(1)} %copy-done.63), channel_id=1, source_target_pairs={{0,3},{1,0},{2,1},{3,2},{4,7},{5,4},{6,5},{7,6},{8,11},{9,8},{10,9... | collective-permute-start | bytes 786440 | tf_op jit(solution)/shard_map/ppermute | solution.py:394
  112.6 29.6 %collective-permute-start.18 = (bf16[128,1024]{1,0:T(8,128)(2,1)S(1)}, bf16[128,1024]{1,0:T(8,128)(2,1)S(1)}, u32[]{:S(2)}, u32[]{:S(2)}) collective-permute-start(bf16[128,1024]{1,0:T(8,128)(2,1)S(1)} %copy-done.63), channel_id=1, source_target_pairs={{0,2},{1,3},{2,0},{3,1},{4,6},{5,7},{6,4},{7,5},{8,10},{9,11},{10,... | collective-permute-start | bytes 786440 | tf_op jit(solution)/shard_map/ppermute | solution.py:394
  114.3 27.8 %collective-permute-start.19 = (bf16[128,1024]{1,0:T(8,128)(2,1)S(1)}, bf16[128,1024]{1,0:T(8,128)(2,1)S(1)}, u32[]{:S(2)}, u32[]{:S(2)}) collective-permute-start(bf16[128,1024]{1,0:T(8,128)(2,1)S(1)} %copy-done.63), channel_id=1, source_target_pairs={{0,1},{1,2},{2,3},{3,0},{4,5},{5,6},{6,7},{7,4},{8,9},{9,10},{10,1... | collective-permute-start | bytes 786440 | tf_op jit(solution)/shard_map/ppermute | solution.py:394
  117.7 24.5 %collective-permute-start.16 = (bf16[384,1024]{1,0:T(8,128)(2,1)S(1)}, bf16[384,1024]{1,0:T(8,128)(2,1)S(1)}, u32[]{:S(2)}, u32[]{:S(2)}) collective-permute-start(bf16[384,1024]{1,0:T(8,128)(2,1)S(1)} %pad_maximum_fusion.8), channel_id=1, source_target_pairs={{0,8},{4,20},{8,0},{12,28},{16,24},{20,4},{24,16},{28,12},{1,9},{5... | collective-permute-start | bytes 2359304 | tf_op jit(solution)/shard_map/ppermute | solution.py:388
  142.3 27.3 %collective-permute-start.20 = (bf16[768,1024]{1,0:T(8,128)(2,1)S(1)}, bf16[768,1024]{1,0:T(8,128)(2,1)}, u32[]{:S(2)}, u32[]{:S(2)}) collective-permute-start(bf16[768,1024]{1,0:T(8,128)(2,1)S(1)} %constant_dynamic-update-slice_fusion), channel_id=1, source_target_pairs={{0,16},{4,12},{8,24},{12,4},{16,0},{20,28},{24,8},{28,20},{1,17},{... | collective-permute-start | bytes 4718600 | tf_op jit(solution)/shard_map/ppermute | solution.py:388
  142.9 20.5 %collective-permute-start.21 = (bf16[384,1024]{1,0:T(8,128)(2,1)S(1)}, bf16[384,1024]{1,0:T(8,128)(2,1)S(1)}, u32[]{:S(2)}, u32[]{:S(2)}) collective-permute-start(bf16[384,1024]{1,0:T(8,128)(2,1)S(1)} %pad_maximum_fusion.9), channel_id=1, source_target_pairs={{0,8},{4,20},{8,0},{12,28},{16,24},{20,4},{24,16},{28,12},{1,9},{5... | collective-permute-start | bytes 2359304 | tf_op jit(solution)/shard_map/ppermute | solution.py:388
  143.5 34.3 %collective-permute-start.24 = (bf16[768,1024]{1,0:T(8,128)(2,1)S(1)}, bf16[768,1024]{1,0:T(8,128)(2,1)S(1)}, u32[]{:S(2)}, u32[]{:S(2)}) collective-permute-start(bf16[768,1024]{1,0:T(8,128)(2,1)S(1)} %constant_dynamic-update-slice_fusion), channel_id=1, source_target_pairs={{0,4},{4,0},{8,12},{12,8},{16,20},{20,16},{24,28},{28,24},{1,5},{5... | collective-permute-start | bytes 4718600 | tf_op jit(solution)/shard_map/ppermute | solution.py:383
  169.6 25.5 %collective-permute-start.23 = (bf16[768,1024]{1,0:T(8,128)(2,1)S(1)}, bf16[768,1024]{1,0:T(8,128)(2,1)S(1)}, u32[]{:S(2)}, u32[]{:S(2)}) collective-permute-start(bf16[768,1024]{1,0:T(8,128)(2,1)S(1)} %constant_dynamic-update-slice_fusion.4), channel_id=1, source_target_pairs={{0,4},{4,0},{8,12},{12,8},{16,20},{20,16},{24,28},{28,24},{1,5},{5... | collective-permute-start | bytes 4718600 | tf_op jit(solution)/shard_map/ppermute | solution.py:383
  169.7 32.1 %collective-permute-start.22 = (bf16[768,1024]{1,0:T(8,128)(2,1)S(1)}, bf16[768,1024]{1,0:T(8,128)(2,1)S(1)}, u32[]{:S(2)}, u32[]{:S(2)}) collective-permute-start(bf16[768,1024]{1,0:T(8,128)(2,1)S(1)} %constant_dynamic-update-slice_fusion.4), channel_id=1, source_target_pairs={{0,16},{4,12},{8,24},{12,4},{16,0},{20,28},{24,8},{28,20},{1,17},{... | collective-permute-start | bytes 4718600 | tf_op jit(solution)/shard_map/ppermute | solution.py:388
  180.4 18.8 %collective-permute-start.26 = (bf16[768,1024]{1,0:T(8,128)(2,1)}, bf16[768,1024]{1,0:T(8,128)(2,1)S(1)}, u32[]{:S(2)}, u32[]{:S(2)}) collective-permute-start(bf16[768,1024]{1,0:T(8,128)(2,1)} %collective-permute-done.20), channel_id=1, source_target_pairs={{0,4},{4,0},{8,12},{12,8},{16,20},{20,16},{24,28},{28,24},{1,5},{5... | collective-permute-start | bytes 4718600 | tf_op jit(solution)/shard_map/ppermute | solution.py:383
  199.0 56.0 %collective-permute-start.35 = (bf16[768,1024]{1,0:T(8,128)(2,1)}, bf16[768,1024]{1,0:T(8,128)(2,1)}, u32[]{:S(2)}, u32[]{:S(2)}) collective-permute-start(bf16[768,1024]{1,0:T(8,128)(2,1)} %convolution_convert_fusion.1), channel_id=1, source_target_pairs={{0,4},{4,0},{8,12},{12,8},{16,20},{20,16},{24,28},{28,24},{1,5},{5... | collective-permute-start | bytes 4718600 | tf_op jit(solution)/shard_map/ppermute | solution.py:383
  217.1 30.9 %collective-permute-start.31 = (bf16[1024,1024]{1,0:T(8,128)(2,1)}, bf16[1024,1024]{1,0:T(8,128)(2,1)}, u32[]{:S(2)}, u32[]{:S(2)}) collective-permute-start(bf16[1024,1024]{1,0:T(8,128)(2,1)} %pad_maximum_fusion.2), channel_id=1, source_target_pairs={{0,16},{4,12},{8,24},{12,4},{16,0},{20,28},{24,8},{28,20},{1,17},{... | collective-permute-start | bytes 6291464 | tf_op jit(solution)/shard_map/ppermute | solution.py:388
  230.1 47.0 %collective-permute-start.32 = (bf16[1024,1024]{1,0:T(8,128)(2,1)}, bf16[1024,1024]{1,0:T(8,128)(2,1)}, u32[]{:S(2)}, u32[]{:S(2)}) collective-permute-start(bf16[1024,1024]{1,0:T(8,128)(2,1)} %pad_maximum_fusion.1), channel_id=1, source_target_pairs={{0,16},{4,12},{8,24},{12,4},{16,0},{20,28},{24,8},{28,20},{1,17},{... | collective-permute-start | bytes 6291464 | tf_op jit(solution)/shard_map/ppermute | solution.py:388
  251.7 24.6 %collective-permute-start.34 = (bf16[512,1024]{1,0:T(8,128)(2,1)}, bf16[512,1024]{1,0:T(8,128)(2,1)}, u32[]{:S(2)}, u32[]{:S(2)}) collective-permute-start(bf16[512,1024]{1,0:T(8,128)(2,1)} %pad_maximum_fusion.4), channel_id=1, source_target_pairs={{0,8},{4,20},{8,0},{12,28},{16,24},{20,4},{24,16},{28,12},{1,9},{5... | collective-permute-start | bytes 3145736 | tf_op jit(solution)/shard_map/ppermute | solution.py:388
  283.3 74.3 %reduce-scatter.3.cloned.1.call-start = ((), (), s32[]{:S(2)}) async-start(), calls=%async_computation.2 | async-start | bytes 1310720 | tf_op jit(solution)/shard_map/reduce_scatter | solution.py:610
  308.4 103.5 %all-gather.5.cloned.1.call-start = ((), (), s32[]{:S(2)}) async-start(), calls=%async_computation.4 | async-start | bytes 2359296 | tf_op jit(solution)/shard_map/all_gather | solution.py:405
  324.8 122.1 %all-gather.7.cloned.1.call-start = ((), (), s32[]{:S(2)}) async-start(), calls=%async_computation.5 | async-start | bytes 2359296 | tf_op jit(solution)/shard_map/all_gather | solution.py:405
  343.8 34.8 %collective-permute-start.41 = (bf16[2,4,256,512]{3,2,1,0:T(8,128)(2,1)}, bf16[2,4,256,512]{3,2,1,0:T(8,128)(2,1)}, u32[]{:S(2)}, u32[]{:S(2)}) collective-permute-start(bf16[2,4,256,512]{3,2,1,0:T(8,128)(2,1)} %get-tuple-element.213), channel_id=1, source_target_pairs={{0,16},{4,12},{8,24},{12,4},{16,0},{20,28},{24,8},{28,20},{1,17},{... | collective-permute-start | bytes 6291464 | tf_op jit(solution)/shard_map/ppermute | solution.py:388
  346.3 50.0 %collective-permute-start.44 = (bf16[512,1024]{1,0:T(8,128)(2,1)}, bf16[512,1024]{1,0:T(8,128)(2,1)}, u32[]{:S(2)}, u32[]{:S(2)}) collective-permute-start(bf16[512,1024]{1,0:T(8,128)(2,1)} %slice.300), channel_id=1, source_target_pairs={{1,0},{2,1},{3,2},{5,4},{6,5},{7,6},{9,8},{10,9},{11,10},{13,12},{... | collective-permute-start | bytes 3145736 | tf_op jit(solution)/shard_map/ppermute | solution.py:394
  350.9 45.4 %collective-permute-start.43 = (bf16[256,1024]{1,0:T(8,128)(2,1)}, bf16[256,1024]{1,0:T(8,128)(2,1)}, u32[]{:S(2)}, u32[]{:S(2)}) collective-permute-start(bf16[256,1024]{1,0:T(8,128)(2,1)} %slice.299), channel_id=1, source_target_pairs={{2,0},{3,1},{6,4},{7,5},{10,8},{11,9},{14,12},{15,13},{18,16},{19,... | collective-permute-start | bytes 1572872 | tf_op jit(solution)/shard_map/ppermute | solution.py:394
  405.9 23.9 %collective-permute-start.46 = (bf16[4,64,512]{2,1,0:T(8,128)(2,1)}, bf16[4,64,512]{2,1,0:T(8,128)(2,1)}, u32[]{:S(2)}, u32[]{:S(2)}) collective-permute-start(bf16[4,64,512]{2,1,0:T(8,128)(2,1)} %get-tuple-element.306), channel_id=1, source_target_pairs={{0,2},{1,3},{2,0},{3,1},{4,6},{5,7},{6,4},{7,5},{8,10},{9,11},{10,... | collective-permute-start | bytes 786440 | tf_op jit(solution)/shard_map/ppermute | solution.py:394
  406.2 23.6 %collective-permute-start.47 = (bf16[4,64,512]{2,1,0:T(8,128)(2,1)}, bf16[4,64,512]{2,1,0:T(8,128)(2,1)}, u32[]{:S(2)}, u32[]{:S(2)}) collective-permute-start(bf16[4,64,512]{2,1,0:T(8,128)(2,1)} %get-tuple-element.305), channel_id=1, source_target_pairs={{0,1},{1,2},{2,3},{3,0},{4,5},{5,6},{6,7},{7,4},{8,9},{9,10},{10,1... | collective-permute-start | bytes 786440 | tf_op jit(solution)/shard_map/ppermute | solution.py:394
  (97 other events, 899.7 us)
Sparse Core Ops, SparseCore 0:
  283.4 25.8 reduce-scatter.4
  311.5 25.7 reduce-scatter.2
  339.3 30.7 all-gather.4
  378.7 27.8 all-gather.6
